TPU v7x, 256 devices: a whole 4x4x8 slice. The times are simulated.
256 devices in a mesh: occ: 32 (over z, x_hi, core), vir: 8 (over x_lo, y).
Axes of the slice: x: 4 (x_hi: 2, x_lo: 2; x = x_hi * 2 + x_lo), y: 4, z: 8, core: 2. Of those that a mesh axis runs over, the one named last changes fastest.
Arguments:
- factors: bfloat16 [32, 1024, 3072], P('occ', 'vir'), may hold values from -0.71875 to 0.71875
- occ_energy: float32 [32], replicated, may hold values from -2 to -0.4
- vir_energy: float32 [1024], replicated, may hold values from 0.4 to 4
- density_in: float32 [32, 1024, 3072], P('occ', 'vir'), may hold values from -3 to 3
Outputs:
- density: float32 [32, 1024, 3072], P('occ', 'vir')
All inputs are finite; a program needn't handle non-finite values.
Results may differ from a plain program's by a relative error of at most 0.0027.
Values may be sent and summed in bfloat16 or wider, within the bound.
No kernel may reach another device: no remote copies, remote signals or barrier semaphores. Data moves between devices by JAX's collectives and lax.ppermute only.
A program may use at most 128 MiB of HBM per device.

v0:
```python
import jax
import jax.numpy as jnp
from jax import lax
from jax.sharding import PartitionSpec as P

VISITS = 3


def passed_along(block, axis, distance):
    devices = range(lax.axis_size(axis))
    route = [((i - distance) % len(devices), i) for i in devices]
    return lax.ppermute(block, axis, route)


def on_device(factors, occ_energy, vir_energy, density_in):
    occ_rows = factors.shape[0]
    vir_local = factors.shape[1]
    aux_width = factors.shape[2]
    vir_whole = vir_energy.shape[0]
    occ_rank = lax.axis_index("occ")
    cycle_size = lax.axis_size("occ")
    vir_rank = lax.axis_index("vir")
    e_own = lax.dynamic_slice_in_dim(occ_energy, occ_rank * occ_rows, occ_rows, 0)
    e_local = lax.dynamic_slice_in_dim(vir_energy, vir_rank * vir_local, vir_local, 0)
    flat_own = factors.reshape(occ_rows * vir_local, aux_width)
    total = density_in.reshape(occ_rows * vir_local, aux_width)
    partner_shard = factors
    partner = factors
    for visit in range(VISITS):
        if visit > 0:
            partner_shard = passed_along(partner_shard, "occ", 1)
        partner = lax.all_gather(partner_shard, "vir", axis=1, tiled=True)
        other = (occ_rank - visit) % cycle_size * occ_rows
        e_partner = lax.dynamic_slice_in_dim(occ_energy, other, occ_rows, 0)
        flat_partner = partner.reshape(occ_rows * vir_whole, aux_width)
        direct = lax.dot_general(
            flat_own, flat_partner, (((1,), (1,)), ((), ())), preferred_element_type=jnp.float32
        )
        direct = direct.astype(jnp.bfloat16).reshape(occ_rows, vir_local, occ_rows, vir_whole)
        swapped = lax.all_to_all(direct, "vir", split_axis=3, concat_axis=1, tiled=True).transpose(
            0, 3, 2, 1
        )
        denom = (
            e_own[:, None, None, None]
            + e_partner[None, None, :, None]
            - e_local[None, :, None, None]
            - vir_energy[None, None, None, :]
        )
        amp = ((2.0 * direct.astype(jnp.float32) - swapped.astype(jnp.float32)) / denom).astype(
            jnp.bfloat16
        )
        total = total + jnp.dot(
            amp.reshape(occ_rows * vir_local, occ_rows * vir_whole),
            flat_partner,
            preferred_element_type=jnp.float32,
        )
    return total.reshape(density_in.shape)


def solution(mesh):
    return jax.shard_map(
        on_device,
        mesh=mesh,
        in_specs=(P("occ", "vir", None), P(), P(), P("occ", "vir", None)),
        out_specs=P("occ", "vir", None),
        check_vma=False,
    )
```

profile of v0, /device:TPU:1, one launch (start us, length us, event | category | flops | bytes accessed | tf_op | source)
XLA Modules:
  0.0 283.7 jit_solution(7729517185686654184)
XLA Ops:
  6.5 0.7 all-gather.4.cloned.1.call-update
  7.3 4.2 %collective-permute-start = (bf16[1,128,3072]{2,1,0:T(8,128)(2,1)}, bf16[1,128,3072]{2,1,0:T(8,128)(2,1)S(1)}, u32[]{:S(2)}, u32[]{:S(2)}) collective-permute-start(bf16[1,128,3072]{2,1,0:T(8,128)(2,1)} %param.4), channel_id=1, source_target_pairs={{248,0},{0,8},{8,16},{16,24},{24,32},{32,40},{40,48},{48,56},{56,6... | collective-permute-start | bytes 2359304 | tf_op jit(solution)/shard_map/ppermute | solution.py:12
  11.5 9.3 %collective-permute-done = bf16[1,128,3072]{2,1,0:T(8,128)(2,1)S(1)} collective-permute-done((bf16[1,128,3072]{2,1,0:T(8,128)(2,1)}, bf16[1,128,3072]{2,1,0:T(8,128)(2,1)S(1)}, u32[]{:S(2)}, u32[]{:S(2)}) %collective-permute-start) | collective-permute-done | bytes 786464 | tf_op jit(solution)/shard_map/ppermute | solution.py:12
  20.8 0.9 copy-done.2
  21.7 4.0 %collective-permute-start.1 = (bf16[1,128,3072]{2,1,0:T(8,128)(2,1)}, bf16[1,128,3072]{2,1,0:T(8,128)(2,1)S(1)}, u32[]{:S(2)}, u32[]{:S(2)}) collective-permute-start(bf16[1,128,3072]{2,1,0:T(8,128)(2,1)} %copy-done.2), channel_id=1, source_target_pairs={{248,0},{0,8},{8,16},{16,24},{24,32},{32,40},{40,48},{48,56},{56,6... | collective-permute-start | bytes 2359304 | tf_op jit(solution)/shard_map/ppermute | solution.py:12
  25.7 26.0 %collective-permute-done.1 = bf16[1,128,3072]{2,1,0:T(8,128)(2,1)S(1)} collective-permute-done((bf16[1,128,3072]{2,1,0:T(8,128)(2,1)}, bf16[1,128,3072]{2,1,0:T(8,128)(2,1)S(1)}, u32[]{:S(2)}, u32[]{:S(2)}) %collective-permute-start.1) | collective-permute-done | bytes 786464 | tf_op jit(solution)/shard_map/ppermute | solution.py:12
  51.7 0.9 copy-done.1
  52.6 43.6 %all-gather.4.cloned.1.call-done = bf16[1,1024,3072]{2,1,0:T(8,128)(2,1)} async-done(((bf16[1,128,3072]{2,1,0:T(8,128)(2,1)}), bf16[1,1024,3072]{2,1,0:T(8,128)(2,1)}) %all-gather.4.cloned.1.call-update) | async-done | bytes 6291472 | tf_op jit(solution)/shard_map/all_gather | solution.py:32
  96.2 5.3 %fusion.24 = bf16[128,1024]{1,0:T(8,128)(2,1)S(1)} fusion(bf16[1,1024,3072]{2,1,0:T(8,128)(2,1)} %all-gather.4.cloned.1.call-done, bf16[1,128,3072]{2,1,0:T(8,128)(2,1)} %param.4), kind=kOutput, calls=%fused_computation.16 | convolution fusion | flops 805437440 | bytes 7340032 | tf_op jit(solution)/shard_map/dot_general | solution.py:36
  102.5 2.2 reduce
  104.7 0.8 reshape.223
  105.5 3.4 %all-to-all-start = ((bf16[8,2,8192]{2,1,0:T(2,128)(2,1)}), bf16[8,2,8192]{2,1,0:T(2,128)(2,1)S(1)}, u32[]{:S(2)}, u32[]{:S(2)}) async-start(bf16[8,2,8192]{2,1,0:T(2,128)(2,1)} %reshape.223), calls=%async_computation | async-start | bytes 524288 | tf_op jit(solution)/shard_map/all_to_all | solution.py:40
  109.0 0.7 fusion.57
  113.5 6.5 %all-to-all-done = bf16[8,2,8192]{2,1,0:T(2,128)(2,1)S(1)} async-done(((bf16[8,2,8192]{2,1,0:T(2,128)(2,1)}), bf16[8,2,8192]{2,1,0:T(2,128)(2,1)S(1)}, u32[]{:S(2)}, u32[]{:S(2)}) %all-to-all-start) | async-done | bytes 262176 | tf_op jit(solution)/shard_map/all_to_all | solution.py:40
  121.3 53.0 %all-gather.6.cloned.1.call-done = bf16[1,1024,3072]{2,1,0:T(8,128)(2,1)} async-done(((bf16[1,128,3072]{2,1,0:T(8,128)(2,1)}), bf16[1,1024,3072]{2,1,0:T(8,128)(2,1)}) %all-gather.6.cloned.1.call-update) | async-done | bytes 6291472 | tf_op jit(solution)/shard_map/all_gather | solution.py:32
  174.2 5.0 %fusion.27 = bf16[128,1024]{1,0:T(8,128)(2,1)S(1)} fusion(bf16[1,1024,3072]{2,1,0:T(8,128)(2,1)} %all-gather.6.cloned.1.call-done, bf16[1,128,3072]{2,1,0:T(8,128)(2,1)S(1)} %copy-done), kind=kOutput, calls=%fused_computation.17 | convolution fusion | flops 805437440 | bytes 7340032 | tf_op jit(solution)/shard_map/dot_general | solution.py:36
  179.6 2.3 reduce.1
  181.9 0.8 reshape.225
  182.6 4.2 %all-to-all-start.1 = ((bf16[8,2,8192]{2,1,0:T(2,128)(2,1)}), bf16[8,2,8192]{2,1,0:T(2,128)(2,1)}, u32[]{:S(2)}, u32[]{:S(2)}) async-start(bf16[8,2,8192]{2,1,0:T(2,128)(2,1)} %reshape.225), calls=%async_computation.1 | async-start | bytes 524288 | tf_op jit(solution)/shard_map/all_to_all | solution.py:40
  186.9 4.4 %fusion.12 = f32[128,3072]{1,0:T(8,128)S(1)} fusion(bf16[1,1024,3072]{2,1,0:T(8,128)(2,1)} %all-gather.4.cloned.1.call-done, f32[1,128,3072]{2,1,0:T(8,128)} %param.7, f32[1,1024,1,128]{1,3,2,0:T(8,128)S(1)} %reshape.217, bf16[128,1024]{1,0:T(8,128)(2,1)S(1)} %fusion.24, f32[1024]{0:T(1024)S(1)} %copy-done.3, f32[128]{0:T(128)S(1)} %get-tuple-element.7), kind=kOutput, calls=%fused_computation.12 | convolution fusion | flops 806486016 | bytes 10228224 | tf_op jit(solution)/shard_map/dot_general | solution.py:52
  191.2 6.5 %all-to-all-done.1 = bf16[8,2,8192]{2,1,0:T(2,128)(2,1)} async-done(((bf16[8,2,8192]{2,1,0:T(2,128)(2,1)}), bf16[8,2,8192]{2,1,0:T(2,128)(2,1)}, u32[]{:S(2)}, u32[]{:S(2)}) %all-to-all-start.1) | async-done | bytes 262176 | tf_op jit(solution)/shard_map/all_to_all | solution.py:40
  197.7 1.2 reshape.226
  199.4 1.1 copy.18
  200.5 1.1 reshape.218
  201.7 50.8 %all-gather.8.cloned.1.call-done = bf16[1,1024,3072]{2,1,0:T(8,128)(2,1)} async-done(((bf16[1,128,3072]{2,1,0:T(8,128)(2,1)}), bf16[1,1024,3072]{2,1,0:T(8,128)(2,1)}) %all-gather.8.cloned.1.call-update) | async-done | bytes 6291472 | tf_op jit(solution)/shard_map/all_gather | solution.py:32
  252.5 5.0 %fusion.30 = bf16[128,1024]{1,0:T(8,128)(2,1)S(1)} fusion(bf16[1,1024,3072]{2,1,0:T(8,128)(2,1)} %all-gather.8.cloned.1.call-done, bf16[1,128,3072]{2,1,0:T(8,128)(2,1)S(1)} %copy-done), kind=kOutput, calls=%fused_computation.18 | convolution fusion | flops 805437440 | bytes 7340032 | tf_op jit(solution)/shard_map/dot_general | solution.py:36
  257.9 2.3 reduce.2
  260.1 0.8 reshape.227
  260.9 3.4 %all-to-all-start.2 = ((bf16[8,2,8192]{2,1,0:T(2,128)(2,1)}), bf16[8,2,8192]{2,1,0:T(2,128)(2,1)S(1)}, u32[]{:S(2)}, u32[]{:S(2)}) async-start(bf16[8,2,8192]{2,1,0:T(2,128)(2,1)} %reshape.227), calls=%async_computation.2 | async-start | bytes 524288 | tf_op jit(solution)/shard_map/all_to_all | solution.py:40
  264.3 5.0 %fusion.15 = f32[128,3072]{1,0:T(8,128)} fusion(f32[128,3072]{1,0:T(8,128)S(1)} %fusion.12, bf16[1,1024,3072]{2,1,0:T(8,128)(2,1)} %all-gather.6.cloned.1.call-done, f32[1,1024,1,128]{1,3,2,0:T(8,128)S(1)} %reshape.218, bf16[128,1024]{1,0:T(8,128)(2,1)S(1)} %fusion.27, f32[128]{0:T(128)S(1)} %get-tuple-element.6, f32[1024]{0:T(1024)S(1)} %copy-done.3), kind=kOutput, calls=%fused_computation.13 | convolution fusion | flops 806486016 | bytes 10228224 | tf_op jit(solution)/shard_map/dot_general | solution.py:52
  269.4 1.1 all-to-all-done.2
  271.7 5.5 %fusion.21 = f32[1,128,3072]{2,1,0:T(8,128)} fusion(f32[128,3072]{1,0:T(8,128)} %fusion.15, bf16[1,1024,3072]{2,1,0:T(8,128)(2,1)} %all-gather.8.cloned.1.call-done, f32[1,1024,1,128]{1,3,2,0:T(8,128)S(1)} %reshape.219, bf16[128,1024]{1,0:T(8,128)(2,1)S(1)} %fusion.30, f32[128]{0:T(128)S(1)} %get-tuple-element.5, f32[1024]{0:T(1024)S(1)} %copy-done.3), kind=kOutput, calls=%fused_computation.15 | convolution fusion | flops 806486016 | bytes 10228224 | tf_op jit(solution)/shard_map/dot_general | solution.py:52
  (27 shorter events, 4.9 us)
Async XLA Ops:
  6.5 102.5 %copy-start.4 = (f32[32]{0:T(128)S(1)}, f32[32]{0:T(128)}, u32[]{:S(2)}) copy-start(f32[32]{0:T(128)} %param.5) | copy-start | bytes 388
  6.5 106.9 %copy-start.3 = (f32[1024]{0:T(1024)S(1)}, f32[1024]{0:T(1024)}, u32[]{:S(2)}) copy-start(f32[1024]{0:T(1024)} %param.6) | copy-start | bytes 12292
  6.5 89.7 %all-gather.4.cloned.1.call-start = ((), (), s32[]{:S(2)}) async-start(), calls=%async_computation.3 | async-start | bytes 7077888 | tf_op jit(solution)/shard_map/all_gather | solution.py:32
  7.3 167.0 %all-gather.6.cloned.1.call-start = ((), (), s32[]{:S(2)}) async-start(), calls=%async_computation.4 | async-start | bytes 7077888 | tf_op jit(solution)/shard_map/all_gather | solution.py:32
  7.3 13.5 %collective-permute-start = (bf16[1,128,3072]{2,1,0:T(8,128)(2,1)}, bf16[1,128,3072]{2,1,0:T(8,128)(2,1)S(1)}, u32[]{:S(2)}, u32[]{:S(2)}) collective-permute-start(bf16[1,128,3072]{2,1,0:T(8,128)(2,1)} %param.4), channel_id=1, source_target_pairs={{248,0},{0,8},{8,16},{16,24},{24,32},{32,40},{40,48},{48,56},{56,6... | collective-permute-start | bytes 2359304 | tf_op jit(solution)/shard_map/ppermute | solution.py:12
  20.8 0.9 copy-start.2
  21.7 230.8 %all-gather.8.cloned.1.call-start = ((), (), s32[]{:S(2)}) async-start(), calls=%async_computation.5 | async-start | bytes 7077888 | tf_op jit(solution)/shard_map/all_gather | solution.py:32
  21.7 29.9 %collective-permute-start.1 = (bf16[1,128,3072]{2,1,0:T(8,128)(2,1)}, bf16[1,128,3072]{2,1,0:T(8,128)(2,1)S(1)}, u32[]{:S(2)}, u32[]{:S(2)}) collective-permute-start(bf16[1,128,3072]{2,1,0:T(8,128)(2,1)} %copy-done.2), channel_id=1, source_target_pairs={{248,0},{0,8},{8,16},{16,24},{24,32},{32,40},{40,48},{48,56},{56,6... | collective-permute-start | bytes 2359304 | tf_op jit(solution)/shard_map/ppermute | solution.py:12
  51.7 0.9 copy-start.1
  52.6 121.6 %copy-start = (bf16[1,128,3072]{2,1,0:T(8,128)(2,1)S(1)}, bf16[1,128,3072]{2,1,0:T(8,128)(2,1)}, u32[]{:S(2)}) copy-start(bf16[1,128,3072]{2,1,0:T(8,128)(2,1)} %param.4) | copy-start | bytes 2359300
  105.5 14.5 %all-to-all-start = ((bf16[8,2,8192]{2,1,0:T(2,128)(2,1)}), bf16[8,2,8192]{2,1,0:T(2,128)(2,1)S(1)}, u32[]{:S(2)}, u32[]{:S(2)}) async-start(bf16[8,2,8192]{2,1,0:T(2,128)(2,1)} %reshape.223), calls=%async_computation | async-start | bytes 524288 | tf_op jit(solution)/shard_map/all_to_all | solution.py:40
  182.6 15.1 %all-to-all-start.1 = ((bf16[8,2,8192]{2,1,0:T(2,128)(2,1)}), bf16[8,2,8192]{2,1,0:T(2,128)(2,1)}, u32[]{:S(2)}, u32[]{:S(2)}) async-start(bf16[8,2,8192]{2,1,0:T(2,128)(2,1)} %reshape.225), calls=%async_computation.1 | async-start | bytes 524288 | tf_op jit(solution)/shard_map/all_to_all | solution.py:40
  260.9 9.6 %all-to-all-start.2 = ((bf16[8,2,8192]{2,1,0:T(2,128)(2,1)}), bf16[8,2,8192]{2,1,0:T(2,128)(2,1)S(1)}, u32[]{:S(2)}, u32[]{:S(2)}) async-start(bf16[8,2,8192]{2,1,0:T(2,128)(2,1)} %reshape.227), calls=%async_computation.2 | async-start | bytes 524288 | tf_op jit(solution)/shard_map/all_to_all | solution.py:40
Sparse Core Ops, SparseCore 0:
  9.1 87.0 all-gather.3
  98.0 76.1 all-gather.5
  176.0 76.4 all-gather.7
where the time goes:
time: 284 us
  waiting for transfers between devices  197 us (69%)
  matrix products  30.1 us (11%)
  starting transfers between devices  19.3 us (7%)
  between operations  17.1 us (6%)
  local copies, waits for them, and re-layouts  11.3 us (4%)
  other arithmetic  8.46 us (3%)
    all_gather x3, waiting for transfers between devices, on_device(): partner = lax.all_gather(partner_shard, 'vir', axis=1, tiled=True)  147 us
    ppermute x2, waiting for transfers between devices, passed_along(): return lax.ppermute(block, axis, route)  35.2 us
    dot_general x3, matrix products, on_device(): lax.dot_general(flat_own, flat_partner, (((1,), (1,)), ((), ())), preferr...  15.2 us
    dot_general x3, matrix products, on_device(): jnp.dot(amp.reshape(occ_rows * vir_local, occ_rows * vir_whole), flat_par...  14.9 us
    all_to_all x3, waiting for transfers between devices, on_device(): lax.all_to_all(direct, 'vir', split_axis=3, concat_axis=1, tiled=True)  14.1 us
    all_to_all x3, starting transfers between devices, on_device(): lax.all_to_all(direct, 'vir', split_axis=3, concat_axis=1, tiled=True)  11 us
    ppermute x2, starting transfers between devices, passed_along(): return lax.ppermute(block, axis, route)  8.17 us
    unnamed x3, other arithmetic  6.75 us
  transfers between devices with their start and end apart: 8, of which 8 were waited for; matrix products, arithmetic and copies ran while one was open for 12% of the time, Pallas kernels for 0%

commit v1 on v0

v1 whole, which is shorter than its diff:
```python
import functools

import jax
import jax.numpy as jnp
from jax import lax
from jax.experimental import pallas as pl
from jax.experimental.pallas import tpu as pltpu
from jax.sharding import Mesh
from jax.sharding import PartitionSpec as P

Z, XH, CORE, XL, Y = 8, 2, 2, 2, 4
GROUPS = Z * XH
AXES = ("z", "xh", "core", "xl", "y")
PLACE = ("z", "xh", "core", "xl")
SLAB = 128
N_SLABS = CORE * Y
STEP = 512
BF16, F32 = jnp.bfloat16, jnp.float32


def place(group, core, xl):
    return ((group % GROUPS) * CORE + core) * XL + xl


def homes_of_workers(shift):
    pairs = []
    for g in range(GROUPS):
        for c in range(CORE):
            for r in range(XL):
                i = 2 * g + r + shift
                pairs.append((place(i // 2, i % 2, c), place(g, c, r)))
    return pairs


def to_workers(block, shift):
    return lax.ppermute(block, PLACE, homes_of_workers(shift))


def to_homes(block, shift):
    return lax.ppermute(block, PLACE, [(w, h) for h, w in homes_of_workers(shift)])


def along_y(block, step):
    pairs = []
    for c in range(CORE):
        sign = 1 - 2 * c
        for y in range(Y):
            pairs.append((c * Y + y, c * Y + (y + sign * step) % Y))
    return lax.ppermute(block, ("core", "y"), pairs)


def to_sibling(block):
    return lax.ppermute(block, "core", [(0, 1), (1, 0)])


def slab_of(q):
    core, y = lax.axis_index("core"), lax.axis_index("y")
    kind, sibling = q // 2, q % 2
    core = 1 - core if sibling else core
    sign = 1 - 2 * core
    y = lax.rem(y + sign * (0, -1, 1, 2)[kind] + 2 * Y, Y)
    return core * Y + y


def integrals_kernel(*refs):
    rows, pieces = refs[:3], refs[3 : 3 + N_SLABS]
    direct_ref, sent_ref, total = refs[3 + N_SLABS :]
    k = pl.program_id(0)
    left = jnp.concatenate([r[...] for r in rows], axis=0)
    right = jnp.concatenate([r[...] for r in pieces], axis=0)
    part = lax.dot_general(left, right, (((1,), (1,)), ((), ())), preferred_element_type=F32)

    @pl.when(k == 0)
    def _():
        total[...] = part

    @pl.when(k > 0)
    def _():
        total[...] += part

    @pl.when(k == pl.num_programs(0) - 1)
    def _():
        direct_ref[...] = total[...].astype(BF16)
        for q in range(N_SLABS):
            for v in range(2):
                tile = total[(v + 1) * SLAB : (v + 2) * SLAB, q * SLAB : (q + 1) * SLAB]
                sent_ref[slab_of(q), v] = tile.T.astype(BF16)


def integrals(rows, pieces):
    width = rows[0].shape[1]
    spec = pl.BlockSpec((SLAB, STEP), lambda k: (0, k))
    return pl.pallas_call(
        integrals_kernel,
        grid=(width // STEP,),
        in_specs=[spec] * (3 + N_SLABS),
        out_specs=[
            pl.BlockSpec((3 * SLAB, N_SLABS * SLAB), lambda k: (0, 0)),
            pl.BlockSpec((N_SLABS, 2, SLAB, SLAB), lambda k: (0, 0, 0, 0)),
        ],
        out_shape=[
            jax.ShapeDtypeStruct((3 * SLAB, N_SLABS * SLAB), BF16),
            jax.ShapeDtypeStruct((N_SLABS, 2, SLAB, SLAB), BF16),
        ],
        scratch_shapes=[pltpu.VMEM((3 * SLAB, N_SLABS * SLAB), F32)],
        cost_estimate=pl.CostEstimate(
            flops=2 * 3 * SLAB * N_SLABS * SLAB * width,
            bytes_accessed=(3 + N_SLABS) * SLAB * width * 2,
            transcendentals=0,
        ),
        compiler_params=pltpu.CompilerParams(vmem_limit_bytes=40 << 20),
        name="integrals",
    )(*rows, *pieces)


def density_kernel(visits, has_swapped, *refs):
    e_occ, e_vir, direct_ref = refs[:3]
    at = 3
    if has_swapped:
        swapped_ref = refs[at]
        at += 1
    pieces, refs = refs[at : at + N_SLABS], refs[at + N_SLABS :]
    outs, amp = refs[: len(visits)], refs[len(visits)]
    k = pl.program_id(0)

    @pl.when(k == 0)
    def _():
        group = lax.axis_index("z") * XH + lax.axis_index("xh")
        j = 2 * group + lax.axis_index("xl")
        own = slab_of(0)
        e_a = jnp.broadcast_to(e_vir[own], (SLAB, SLAB)).T
        for n, v in enumerate(visits):
            pair = e_occ[lax.rem(j + v, 2 * GROUPS)] + e_occ[j]
            for q in range(N_SLABS):
                slab = slab_of(q)
                d = direct_ref[v * SLAB : (v + 1) * SLAB, q * SLAB : (q + 1) * SLAB].astype(F32)
                s = d if v == 0 else swapped_ref[slab, v - 1].astype(F32)
                denom = pair - e_a - e_vir[slab]
                amp[n * SLAB : (n + 1) * SLAB, q * SLAB : (q + 1) * SLAB] = ((2.0 * d - s) / denom).astype(BF16)

    right = jnp.concatenate([r[...] for r in pieces], axis=0)
    out = jnp.dot(amp[...], right, preferred_element_type=F32)
    for n in range(len(visits)):
        outs[n][...] = out[n * SLAB : (n + 1) * SLAB].astype(BF16)


def density(visits, e_occ, e_vir, direct, swapped, pieces):
    width = pieces[0].shape[1]
    spec = pl.BlockSpec((SLAB, STEP), lambda k: (0, k))
    whole = lambda *shape: pl.BlockSpec(shape, lambda k: (0,) * len(shape))
    has_swapped = swapped is not None
    rows = len(visits) * SLAB
    return pl.pallas_call(
        functools.partial(density_kernel, visits, has_swapped),
        grid=(width // STEP,),
        in_specs=[pl.BlockSpec(memory_space=pltpu.SMEM), whole(N_SLABS, 1, SLAB), whole(3 * SLAB, N_SLABS * SLAB)]
        + ([whole(N_SLABS, 2, SLAB, SLAB)] if has_swapped else [])
        + [spec] * N_SLABS,
        out_specs=[spec] * len(visits),
        out_shape=[jax.ShapeDtypeStruct((SLAB, width), BF16)] * len(visits),
        scratch_shapes=[pltpu.VMEM((rows, N_SLABS * SLAB), BF16)],
        cost_estimate=pl.CostEstimate(
            flops=2 * rows * N_SLABS * SLAB * width,
            bytes_accessed=(len(visits) + N_SLABS) * SLAB * width * 2,
            transcendentals=0,
        ),
        compiler_params=pltpu.CompilerParams(vmem_limit_bytes=40 << 20),
        name="density",
    )(e_occ, e_vir, direct, *([swapped] if has_swapped else []), *pieces)


def on_device(factors, occ_energy, vir_energy, density_in):
    width = factors.shape[2]
    home = factors.reshape(SLAB, width)
    own = to_workers(home, 0)
    next_1 = to_workers(home, 1)
    next_2 = to_workers(home, 2)
    one = along_y(own, 1)
    other = along_y(own, -1)
    two = along_y(one, 1)
    mine = [own, one, other, two]
    pieces = []
    for piece in mine:
        pieces += [piece, to_sibling(piece)]
    e_vir = vir_energy.reshape(N_SLABS, 1, SLAB)
    direct, sent = integrals([own, next_1, next_2], pieces)
    swapped = lax.all_to_all(sent, ("core", "y"), split_axis=0, concat_axis=0, tiled=True)
    (part_0,) = density((0,), occ_energy, e_vir, direct, None, pieces)
    part_1, part_2 = density((1, 2), occ_energy, e_vir, direct, swapped, pieces)
    total = density_in.reshape(SLAB, width)
    for shift, part in enumerate((part_0, part_1, part_2)):
        total = total + to_homes(part, shift).astype(F32)
    return total.reshape(density_in.shape)


def solution(mesh):
    fine = Mesh(mesh.devices.reshape(Z, XH, CORE, XL, Y), AXES)
    split = P(("z", "xh", "core"), ("xl", "y"), None)
    return jax.shard_map(
        on_device,
        mesh=fine,
        in_specs=(split, P(), P(), split),
        out_specs=split,
        check_vma=False,
    )
```

time: 284 us -> 136 us (0.48)
  the two profiles are of different devices: /device:TPU:1 before, /device:TPU:10 now
where the time goes in v1:
time: 136 us; the launch traced here: 135 us
  waiting for transfers between devices  79 us (58%)
  starting transfers between devices  25 us (18%)
  Pallas kernels  14.8 us (11%)
  local copies, waits for them, and re-layouts  13 us (10%)
  other arithmetic  2.67 us (2%)
    ppermute x3, waiting for transfers between devices, to_homes(): lax.ppermute(block, PLACE, [(w, h) for h, w in homes_of_workers(shift)])  34.6 us
    ppermute x3, waiting for transfers between devices, to_workers(): return lax.ppermute(block, PLACE, homes_of_workers(shift))  26.9 us
    ppermute x3, waiting for transfers between devices, along_y(): return lax.ppermute(block, ('core', 'y'), pairs)  17.5 us
    unnamed x38, local copies, waits for them, and re-layouts  13 us
    ppermute x3, starting transfers between devices, to_homes(): lax.ppermute(block, PLACE, [(w, h) for h, w in homes_of_workers(shift)])  10.5 us
    pallas_call x2, Pallas kernels, density(): pl.pallas_call(functools.partial(density_kernel, visits, has_swapped), gr...  9.32 us
    ppermute x3, starting transfers between devices, to_workers(): return lax.ppermute(block, PLACE, homes_of_workers(shift))  5.54 us
    pallas_call x1, Pallas kernels, integrals(): pl.pallas_call(integrals_kernel, grid=(width // STEP,), in_specs=[spec] *...  5.48 us
  transfers between devices with their start and end apart: 14, of which 6 were waited for; matrix products, arithmetic and copies ran while one was open for 0% of the time, Pallas kernels for 7%

profile of v1, /device:TPU:10, one launch (start us, length us, event | category | flops | bytes accessed | tf_op | source)
XLA Modules:
  0.0 134.7 jit_solution(10992075212279548357)
XLA Ops:
  0.0 2.0 %collective-permute-start = (bf16[128,3072]{1,0:T(8,128)(2,1)}, bf16[128,3072]{1,0:T(8,128)(2,1)S(1)}, u32[]{:S(2)}, u32[]{:S(2)}) collective-permute-start(bf16[128,3072]{1,0:T(8,128)(2,1)} %bitcast.14), channel_id=1, source_target_pairs={{0,0},{8,4},{4,8},{12,12},{16,16},{24,20},{20,24},{28,28},{32,32},... | collective-permute-start | bytes 2359304 | tf_op jit(solution)/shard_map/ppermute | solution.py:36
  2.1 11.6 %collective-permute-done.refs_0_.refs_3_.refs_4_ = bf16[128,3072]{1,0:T(8,128)(2,1)S(1)} collective-permute-done((bf16[128,3072]{1,0:T(8,128)(2,1)}, bf16[128,3072]{1,0:T(8,128)(2,1)S(1)}, u32[]{:S(2)}, u32[]{:S(2)}) %collective-permute-start) | collective-permute-done | bytes 786464 | tf_op jit(solution)/shard_map/ppermute | solution.py:36
  13.6 1.6 %collective-permute-start.4 = (bf16[128,3072]{1,0:T(8,128)(2,1)S(1)}, bf16[128,3072]{1,0:T(8,128)(2,1)S(1)}, u32[]{:S(2)}, u32[]{:S(2)}) collective-permute-start(bf16[128,3072]{1,0:T(8,128)(2,1)S(1)} %collective-permute-done.refs_0_.refs_3_.refs_4_), channel_id=1, source_target_pairs={{0,1},{1,2},{2,3},{3,0},{8,11},{9,8},{10,9},{11,10},{4,5},{5,6},{6... | collective-permute-start | bytes 2359304 | tf_op jit(solution)/shard_map/ppermute | solution.py:49
  15.2 0.4 collective-permute-start.6
  15.7 17.5 %collective-permute-done.4.refs_5_.refs_6_ = bf16[128,3072]{1,0:T(8,128)(2,1)S(1)} collective-permute-done((bf16[128,3072]{1,0:T(8,128)(2,1)S(1)}, bf16[128,3072]{1,0:T(8,128)(2,1)S(1)}, u32[]{:S(2)}, u32[]{:S(2)}) %collective-permute-start.4) | collective-permute-done | bytes 786464 | tf_op jit(solution)/shard_map/ppermute | solution.py:49
  33.2 2.1 %collective-permute-start.8 = (bf16[128,3072]{1,0:T(8,128)(2,1)S(1)}, bf16[128,3072]{1,0:T(8,128)(2,1)S(1)}, u32[]{:S(2)}, u32[]{:S(2)}) collective-permute-start(bf16[128,3072]{1,0:T(8,128)(2,1)S(1)} %collective-permute-done.4.refs_5_.refs_6_), channel_id=1, source_target_pairs={{0,1},{1,2},{2,3},{3,0},{8,11},{9,8},{10,9},{11,10},{4,5},{5,6},{6... | collective-permute-start | bytes 2359304 | tf_op jit(solution)/shard_map/ppermute | solution.py:49
  35.3 3.5 %collective-permute-start.2 = (bf16[128,3072]{1,0:T(8,128)(2,1)}, bf16[128,3072]{1,0:T(8,128)(2,1)S(1)}, u32[]{:S(2)}, u32[]{:S(2)}) collective-permute-start(bf16[128,3072]{1,0:T(8,128)(2,1)} %bitcast.16), channel_id=1, source_target_pairs={{16,0},{24,4},{20,8},{28,12},{32,16},{40,20},{36,24},{44,28},{48,3... | collective-permute-start | bytes 2359304 | tf_op jit(solution)/shard_map/ppermute | solution.py:36
  38.8 6.7 %collective-permute-done.1.refs_1_ = bf16[128,3072]{1,0:T(8,128)(2,1)S(1)} collective-permute-done((bf16[128,3072]{1,0:T(8,128)(2,1)}, bf16[128,3072]{1,0:T(8,128)(2,1)S(1)}, u32[]{:S(2)}, u32[]{:S(2)}) %collective-permute-start.1) | collective-permute-done | bytes 786464 | tf_op jit(solution)/shard_map/ppermute | solution.py:36
  45.4 0.5 collective-permute-start.7
  46.0 8.6 %collective-permute-done.2.refs_2_ = bf16[128,3072]{1,0:T(8,128)(2,1)S(1)} collective-permute-done((bf16[128,3072]{1,0:T(8,128)(2,1)}, bf16[128,3072]{1,0:T(8,128)(2,1)S(1)}, u32[]{:S(2)}, u32[]{:S(2)}) %collective-permute-start.2) | collective-permute-done | bytes 786464 | tf_op jit(solution)/shard_map/ppermute | solution.py:36
  54.7 5.5 %integrals.1 = (bf16[384,1024]{1,0:T(8,128)(2,1)S(1)}, bf16[8,2,128,128]{3,2,1,0:T(8,128)(2,1)S(1)}) custom-call(bf16[128,3072]{1,0:T(8,128)(2,1)S(1)} %collective-permute-done.refs_0_.refs_3_.refs_4_, bf16[128,3072]{1,0:T(8,128)(2,1)S(1)} %collective-permute-done.1.refs_1_, bf16[128,3072]{1,0:T(8,128)(2,1)S(1)} %collective-permute-done.2.refs_2_, ...), custom_call_target="tpu_custom_call" | custom-call | flops 2415919104 | bytes 8650752 | tf_op jit(solution)/shard_map/integrals/pallas_call | solution.py:93
  60.2 0.9 copy-done.12
  61.1 0.8 copy-done.15
  61.9 4.3 %all-to-all-start = ((bf16[8,2,128,128]{3,2,1,0:T(8,128)(2,1)}), bf16[8,2,128,128]{3,2,1,0:T(8,128)(2,1)}, u32[]{:S(2)}, u32[]{:S(2)}) async-start(bf16[8,2,128,128]{3,2,1,0:T(8,128)(2,1)} %copy-done.15), calls=%async_computation | async-start | bytes 1048576 | tf_op jit(solution)/shard_map/all_to_all | solution.py:187
  66.2 1.1 copy-done.1
  67.3 1.1 copy-done.4
  68.5 1.1 copy-done.7
  69.6 1.1 copy-done.10
  70.7 1.1 copy-done.13
  71.9 4.4 %density.2 = bf16[128,3072]{1,0:T(8,128)(2,1)} custom-call(f32[32]{0:T(128)S(1)} %copy-done.17, f32[8,1,128]{2,1,0:T(1,128)S(1)} %bitcast.12, bf16[384,1024]{1,0:T(8,128)(2,1)S(1)} %copy-done.13, bf16[128,3072]{1,0:T(8,128)(2,1)S(1)} %collective-permute-done.refs_0_.refs_3_.refs_4_, bf16[128,3072]{1,0:T(8,128)(2,1)S(1)} %copy-done.1, ...), custom_call_target="tpu_custom_call" | custom-call | flops 805306368 | bytes 7077888 | tf_op jit(solution)/shard_map/density/pallas_call | solution.py:153
  76.3 4.7 %collective-permute-start.10 = (bf16[128,3072]{1,0:T(8,128)(2,1)}, bf16[128,3072]{1,0:T(8,128)(2,1)}, u32[]{:S(2)}, u32[]{:S(2)}) collective-permute-start(bf16[128,3072]{1,0:T(8,128)(2,1)} %density.2), channel_id=1, source_target_pairs={{0,0},{4,8},{8,4},{12,12},{16,16},{20,24},{24,20},{28,28},{32,32},... | collective-permute-start | bytes 2359304 | tf_op jit(solution)/shard_map/ppermute | solution.py:40
  81.0 1.1 copy-done.2
  82.1 1.1 copy-done.5
  83.3 1.1 copy-done.8
  84.4 1.1 copy-done.11
  85.5 1.1 copy-done.14
  86.7 4.9 %density.3 = (bf16[128,3072]{1,0:T(8,128)(2,1)S(1)}, bf16[128,3072]{1,0:T(8,128)(2,1)S(1)}) custom-call(f32[32]{0:T(128)S(1)} %copy-done.17, f32[8,1,128]{2,1,0:T(1,128)S(1)} %bitcast.13, bf16[384,1024]{1,0:T(8,128)(2,1)S(1)} %copy-done.14, bf16[8,2,128,128]{3,2,1,0:T(8,128)(2,1)} %all-to-all-done.refs_3_, ...), custom_call_target="tpu_custom_call" | custom-call | flops 1610612736 | bytes 7864320 | tf_op jit(solution)/shard_map/density/pallas_call | solution.py:153
  91.6 1.0 collective-permute-start.12
  92.6 4.8 %collective-permute-start.11 = (bf16[128,3072]{1,0:T(8,128)(2,1)S(1)}, bf16[128,3072]{1,0:T(8,128)(2,1)S(1)}, u32[]{:S(2)}, u32[]{:S(2)}) collective-permute-start(bf16[128,3072]{1,0:T(8,128)(2,1)S(1)} %get-tuple-element.11), channel_id=1, source_target_pairs={{0,8},{4,16},{8,12},{12,20},{16,24},{20,32},{24,28},{28,36},{32,40... | collective-permute-start | bytes 2359304 | tf_op jit(solution)/shard_map/ppermute | solution.py:40
  97.4 13.4 %collective-permute-done.12 = bf16[128,3072]{1,0:T(8,128)(2,1)S(1)} collective-permute-done((bf16[128,3072]{1,0:T(8,128)(2,1)S(1)}, bf16[128,3072]{1,0:T(8,128)(2,1)S(1)}, u32[]{:S(2)}, u32[]{:S(2)}) %collective-permute-start.12) | collective-permute-done | bytes 786464 | tf_op jit(solution)/shard_map/ppermute | solution.py:40
  110.8 21.2 %collective-permute-done.11 = bf16[128,3072]{1,0:T(8,128)(2,1)S(1)} collective-permute-done((bf16[128,3072]{1,0:T(8,128)(2,1)S(1)}, bf16[128,3072]{1,0:T(8,128)(2,1)S(1)}, u32[]{:S(2)}, u32[]{:S(2)}) %collective-permute-start.11) | collective-permute-done | bytes 786464 | tf_op jit(solution)/shard_map/ppermute | solution.py:40
  132.0 2.7 %fusion.2 = f32[1,128,3072]{2,1,0:T(8,128)} fusion(f32[1,128,3072]{2,1,0:T(8,128)S(1)} %copy-done.18, bf16[128,3072]{1,0:T(8,128)(2,1)S(1)} %collective-permute-done.12, bf16[128,3072]{1,0:T(8,128)(2,1)S(1)} %collective-permute-done.11, bf16[128,3072]{1,0:T(8,128)(2,1)} %collective-permute-done.10), kind=kLoop, calls=%fused_computation.3 | loop fusion | flops 2359296 | bytes 5505024 | tf_op jit(solution)/shard_map/reshape | solution.py:193
  (38 shorter events, 0.2 us)
Async XLA Ops:
  0.0 66.2 %copy-start.16 = (f32[1024]{0:T(1024)S(1)}, f32[1024]{0:T(1024)}, u32[]{:S(2)}) copy-start(f32[1024]{0:T(1024)} %param.6) | copy-start | bytes 12292
  0.0 66.2 %copy-start.17 = (f32[32]{0:T(128)S(1)}, f32[32]{0:T(128)}, u32[]{:S(2)}) copy-start(f32[32]{0:T(128)} %refs_0_.3) | copy-start | bytes 388
  0.0 13.6 %collective-permute-start = (bf16[128,3072]{1,0:T(8,128)(2,1)}, bf16[128,3072]{1,0:T(8,128)(2,1)S(1)}, u32[]{:S(2)}, u32[]{:S(2)}) collective-permute-start(bf16[128,3072]{1,0:T(8,128)(2,1)} %bitcast.14), channel_id=1, source_target_pairs={{0,0},{8,4},{4,8},{12,12},{16,16},{24,20},{20,24},{28,28},{32,32},... | collective-permute-start | bytes 2359304 | tf_op jit(solution)/shard_map/ppermute | solution.py:36
  13.6 19.5 %collective-permute-start.4 = (bf16[128,3072]{1,0:T(8,128)(2,1)S(1)}, bf16[128,3072]{1,0:T(8,128)(2,1)S(1)}, u32[]{:S(2)}, u32[]{:S(2)}) collective-permute-start(bf16[128,3072]{1,0:T(8,128)(2,1)S(1)} %collective-permute-done.refs_0_.refs_3_.refs_4_), channel_id=1, source_target_pairs={{0,1},{1,2},{2,3},{3,0},{8,11},{9,8},{10,9},{11,10},{4,5},{5,6},{6... | collective-permute-start | bytes 2359304 | tf_op jit(solution)/shard_map/ppermute | solution.py:49
  15.2 30.2 %collective-permute-start.1 = (bf16[128,3072]{1,0:T(8,128)(2,1)}, bf16[128,3072]{1,0:T(8,128)(2,1)S(1)}, u32[]{:S(2)}, u32[]{:S(2)}) collective-permute-start(bf16[128,3072]{1,0:T(8,128)(2,1)} %bitcast.15), channel_id=1, source_target_pairs={{8,0},{16,4},{12,8},{20,12},{24,16},{32,20},{28,24},{36,28},{40,32... | collective-permute-start | bytes 2359304 | tf_op jit(solution)/shard_map/ppermute | solution.py:36
  15.2 30.2 %collective-permute-start.6 = (bf16[128,3072]{1,0:T(8,128)(2,1)S(1)}, bf16[128,3072]{1,0:T(8,128)(2,1)S(1)}, u32[]{:S(2)}, u32[]{:S(2)}) collective-permute-start(bf16[128,3072]{1,0:T(8,128)(2,1)S(1)} %collective-permute-done.refs_0_.refs_3_.refs_4_), channel_id=1, source_target_pairs={{0,3},{1,0},{2,1},{3,2},{8,9},{9,10},{10,11},{11,8},{4,7},{5,4},{6... | collective-permute-start | bytes 2359304 | tf_op jit(solution)/shard_map/ppermute | solution.py:49
  33.2 12.8 %collective-permute-start.8 = (bf16[128,3072]{1,0:T(8,128)(2,1)S(1)}, bf16[128,3072]{1,0:T(8,128)(2,1)S(1)}, u32[]{:S(2)}, u32[]{:S(2)}) collective-permute-start(bf16[128,3072]{1,0:T(8,128)(2,1)S(1)} %collective-permute-done.4.refs_5_.refs_6_), channel_id=1, source_target_pairs={{0,1},{1,2},{2,3},{3,0},{8,11},{9,8},{10,9},{11,10},{4,5},{5,6},{6... | collective-permute-start | bytes 2359304 | tf_op jit(solution)/shard_map/ppermute | solution.py:49
  35.3 19.4 %collective-permute-start.2 = (bf16[128,3072]{1,0:T(8,128)(2,1)}, bf16[128,3072]{1,0:T(8,128)(2,1)S(1)}, u32[]{:S(2)}, u32[]{:S(2)}) collective-permute-start(bf16[128,3072]{1,0:T(8,128)(2,1)} %bitcast.16), channel_id=1, source_target_pairs={{16,0},{24,4},{20,8},{28,12},{32,16},{40,20},{36,24},{44,28},{48,3... | collective-permute-start | bytes 2359304 | tf_op jit(solution)/shard_map/ppermute | solution.py:36
  38.8 15.9 %collective-permute-start.3 = (bf16[128,3072]{1,0:T(8,128)(2,1)S(1)}, bf16[128,3072]{1,0:T(8,128)(2,1)S(1)}, u32[]{:S(2)}, u32[]{:S(2)}) collective-permute-start(bf16[128,3072]{1,0:T(8,128)(2,1)S(1)} %collective-permute-done.refs_0_.refs_3_.refs_4_), channel_id=1, source_target_pairs={{0,8},{8,0},{1,9},{9,1},{2,10},{10,2},{3,11},{11,3},{4,12},{12,4},... | collective-permute-start | bytes 2359304 | tf_op jit(solution)/shard_map/ppermute | solution.py:53
  45.4 9.2 %collective-permute-start.5 = (bf16[128,3072]{1,0:T(8,128)(2,1)S(1)}, bf16[128,3072]{1,0:T(8,128)(2,1)S(1)}, u32[]{:S(2)}, u32[]{:S(2)}) collective-permute-start(bf16[128,3072]{1,0:T(8,128)(2,1)S(1)} %collective-permute-done.4.refs_5_.refs_6_), channel_id=1, source_target_pairs={{0,8},{8,0},{1,9},{9,1},{2,10},{10,2},{3,11},{11,3},{4,12},{12,4},... | collective-permute-start | bytes 2359304 | tf_op jit(solution)/shard_map/ppermute | solution.py:53
  45.4 9.2 %collective-permute-start.7 = (bf16[128,3072]{1,0:T(8,128)(2,1)S(1)}, bf16[128,3072]{1,0:T(8,128)(2,1)S(1)}, u32[]{:S(2)}, u32[]{:S(2)}) collective-permute-start(bf16[128,3072]{1,0:T(8,128)(2,1)S(1)} %collective-permute-done.6.refs_7_.refs_8_), channel_id=1, source_target_pairs={{0,8},{8,0},{1,9},{9,1},{2,10},{10,2},{3,11},{11,3},{4,12},{12,4},... | collective-permute-start | bytes 2359304 | tf_op jit(solution)/shard_map/ppermute | solution.py:53
  45.9 8.7 %collective-permute-start.9 = (bf16[128,3072]{1,0:T(8,128)(2,1)S(1)}, bf16[128,3072]{1,0:T(8,128)(2,1)S(1)}, u32[]{:S(2)}, u32[]{:S(2)}) collective-permute-start(bf16[128,3072]{1,0:T(8,128)(2,1)S(1)} %collective-permute-done.8.refs_9_.refs_10_), channel_id=1, source_target_pairs={{0,8},{8,0},{1,9},{9,1},{2,10},{10,2},{3,11},{11,3},{4,12},{12,4},... | collective-permute-start | bytes 2359304 | tf_op jit(solution)/shard_map/ppermute | solution.py:53
  54.7 5.5 %copy-start = (bf16[128,3072]{1,0:T(8,128)(2,1)}, bf16[128,3072]{1,0:T(8,128)(2,1)S(1)}, u32[]{:S(2)}) copy-start(bf16[128,3072]{1,0:T(8,128)(2,1)S(1)} %collective-permute-done.3.refs_4_.refs_5_) | copy-start | bytes 2359300
  54.7 5.5 %copy-start.3 = (bf16[128,3072]{1,0:T(8,128)(2,1)}, bf16[128,3072]{1,0:T(8,128)(2,1)S(1)}, u32[]{:S(2)}) copy-start(bf16[128,3072]{1,0:T(8,128)(2,1)S(1)} %collective-permute-done.5.refs_6_.refs_7_) | copy-start | bytes 2359300
  54.7 5.5 %copy-start.6 = (bf16[128,3072]{1,0:T(8,128)(2,1)}, bf16[128,3072]{1,0:T(8,128)(2,1)S(1)}, u32[]{:S(2)}) copy-start(bf16[128,3072]{1,0:T(8,128)(2,1)S(1)} %collective-permute-done.7.refs_8_.refs_9_) | copy-start | bytes 2359300
  54.7 5.5 %copy-start.9 = (bf16[128,3072]{1,0:T(8,128)(2,1)}, bf16[128,3072]{1,0:T(8,128)(2,1)S(1)}, u32[]{:S(2)}) copy-start(bf16[128,3072]{1,0:T(8,128)(2,1)S(1)} %collective-permute-done.9.refs_10_.refs_11_) | copy-start | bytes 2359300
  60.2 0.9 copy-start.12
  61.9 19.1 %all-to-all-start = ((bf16[8,2,128,128]{3,2,1,0:T(8,128)(2,1)}), bf16[8,2,128,128]{3,2,1,0:T(8,128)(2,1)}, u32[]{:S(2)}, u32[]{:S(2)}) async-start(bf16[8,2,128,128]{3,2,1,0:T(8,128)(2,1)} %copy-done.15), calls=%async_computation | async-start | bytes 1048576 | tf_op jit(solution)/shard_map/all_to_all | solution.py:187
  66.2 1.1 copy-start.1
  67.3 1.1 copy-start.4
  68.5 1.1 copy-start.7
  69.6 1.1 copy-start.10
  70.7 1.1 copy-start.13
  76.3 21.1 %collective-permute-start.10 = (bf16[128,3072]{1,0:T(8,128)(2,1)}, bf16[128,3072]{1,0:T(8,128)(2,1)}, u32[]{:S(2)}, u32[]{:S(2)}) collective-permute-start(bf16[128,3072]{1,0:T(8,128)(2,1)} %density.2), channel_id=1, source_target_pairs={{0,0},{4,8},{8,4},{12,12},{16,16},{20,24},{24,20},{28,28},{32,32},... | collective-permute-start | bytes 2359304 | tf_op jit(solution)/shard_map/ppermute | solution.py:40
  81.0 1.1 copy-start.2
  82.1 1.1 copy-start.5
  83.3 1.1 copy-start.8
  84.4 1.1 copy-start.11
  85.5 1.1 copy-start.14
  86.7 45.3 %copy-start.18 = (f32[1,128,3072]{2,1,0:T(8,128)S(1)}, f32[1,128,3072]{2,1,0:T(8,128)}, u32[]{:S(2)}) copy-start(f32[1,128,3072]{2,1,0:T(8,128)} %param.7) | copy-start | bytes 4718596
  91.6 19.2 %collective-permute-start.12 = (bf16[128,3072]{1,0:T(8,128)(2,1)S(1)}, bf16[128,3072]{1,0:T(8,128)(2,1)S(1)}, u32[]{:S(2)}, u32[]{:S(2)}) collective-permute-start(bf16[128,3072]{1,0:T(8,128)(2,1)S(1)} %get-tuple-element.12), channel_id=1, source_target_pairs={{0,16},{4,24},{8,20},{12,28},{16,32},{20,40},{24,36},{28,44},{32,4... | collective-permute-start | bytes 2359304 | tf_op jit(solution)/shard_map/ppermute | solution.py:40
  92.6 39.4 %collective-permute-start.11 = (bf16[128,3072]{1,0:T(8,128)(2,1)S(1)}, bf16[128,3072]{1,0:T(8,128)(2,1)S(1)}, u32[]{:S(2)}, u32[]{:S(2)}) collective-permute-start(bf16[128,3072]{1,0:T(8,128)(2,1)S(1)} %get-tuple-element.11), channel_id=1, source_target_pairs={{0,8},{4,16},{8,12},{12,20},{16,24},{20,32},{24,28},{28,36},{32,40... | collective-permute-start | bytes 2359304 | tf_op jit(solution)/shard_map/ppermute | solution.py:40
  (1 other events, 0.8 us)

commit v2 on v1

v2 whole, which is shorter than its diff:
```python
import functools

import jax
import jax.numpy as jnp
from jax import lax
from jax.experimental import pallas as pl
from jax.experimental.pallas import tpu as pltpu
from jax.sharding import Mesh
from jax.sharding import PartitionSpec as P

Z, XH, CORE, XL, Y = 8, 2, 2, 2, 4
GROUPS = Z * XH
AXES = ("z", "xh", "core", "xl", "y")
PLACE = ("z", "xh", "core", "xl")
SLAB = 128
N_SLABS = CORE * Y
STEP = 512
EARLY = 6
BF16, F32 = jnp.bfloat16, jnp.float32


def place(group, core, xl):
    return ((group % GROUPS) * CORE + core) * XL + xl


def homes_of_workers(shift):
    pairs = []
    for g in range(GROUPS):
        for c in range(CORE):
            for r in range(XL):
                i = 2 * g + r + shift
                pairs.append((place(i // 2, i % 2, c), place(g, c, r)))
    return pairs


def to_workers(block, shift):
    return lax.ppermute(block, PLACE, homes_of_workers(shift))


def to_homes(block, shift):
    return lax.ppermute(block, PLACE, [(w, h) for h, w in homes_of_workers(shift)])


def along_y(block, step):
    pairs = []
    for c in range(CORE):
        sign = 1 - 2 * c
        for y in range(Y):
            pairs.append((c * Y + y, c * Y + (y + sign * step) % Y))
    return lax.ppermute(block, ("core", "y"), pairs)


def to_sibling(block):
    return lax.ppermute(block, "core", [(0, 1), (1, 0)])


def exchanged(tiles):
    def across(block, step):
        pairs = []
        for c in range(CORE):
            sign = 1 - 2 * c
            for y in range(Y):
                pairs.append((c * Y + y, (1 - c) * Y + (y + sign * step) % Y))
        return lax.ppermute(block, ("core", "y"), pairs)

    beside, down, beside_down, up, beside_up, far, beside_far = tiles
    return [
        to_sibling(beside),
        along_y(up, 1),
        across(beside_down, 1),
        along_y(down, -1),
        across(beside_up, -1),
        along_y(far, 2),
        across(beside_far, 2),
    ]


def slab_of(q):
    core, y = lax.axis_index("core"), lax.axis_index("y")
    kind, sibling = q // 2, q % 2
    core = 1 - core if sibling else core
    sign = 1 - 2 * core
    y = lax.rem(y + sign * (0, -1, 1, 2)[kind] + 2 * Y, Y)
    return core * Y + y


def integrals_kernel(count, *refs):
    rows, pieces, refs = refs[:3], refs[3 : 3 + count], refs[3 + count :]
    direct_ref, tile_refs, total = refs[0], refs[1:-1], refs[-1]
    total[...] = jnp.zeros_like(total)

    @pl.loop(0, rows[0].shape[1] // STEP)
    def _(k):
        part = pl.ds(pl.multiple_of(k * STEP, STEP), STEP)
        left = jnp.concatenate([r[:, part] for r in rows], axis=0)
        right = jnp.concatenate([r[:, part] for r in pieces], axis=0)
        total[...] += lax.dot_general(left, right, (((1,), (1,)), ((), ())), preferred_element_type=F32)

    direct_ref[...] = total[...].astype(BF16)
    for at, tile_ref in enumerate(tile_refs, start=count - len(tile_refs)):
        for v in range(2):
            tile_ref[v] = total[(v + 1) * SLAB : (v + 2) * SLAB, at * SLAB : (at + 1) * SLAB].T.astype(BF16)


def in_vmem(count):
    return [pl.BlockSpec(memory_space=pltpu.VMEM)] * count


def integrals(rows, pieces, tiles):
    width = rows[0].shape[1]
    count = len(pieces)
    columns = count * SLAB
    return pl.pallas_call(
        functools.partial(integrals_kernel, count),
        in_specs=in_vmem(3 + count),
        out_specs=in_vmem(1 + tiles),
        out_shape=[jax.ShapeDtypeStruct((3 * SLAB, columns), BF16)]
        + [jax.ShapeDtypeStruct((2, SLAB, SLAB), BF16)] * tiles,
        scratch_shapes=[pltpu.VMEM((3 * SLAB, columns), F32)],
        cost_estimate=pl.CostEstimate(
            flops=2 * 3 * SLAB * columns * width,
            bytes_accessed=(3 + count) * SLAB * width * 2,
            transcendentals=0,
        ),
        compiler_params=pltpu.CompilerParams(vmem_limit_bytes=12 << 20),
        name="integrals",
    )(*rows, *pieces)


def density_kernel(visits, has_swapped, *refs):
    (e_occ, e_vir, early_ref, late_ref), refs = refs[:4], refs[4:]
    if has_swapped:
        swapped_refs, refs = (None, *refs[: N_SLABS - 1]), refs[N_SLABS - 1 :]
    pieces, refs = refs[:N_SLABS], refs[N_SLABS:]
    outs, amp = refs[: len(visits)], refs[len(visits)]
    group = lax.axis_index("z") * XH + lax.axis_index("xh")
    j = 2 * group + lax.axis_index("xl")
    e_a = jnp.broadcast_to(e_vir[slab_of(0)], (SLAB, SLAB)).T
    for n, v in enumerate(visits):
        pair = e_occ[lax.rem(j + v, 2 * GROUPS)] + e_occ[j]
        for q in range(N_SLABS):
            slab = slab_of(q)
            direct_ref, p = (early_ref, q) if q < EARLY else (late_ref, q - EARLY)
            d = direct_ref[v * SLAB : (v + 1) * SLAB, p * SLAB : (p + 1) * SLAB].astype(F32)
            if v == 0:
                s = d
            elif q == 0:
                s = d.T
            else:
                s = swapped_refs[q][v - 1].astype(F32)
            denom = pair - e_a - e_vir[slab]
            amp[n * SLAB : (n + 1) * SLAB, q * SLAB : (q + 1) * SLAB] = ((2.0 * d - s) / denom).astype(BF16)

    @pl.loop(0, pieces[0].shape[1] // STEP)
    def _(k):
        part = pl.ds(pl.multiple_of(k * STEP, STEP), STEP)
        right = jnp.concatenate([r[:, part] for r in pieces], axis=0)
        out = jnp.dot(amp[...], right, preferred_element_type=F32)
        for n in range(len(visits)):
            outs[n][:, part] = out[n * SLAB : (n + 1) * SLAB].astype(BF16)


def density(visits, e_occ, e_vir, direct, swapped, pieces):
    width = pieces[0].shape[1]
    rows = len(visits) * SLAB
    operands = [e_vir, *direct] + ([] if swapped is None else swapped) + pieces
    return pl.pallas_call(
        functools.partial(density_kernel, visits, swapped is not None),
        in_specs=[pl.BlockSpec(memory_space=pltpu.SMEM)] + in_vmem(len(operands)),
        out_specs=in_vmem(len(visits)),
        out_shape=[jax.ShapeDtypeStruct((SLAB, width), BF16)] * len(visits),
        scratch_shapes=[pltpu.VMEM((rows, N_SLABS * SLAB), BF16)],
        cost_estimate=pl.CostEstimate(
            flops=2 * rows * N_SLABS * SLAB * width,
            bytes_accessed=(len(visits) + N_SLABS) * SLAB * width * 2,
            transcendentals=0,
        ),
        compiler_params=pltpu.CompilerParams(vmem_limit_bytes=12 << 20),
        name="density",
    )(e_occ, *operands)


def on_device(factors, occ_energy, vir_energy, density_in):
    width = factors.shape[2]
    home = factors.reshape(SLAB, width)
    own = (to_workers(home, 0))
    next_1 = (to_workers(home, 1))
    next_2 = (to_workers(home, 2))
    one = (along_y(own, 1))
    other = (along_y(own, -1))
    two = (along_y(one, 1))
    mine = [own, one, other, two]
    pieces = []
    for piece in mine:
        pieces += [piece, (to_sibling(piece))]
    e_vir = vir_energy.reshape(N_SLABS, 1, SLAB)
    rows = [own, next_1, next_2]
    early, *tiles = integrals(rows, pieces[:EARLY], EARLY - 1)
    late, *last_tiles = integrals(rows, pieces[EARLY:], N_SLABS - EARLY)
    direct = (early, late)
    swapped = exchanged(tiles + last_tiles)
    (part_0,) = density((0,), occ_energy, e_vir, direct, None, pieces)
    part_1, part_2 = density((1, 2), occ_energy, e_vir, direct, swapped, pieces)
    total = density_in.reshape(SLAB, width)
    for shift, part in enumerate((part_0, part_1, part_2)):
        total = total + to_homes(part, shift).astype(F32)
    return total.reshape(density_in.shape)


def solution(mesh):
    fine = Mesh(mesh.devices.reshape(Z, XH, CORE, XL, Y), AXES)
    split = P(("z", "xh", "core"), ("xl", "y"), None)
    return jax.shard_map(
        on_device,
        mesh=fine,
        in_specs=(split, P(), P(), split),
        out_specs=split,
        check_vma=False,
    )
```

time: 136 us -> 119 us (0.88)
  the two profiles are of different devices: /device:TPU:10 before, /device:TPU:2 now
where the time goes in v2:
time: 119 us
  waiting for transfers between devices  77 us (65%)
  starting transfers between devices  28.7 us (24%)
  Pallas kernels  11.4 us (10%)
  other arithmetic  1.57 us (1%)
    ppermute x3, waiting for transfers between devices, to_homes(): lax.ppermute(block, PLACE, [(w, h) for h, w in homes_of_workers(shift)])  37.4 us
    ppermute x6, waiting for transfers between devices, along_y(): return lax.ppermute(block, ('core', 'y'), pairs)  20.5 us
    ppermute x3, waiting for transfers between devices, to_workers(): return lax.ppermute(block, PLACE, homes_of_workers(shift))  19.1 us
    ppermute x6, starting transfers between devices, along_y(): return lax.ppermute(block, ('core', 'y'), pairs)  10.5 us
    ppermute x3, starting transfers between devices, to_workers(): return lax.ppermute(block, PLACE, homes_of_workers(shift))  9.15 us
    ppermute x3, starting transfers between devices, to_homes(): lax.ppermute(block, PLACE, [(w, h) for h, w in homes_of_workers(shift)])  6.85 us
    pallas_call x2, Pallas kernels, density(): pl.pallas_call(functools.partial(density_kernel, visits, swapped is not N...  6.15 us
    pallas_call x2, Pallas kernels, integrals(): pl.pallas_call(functools.partial(integrals_kernel, count), in_specs=in_vm...  5.24 us
  transfers between devices with their start and end apart: 20, of which 7 were waited for; matrix products, arithmetic and copies ran while one was open for 0% of the time, Pallas kernels for 10%

profile of v2, /device:TPU:2, one launch (start us, length us, event | category | flops | bytes accessed | tf_op | source)
XLA Modules:
  0.0 118.8 jit_solution(11067363280223984327)
XLA Ops:
  0.0 1.9 %collective-permute-start = (bf16[128,3072]{1,0:T(8,128)(2,1)}, bf16[128,3072]{1,0:T(8,128)(2,1)S(1)}, u32[]{:S(2)}, u32[]{:S(2)}) collective-permute-start(bf16[128,3072]{1,0:T(8,128)(2,1)} %bitcast.14), channel_id=1, source_target_pairs={{0,0},{8,4},{4,8},{12,12},{16,16},{24,20},{20,24},{28,28},{32,32},... | collective-permute-start | bytes 2359304 | tf_op jit(solution)/shard_map/ppermute | solution.py:37
  1.9 11.6 %collective-permute-done.refs_0_.refs_3_.refs_4_.refs_11_ = bf16[128,3072]{1,0:T(8,128)(2,1)S(1)} collective-permute-done((bf16[128,3072]{1,0:T(8,128)(2,1)}, bf16[128,3072]{1,0:T(8,128)(2,1)S(1)}, u32[]{:S(2)}, u32[]{:S(2)}) %collective-permute-start) | collective-permute-done | bytes 786464 | tf_op jit(solution)/shard_map/ppermute | solution.py:37
  13.5 1.6 %collective-permute-start.4 = (bf16[128,3072]{1,0:T(8,128)(2,1)S(1)}, bf16[128,3072]{1,0:T(8,128)(2,1)S(1)}, u32[]{:S(2)}, u32[]{:S(2)}) collective-permute-start(bf16[128,3072]{1,0:T(8,128)(2,1)S(1)} %collective-permute-done.refs_0_.refs_3_.refs_4_.refs_11_), channel_id=1, source_target_pairs={{0,1},{1,2},{2,3},{3,0},{8,11},{9,8},{10,9},{11,10},{4,5},{5,6},{6... | collective-permute-start | bytes 2359304 | tf_op jit(solution)/shard_map/ppermute | solution.py:50
  15.1 0.0 collective-permute-start.1
  15.1 1.7 %collective-permute-start.6 = (bf16[128,3072]{1,0:T(8,128)(2,1)S(1)}, bf16[128,3072]{1,0:T(8,128)(2,1)S(1)}, u32[]{:S(2)}, u32[]{:S(2)}) collective-permute-start(bf16[128,3072]{1,0:T(8,128)(2,1)S(1)} %collective-permute-done.refs_0_.refs_3_.refs_4_.refs_11_), channel_id=1, source_target_pairs={{0,3},{1,0},{2,1},{3,2},{8,9},{9,10},{10,11},{11,8},{4,7},{5,4},{6... | collective-permute-start | bytes 2359304 | tf_op jit(solution)/shard_map/ppermute | solution.py:50
  16.7 16.1 %collective-permute-done.4.refs_5_.refs_6_.refs_13_ = bf16[128,3072]{1,0:T(8,128)(2,1)S(1)} collective-permute-done((bf16[128,3072]{1,0:T(8,128)(2,1)S(1)}, bf16[128,3072]{1,0:T(8,128)(2,1)S(1)}, u32[]{:S(2)}, u32[]{:S(2)}) %collective-permute-start.4) | collective-permute-done | bytes 786464 | tf_op jit(solution)/shard_map/ppermute | solution.py:50
  32.9 1.7 %collective-permute-start.8 = (bf16[128,3072]{1,0:T(8,128)(2,1)S(1)}, bf16[128,3072]{1,0:T(8,128)(2,1)S(1)}, u32[]{:S(2)}, u32[]{:S(2)}) collective-permute-start(bf16[128,3072]{1,0:T(8,128)(2,1)S(1)} %collective-permute-done.4.refs_5_.refs_6_.refs_13_), channel_id=1, source_target_pairs={{0,1},{1,2},{2,3},{3,0},{8,11},{9,8},{10,9},{11,10},{4,5},{5,6},{6... | collective-permute-start | bytes 2359304 | tf_op jit(solution)/shard_map/ppermute | solution.py:50
  34.6 7.2 %collective-permute-start.2 = (bf16[128,3072]{1,0:T(8,128)(2,1)}, bf16[128,3072]{1,0:T(8,128)(2,1)S(1)}, u32[]{:S(2)}, u32[]{:S(2)}) collective-permute-start(bf16[128,3072]{1,0:T(8,128)(2,1)} %bitcast.16), channel_id=1, source_target_pairs={{16,0},{24,4},{20,8},{28,12},{32,16},{40,20},{36,24},{44,28},{48,3... | collective-permute-start | bytes 2359304 | tf_op jit(solution)/shard_map/ppermute | solution.py:37
  41.9 0.0 collective-permute-start.3
  41.9 0.0 collective-permute-done.1.refs_1_
  41.9 0.5 collective-permute-start.5
  42.4 0.1 collective-permute-start.7
  42.5 4.3 %collective-permute-done.8.refs_3_.refs_10_.refs_17_ = bf16[128,3072]{1,0:T(8,128)(2,1)S(1)} collective-permute-done((bf16[128,3072]{1,0:T(8,128)(2,1)S(1)}, bf16[128,3072]{1,0:T(8,128)(2,1)S(1)}, u32[]{:S(2)}, u32[]{:S(2)}) %collective-permute-start.8) | collective-permute-done | bytes 786464 | tf_op jit(solution)/shard_map/ppermute | solution.py:50
  46.8 7.5 %collective-permute-done.2.refs_2_ = bf16[128,3072]{1,0:T(8,128)(2,1)S(1)} collective-permute-done((bf16[128,3072]{1,0:T(8,128)(2,1)}, bf16[128,3072]{1,0:T(8,128)(2,1)S(1)}, u32[]{:S(2)}, u32[]{:S(2)}) %collective-permute-start.2) | collective-permute-done | bytes 786464 | tf_op jit(solution)/shard_map/ppermute | solution.py:37
  54.4 3.3 %integrals.2 = (bf16[384,768]{1,0:T(8,128)(2,1)S(1)}, bf16[2,128,128]{2,1,0:T(8,128)(2,1)S(1)}, bf16[2,128,128]{2,1,0:T(8,128)(2,1)S(1)}, bf16[2,128,128]{2,1,0:...) custom-call(bf16[128,3072]{1,0:T(8,128)(2,1)S(1)} %collective-permute-done.refs_0_.refs_3_.refs_4_.ref, ...), custom_call_target="tpu_custom_call" | custom-call | flops 1811939328 | bytes 7077888 | tf_op jit(solution)/shard_map/integrals/pallas_call | solution.py:113
  57.7 0.1 collective-permute-start.11
  57.8 1.8 %collective-permute-start.12 = (bf16[2,128,128]{2,1,0:T(8,128)(2,1)S(1)}, bf16[2,128,128]{2,1,0:T(8,128)(2,1)S(1)}, u32[]{:S(2)}, u32[]{:S(2)}) collective-permute-start(bf16[2,128,128]{2,1,0:T(8,128)(2,1)S(1)} %get-tuple-element.19), channel_id=1, source_target_pairs={{0,1},{1,2},{2,3},{3,0},{8,11},{9,8},{10,9},{11,10},{4,5},{5,6},{6... | collective-permute-start | bytes 196616 | tf_op jit(solution)/shard_map/ppermute | solution.py:50
  59.6 0.0 collective-permute-start.13
  59.7 3.7 %collective-permute-start.14 = (bf16[2,128,128]{2,1,0:T(8,128)(2,1)S(1)}, bf16[2,128,128]{2,1,0:T(8,128)(2,1)S(1)}, u32[]{:S(2)}, u32[]{:S(2)}) collective-permute-start(bf16[2,128,128]{2,1,0:T(8,128)(2,1)S(1)} %get-tuple-element.21), channel_id=1, source_target_pairs={{0,3},{1,0},{2,1},{3,2},{8,9},{9,10},{10,11},{11,8},{4,7},{5,4},{6... | collective-permute-start | bytes 196616 | tf_op jit(solution)/shard_map/ppermute | solution.py:50
  63.3 0.5 collective-permute-start.15
  63.8 1.9 %integrals.3 = (bf16[384,256]{1,0:T(8,128)(2,1)S(1)}, bf16[2,128,128]{2,1,0:T(8,128)(2,1)S(1)}, bf16[2,128,128]{2,1,0:T(8,128)(2,1)S(1)}) custom-call(bf16[128,3072]{1,0:T(8,128)(2,1)S(1)} %collective-permute-done.refs_0_.refs_3_.refs_4_.refs_11_, bf16[128,3072]{1,0:T(8,128)(2,1)S(1)} %collective-permute-done.1.refs_1_, ...), custom_call_target="tpu_custom_call" | custom-call | flops 603979776 | bytes 3932160 | tf_op jit(solution)/shard_map/integrals/pallas_call | solution.py:113
  65.7 0.1 collective-permute-start.16
  65.8 0.9 collective-permute-start.17
  66.7 2.6 %density.2 = bf16[128,3072]{1,0:T(8,128)(2,1)S(1)} custom-call(f32[32]{0:T(128)S(1)} %copy-done.1, f32[8,1,128]{2,1,0:T(1,128)S(1)} %bitcast.12, bf16[384,768]{1,0:T(8,128)(2,1)S(1)} %get-tuple-element.16.refs_2_, bf16[384,256]{1,0:T(8,128)(2,1)S(1)} %get-tuple-element.17.refs_3_, ...), custom_call_target="tpu_custom_call" | custom-call | flops 805306368 | bytes 7077888 | tf_op jit(solution)/shard_map/density/pallas_call | solution.py:167
  69.4 0.0 copy-start.2
  69.4 5.3 %collective-permute-start.10 = (bf16[128,3072]{1,0:T(8,128)(2,1)S(1)}, bf16[128,3072]{1,0:T(8,128)(2,1)S(1)}, u32[]{:S(2)}, u32[]{:S(2)}) collective-permute-start(bf16[128,3072]{1,0:T(8,128)(2,1)S(1)} %density.2), channel_id=1, source_target_pairs={{0,0},{4,8},{8,4},{12,12},{16,16},{20,24},{24,20},{28,28},{32,32},... | collective-permute-start | bytes 2359304 | tf_op jit(solution)/shard_map/ppermute | solution.py:41
  74.7 3.5 %density.3 = (bf16[128,3072]{1,0:T(8,128)(2,1)S(1)}, bf16[128,3072]{1,0:T(8,128)(2,1)S(1)}) custom-call(f32[32]{0:T(128)S(1)} %copy-done.1, f32[8,1,128]{2,1,0:T(1,128)S(1)} %bitcast.13, bf16[384,768]{1,0:T(8,128)(2,1)S(1)} %get-tuple-element.16.refs_2_, bf16[384,256]{1,0:T(8,128)(2,1)S(1)} %get-tuple-element.17.refs_3_, ...), custom_call_target="tpu_custom_call" | custom-call | flops 1610612736 | bytes 7864320 | tf_op jit(solution)/shard_map/density/pallas_call | solution.py:167
  78.3 1.6 %collective-permute-start.19 = (bf16[128,3072]{1,0:T(8,128)(2,1)S(1)}, bf16[128,3072]{1,0:T(8,128)(2,1)S(1)}, u32[]{:S(2)}, u32[]{:S(2)}) collective-permute-start(bf16[128,3072]{1,0:T(8,128)(2,1)S(1)} %get-tuple-element.26), channel_id=1, source_target_pairs={{0,16},{4,24},{8,20},{12,28},{16,32},{20,40},{24,36},{28,44},{32,4... | collective-permute-start | bytes 2359304 | tf_op jit(solution)/shard_map/ppermute | solution.py:41
  79.8 8.1 %collective-permute-done.10 = bf16[128,3072]{1,0:T(8,128)(2,1)S(1)} collective-permute-done((bf16[128,3072]{1,0:T(8,128)(2,1)S(1)}, bf16[128,3072]{1,0:T(8,128)(2,1)S(1)}, u32[]{:S(2)}, u32[]{:S(2)}) %collective-permute-start.10) | collective-permute-done | bytes 786464 | tf_op jit(solution)/shard_map/ppermute | solution.py:41
  87.9 13.5 %collective-permute-done.19 = bf16[128,3072]{1,0:T(8,128)(2,1)S(1)} collective-permute-done((bf16[128,3072]{1,0:T(8,128)(2,1)S(1)}, bf16[128,3072]{1,0:T(8,128)(2,1)S(1)}, u32[]{:S(2)}, u32[]{:S(2)}) %collective-permute-start.19) | collective-permute-done | bytes 786464 | tf_op jit(solution)/shard_map/ppermute | solution.py:41
  101.4 15.9 %collective-permute-done.18 = bf16[128,3072]{1,0:T(8,128)(2,1)S(1)} collective-permute-done((bf16[128,3072]{1,0:T(8,128)(2,1)S(1)}, bf16[128,3072]{1,0:T(8,128)(2,1)S(1)}, u32[]{:S(2)}, u32[]{:S(2)}) %collective-permute-start.18) | collective-permute-done | bytes 786464 | tf_op jit(solution)/shard_map/ppermute | solution.py:41
  117.2 1.6 %fusion.2 = f32[1,128,3072]{2,1,0:T(8,128)} fusion(f32[1,128,3072]{2,1,0:T(8,128)S(1)} %copy-done.2, bf16[128,3072]{1,0:T(8,128)(2,1)S(1)} %collective-permute-done.19, bf16[128,3072]{1,0:T(8,128)(2,1)S(1)} %collective-permute-done.18, bf16[128,3072]{1,0:T(8,128)(2,1)S(1)} %collective-permute-done.10), kind=kLoop, calls=%fused_computation.3 | loop fusion | flops 2359296 | bytes 5505024 | tf_op jit(solution)/shard_map/reshape | solution.py:207
  (19 shorter events, 0.0 us)
Async XLA Ops:
  0.0 13.5 %collective-permute-start = (bf16[128,3072]{1,0:T(8,128)(2,1)}, bf16[128,3072]{1,0:T(8,128)(2,1)S(1)}, u32[]{:S(2)}, u32[]{:S(2)}) collective-permute-start(bf16[128,3072]{1,0:T(8,128)(2,1)} %bitcast.14), channel_id=1, source_target_pairs={{0,0},{8,4},{4,8},{12,12},{16,16},{24,20},{20,24},{28,28},{32,32},... | collective-permute-start | bytes 2359304 | tf_op jit(solution)/shard_map/ppermute | solution.py:37
  13.5 19.4 %collective-permute-start.4 = (bf16[128,3072]{1,0:T(8,128)(2,1)S(1)}, bf16[128,3072]{1,0:T(8,128)(2,1)S(1)}, u32[]{:S(2)}, u32[]{:S(2)}) collective-permute-start(bf16[128,3072]{1,0:T(8,128)(2,1)S(1)} %collective-permute-done.refs_0_.refs_3_.refs_4_.refs_11_), channel_id=1, source_target_pairs={{0,1},{1,2},{2,3},{3,0},{8,11},{9,8},{10,9},{11,10},{4,5},{5,6},{6... | collective-permute-start | bytes 2359304 | tf_op jit(solution)/shard_map/ppermute | solution.py:50
  15.1 26.8 %collective-permute-start.1 = (bf16[128,3072]{1,0:T(8,128)(2,1)}, bf16[128,3072]{1,0:T(8,128)(2,1)S(1)}, u32[]{:S(2)}, u32[]{:S(2)}) collective-permute-start(bf16[128,3072]{1,0:T(8,128)(2,1)} %bitcast.15), channel_id=1, source_target_pairs={{8,0},{16,4},{12,8},{20,12},{24,16},{32,20},{28,24},{36,28},{40,32... | collective-permute-start | bytes 2359304 | tf_op jit(solution)/shard_map/ppermute | solution.py:37
  15.1 27.3 %collective-permute-start.6 = (bf16[128,3072]{1,0:T(8,128)(2,1)S(1)}, bf16[128,3072]{1,0:T(8,128)(2,1)S(1)}, u32[]{:S(2)}, u32[]{:S(2)}) collective-permute-start(bf16[128,3072]{1,0:T(8,128)(2,1)S(1)} %collective-permute-done.refs_0_.refs_3_.refs_4_.refs_11_), channel_id=1, source_target_pairs={{0,3},{1,0},{2,1},{3,2},{8,9},{9,10},{10,11},{11,8},{4,7},{5,4},{6... | collective-permute-start | bytes 2359304 | tf_op jit(solution)/shard_map/ppermute | solution.py:50
  32.9 13.9 %collective-permute-start.8 = (bf16[128,3072]{1,0:T(8,128)(2,1)S(1)}, bf16[128,3072]{1,0:T(8,128)(2,1)S(1)}, u32[]{:S(2)}, u32[]{:S(2)}) collective-permute-start(bf16[128,3072]{1,0:T(8,128)(2,1)S(1)} %collective-permute-done.4.refs_5_.refs_6_.refs_13_), channel_id=1, source_target_pairs={{0,1},{1,2},{2,3},{3,0},{8,11},{9,8},{10,9},{11,10},{4,5},{5,6},{6... | collective-permute-start | bytes 2359304 | tf_op jit(solution)/shard_map/ppermute | solution.py:50
  34.6 19.7 %collective-permute-start.2 = (bf16[128,3072]{1,0:T(8,128)(2,1)}, bf16[128,3072]{1,0:T(8,128)(2,1)S(1)}, u32[]{:S(2)}, u32[]{:S(2)}) collective-permute-start(bf16[128,3072]{1,0:T(8,128)(2,1)} %bitcast.16), channel_id=1, source_target_pairs={{16,0},{24,4},{20,8},{28,12},{32,16},{40,20},{36,24},{44,28},{48,3... | collective-permute-start | bytes 2359304 | tf_op jit(solution)/shard_map/ppermute | solution.py:37
  41.9 12.5 %collective-permute-start.3 = (bf16[128,3072]{1,0:T(8,128)(2,1)S(1)}, bf16[128,3072]{1,0:T(8,128)(2,1)S(1)}, u32[]{:S(2)}, u32[]{:S(2)}) collective-permute-start(bf16[128,3072]{1,0:T(8,128)(2,1)S(1)} %collective-permute-done.refs_0_.refs_3_.refs_4_.refs_11_), channel_id=1, source_target_pairs={{0,8},{8,0},{1,9},{9,1},{2,10},{10,2},{3,11},{11,3},{4,12},{12,4},... | collective-permute-start | bytes 2359304 | tf_op jit(solution)/shard_map/ppermute | solution.py:54
  41.9 12.5 %collective-permute-start.5 = (bf16[128,3072]{1,0:T(8,128)(2,1)S(1)}, bf16[128,3072]{1,0:T(8,128)(2,1)S(1)}, u32[]{:S(2)}, u32[]{:S(2)}) collective-permute-start(bf16[128,3072]{1,0:T(8,128)(2,1)S(1)} %collective-permute-done.4.refs_5_.refs_6_.refs_13_), channel_id=1, source_target_pairs={{0,8},{8,0},{1,9},{9,1},{2,10},{10,2},{3,11},{11,3},{4,12},{12,4},... | collective-permute-start | bytes 2359304 | tf_op jit(solution)/shard_map/ppermute | solution.py:54
  42.4 12.0 %collective-permute-start.7 = (bf16[128,3072]{1,0:T(8,128)(2,1)S(1)}, bf16[128,3072]{1,0:T(8,128)(2,1)S(1)}, u32[]{:S(2)}, u32[]{:S(2)}) collective-permute-start(bf16[128,3072]{1,0:T(8,128)(2,1)S(1)} %collective-permute-done.6.refs_7_.refs_8_.refs_15_), channel_id=1, source_target_pairs={{0,8},{8,0},{1,9},{9,1},{2,10},{10,2},{3,11},{11,3},{4,12},{12,4},... | collective-permute-start | bytes 2359304 | tf_op jit(solution)/shard_map/ppermute | solution.py:54
  46.8 16.5 %collective-permute-start.9 = (bf16[128,3072]{1,0:T(8,128)(2,1)S(1)}, bf16[128,3072]{1,0:T(8,128)(2,1)S(1)}, u32[]{:S(2)}, u32[]{:S(2)}) collective-permute-start(bf16[128,3072]{1,0:T(8,128)(2,1)S(1)} %collective-permute-done.8.refs_3_.refs_10_.refs_17_), channel_id=1, source_target_pairs={{0,8},{8,0},{1,9},{9,1},{2,10},{10,2},{3,11},{11,3},{4,12},{12,4},... | collective-permute-start | bytes 2359304 | tf_op jit(solution)/shard_map/ppermute | solution.py:54
  57.7 8.0 %collective-permute-start.11 = (bf16[2,128,128]{2,1,0:T(8,128)(2,1)S(1)}, bf16[2,128,128]{2,1,0:T(8,128)(2,1)S(1)}, u32[]{:S(2)}, u32[]{:S(2)}) collective-permute-start(bf16[2,128,128]{2,1,0:T(8,128)(2,1)S(1)} %get-tuple-element.18), channel_id=1, source_target_pairs={{0,8},{8,0},{1,9},{9,1},{2,10},{10,2},{3,11},{11,3},{4,12},{12,4},... | collective-permute-start | bytes 196616 | tf_op jit(solution)/shard_map/ppermute | solution.py:54
  57.8 8.0 %collective-permute-start.12 = (bf16[2,128,128]{2,1,0:T(8,128)(2,1)S(1)}, bf16[2,128,128]{2,1,0:T(8,128)(2,1)S(1)}, u32[]{:S(2)}, u32[]{:S(2)}) collective-permute-start(bf16[2,128,128]{2,1,0:T(8,128)(2,1)S(1)} %get-tuple-element.19), channel_id=1, source_target_pairs={{0,1},{1,2},{2,3},{3,0},{8,11},{9,8},{10,9},{11,10},{4,5},{5,6},{6... | collective-permute-start | bytes 196616 | tf_op jit(solution)/shard_map/ppermute | solution.py:50
  59.6 9.8 %collective-permute-start.13 = (bf16[2,128,128]{2,1,0:T(8,128)(2,1)S(1)}, bf16[2,128,128]{2,1,0:T(8,128)(2,1)S(1)}, u32[]{:S(2)}, u32[]{:S(2)}) collective-permute-start(bf16[2,128,128]{2,1,0:T(8,128)(2,1)S(1)} %get-tuple-element.20), channel_id=1, source_target_pairs={{0,9},{1,10},{2,11},{3,8},{8,3},{9,0},{10,1},{11,2},{4,13},{5,14},... | collective-permute-start | bytes 196616 | tf_op jit(solution)/shard_map/ppermute | solution.py:64
  59.7 15.0 %collective-permute-start.14 = (bf16[2,128,128]{2,1,0:T(8,128)(2,1)S(1)}, bf16[2,128,128]{2,1,0:T(8,128)(2,1)S(1)}, u32[]{:S(2)}, u32[]{:S(2)}) collective-permute-start(bf16[2,128,128]{2,1,0:T(8,128)(2,1)S(1)} %get-tuple-element.21), channel_id=1, source_target_pairs={{0,3},{1,0},{2,1},{3,2},{8,9},{9,10},{10,11},{11,8},{4,7},{5,4},{6... | collective-permute-start | bytes 196616 | tf_op jit(solution)/shard_map/ppermute | solution.py:50
  63.3 3.4 %copy-start = (f32[1024]{0:T(1024)S(1)}, f32[1024]{0:T(1024)}, u32[]{:S(2)}) copy-start(f32[1024]{0:T(1024)} %param.6) | copy-start | bytes 12292
  63.3 3.4 %copy-start.1 = (f32[32]{0:T(128)S(1)}, f32[32]{0:T(128)}, u32[]{:S(2)}) copy-start(f32[32]{0:T(128)} %refs_0_.3) | copy-start | bytes 388
  63.3 11.4 %collective-permute-start.15 = (bf16[2,128,128]{2,1,0:T(8,128)(2,1)S(1)}, bf16[2,128,128]{2,1,0:T(8,128)(2,1)S(1)}, u32[]{:S(2)}, u32[]{:S(2)}) collective-permute-start(bf16[2,128,128]{2,1,0:T(8,128)(2,1)S(1)} %get-tuple-element.22), channel_id=1, source_target_pairs={{0,11},{1,8},{2,9},{3,10},{8,1},{9,2},{10,3},{11,0},{4,15},{5,12},... | collective-permute-start | bytes 196616 | tf_op jit(solution)/shard_map/ppermute | solution.py:64
  65.7 9.0 %collective-permute-start.16 = (bf16[2,128,128]{2,1,0:T(8,128)(2,1)S(1)}, bf16[2,128,128]{2,1,0:T(8,128)(2,1)S(1)}, u32[]{:S(2)}, u32[]{:S(2)}) collective-permute-start(bf16[2,128,128]{2,1,0:T(8,128)(2,1)S(1)} %get-tuple-element.23), channel_id=1, source_target_pairs={{0,2},{1,3},{2,0},{3,1},{8,10},{9,11},{10,8},{11,9},{4,6},{5,7},{6... | collective-permute-start | bytes 196616 | tf_op jit(solution)/shard_map/ppermute | solution.py:50
  65.8 8.9 %collective-permute-start.17 = (bf16[2,128,128]{2,1,0:T(8,128)(2,1)S(1)}, bf16[2,128,128]{2,1,0:T(8,128)(2,1)S(1)}, u32[]{:S(2)}, u32[]{:S(2)}) collective-permute-start(bf16[2,128,128]{2,1,0:T(8,128)(2,1)S(1)} %get-tuple-element.24), channel_id=1, source_target_pairs={{0,10},{1,11},{2,8},{3,9},{8,2},{9,3},{10,0},{11,1},{4,14},{5,15},... | collective-permute-start | bytes 196616 | tf_op jit(solution)/shard_map/ppermute | solution.py:64
  69.4 47.9 %copy-start.2 = (f32[1,128,3072]{2,1,0:T(8,128)S(1)}, f32[1,128,3072]{2,1,0:T(8,128)}, u32[]{:S(2)}) copy-start(f32[1,128,3072]{2,1,0:T(8,128)} %param.7) | copy-start | bytes 4718596
  69.4 18.5 %collective-permute-start.10 = (bf16[128,3072]{1,0:T(8,128)(2,1)S(1)}, bf16[128,3072]{1,0:T(8,128)(2,1)S(1)}, u32[]{:S(2)}, u32[]{:S(2)}) collective-permute-start(bf16[128,3072]{1,0:T(8,128)(2,1)S(1)} %density.2), channel_id=1, source_target_pairs={{0,0},{4,8},{8,4},{12,12},{16,16},{20,24},{24,20},{28,28},{32,32},... | collective-permute-start | bytes 2359304 | tf_op jit(solution)/shard_map/ppermute | solution.py:41
  78.3 23.1 %collective-permute-start.19 = (bf16[128,3072]{1,0:T(8,128)(2,1)S(1)}, bf16[128,3072]{1,0:T(8,128)(2,1)S(1)}, u32[]{:S(2)}, u32[]{:S(2)}) collective-permute-start(bf16[128,3072]{1,0:T(8,128)(2,1)S(1)} %get-tuple-element.26), channel_id=1, source_target_pairs={{0,16},{4,24},{8,20},{12,28},{16,32},{20,40},{24,36},{28,44},{32,4... | collective-permute-start | bytes 2359304 | tf_op jit(solution)/shard_map/ppermute | solution.py:41
  79.8 37.4 %collective-permute-start.18 = (bf16[128,3072]{1,0:T(8,128)(2,1)S(1)}, bf16[128,3072]{1,0:T(8,128)(2,1)S(1)}, u32[]{:S(2)}, u32[]{:S(2)}) collective-permute-start(bf16[128,3072]{1,0:T(8,128)(2,1)S(1)} %get-tuple-element.25), channel_id=1, source_target_pairs={{0,8},{4,16},{8,12},{12,20},{16,24},{20,32},{24,28},{28,36},{32,40... | collective-permute-start | bytes 2359304 | tf_op jit(solution)/shard_map/ppermute | solution.py:41

commit v3 on v2

v3 whole, which is shorter than its diff:
```python
import functools

import jax
import jax.numpy as jnp
from jax import lax
from jax.experimental import pallas as pl
from jax.experimental.pallas import tpu as pltpu
from jax.sharding import Mesh
from jax.sharding import PartitionSpec as P

Z, XH, CORE, XL, Y = 8, 2, 2, 2, 4
GROUPS = Z * XH
AXES = ("z", "xh", "core", "xl", "y")
SLAB = 128
N_SLABS = XL * Y
PIECES = ((0, 0), (0, -1), (0, 1), (0, 2), (1, 0), (1, -1), (1, 1), (1, 2))
BACK = (0, 2, 1, 3, 4, 6, 5, 7)
STEP = 512
EARLY = 7
TURNED = 4
BF16, F32 = jnp.bfloat16, jnp.float32


def two_blocks_on(block, step):
    pairs = []
    for g in range(GROUPS):
        for c in range(CORE):
            for x in range(XL):
                to = (g + step) % GROUPS * CORE + c
                pairs.append(((g * CORE + c) * XL + x, to * XL + 1 - x))
    return lax.ppermute(block, ("z", "xh", "core", "xl"), pairs)


def one_block_on(block, core):
    return lax.ppermute(block, ("core", "xl"), [(core * XL + x, (1 - core) * XL + (x if core else 1 - x)) for x in range(XL)])


def to_sibling(block):
    return lax.ppermute(block, "core", [(0, 1), (1, 0)])


def within(block, across, step):
    pairs = []
    for c in range(CORE):
        sign = 1 - 2 * c
        for x in range(XL):
            for y in range(Y):
                to = (x ^ across) * Y + (y + sign * step) % Y
                pairs.append((c * N_SLABS + x * Y + y, c * N_SLABS + to))
    return lax.ppermute(block, ("core", "xl", "y"), pairs)


def after(block, *done):
    return lax.optimization_barrier((block, *done))[0]


def gathered(home):
    cross = within(home, 1, 0)
    down = within(home, 0, 1)
    up = within(home, 0, -1)
    far = within(down, 0, 1)
    cross_up = within(up, 1, 0)
    cross_down = within(after(cross, down, up), 0, 1)
    cross_far = within(after(cross_down, far), 0, 1)
    return [home, down, up, far, cross, cross_down, cross_up, cross_far]


def exchanged(tiles):
    return {BACK[q]: within(tile, 1 - PIECES[q][0], PIECES[q][1]) for q, tile in tiles.items()}


def slab_of(q):
    across, step = PIECES[q]
    x, y = lax.axis_index("xl"), lax.axis_index("y")
    x = 1 - x if across else x
    return x * Y + lax.rem(y + step * (1 - 2 * lax.axis_index("core")) + Y, Y)


def in_vmem(count):
    return [pl.BlockSpec(memory_space=pltpu.VMEM)] * count


def integrals_kernel(count, sent, *refs):
    rows, pieces, refs = refs[:3], refs[3 : 3 + count], refs[3 + count :]
    direct_ref, tile_refs, total = refs[0], refs[1:-1], refs[-1]
    total[...] = jnp.zeros_like(total)

    @pl.loop(0, rows[0].shape[1] // STEP)
    def _(k):
        part = pl.ds(pl.multiple_of(k * STEP, STEP), STEP)
        left = jnp.concatenate([r[:, part] for r in rows], axis=0)
        right = jnp.concatenate([r[:, part] for r in pieces], axis=0)
        total[...] += lax.dot_general(left, right, (((1,), (1,)), ((), ())), preferred_element_type=F32)

    direct_ref[...] = total[...].astype(BF16)
    for at, tile_ref in zip(sent, tile_refs):
        for v in range(2):
            tile_ref[v] = total[(v + 1) * SLAB : (v + 2) * SLAB, at * SLAB : (at + 1) * SLAB].T.astype(BF16)


def integrals(rows, pieces, sent):
    width = rows[0].shape[1]
    count = len(pieces)
    columns = count * SLAB
    return pl.pallas_call(
        functools.partial(integrals_kernel, count, sent),
        in_specs=in_vmem(3 + count),
        out_specs=in_vmem(1 + len(sent)),
        out_shape=[jax.ShapeDtypeStruct((3 * SLAB, columns), BF16)]
        + [jax.ShapeDtypeStruct((2, SLAB, SLAB), BF16)] * len(sent),
        scratch_shapes=[pltpu.VMEM((3 * SLAB, columns), F32)],
        cost_estimate=pl.CostEstimate(
            flops=2 * 3 * SLAB * columns * width,
            bytes_accessed=(3 + count) * SLAB * width * 2,
            transcendentals=0,
        ),
        compiler_params=pltpu.CompilerParams(vmem_limit_bytes=8 << 20),
        name="integrals",
    )(*rows, *pieces)


def density_kernel(visit, e_occ, e_vir, early_ref, late_ref, *refs):
    swapped_refs, refs = (refs[: N_SLABS - 1], refs[N_SLABS - 1 :]) if visit else (None, refs)
    pieces, refs = refs[:N_SLABS], refs[N_SLABS:]
    before_ref = refs[0]
    out_ref, amp = refs[-2:]
    group, core = lax.axis_index("z") * XH + lax.axis_index("xh"), lax.axis_index("core")
    j = CORE * group + core
    pair = e_occ[lax.rem(j + visit, CORE * GROUPS)] + e_occ[j]
    e_a = jnp.broadcast_to(e_vir[slab_of(TURNED if visit else 0)], (SLAB, SLAB)).T
    for q in range(N_SLABS):
        direct_ref, p = (early_ref, q) if q < EARLY else (late_ref, q - EARLY)
        d = direct_ref[visit * SLAB : (visit + 1) * SLAB, p * SLAB : (p + 1) * SLAB].astype(F32)
        if visit == 0:
            s = d
        elif q == TURNED:
            s = d.T
        else:
            s = swapped_refs[q - (q > TURNED)][visit - 1].astype(F32)
        denom = pair - e_a - e_vir[slab_of(q)]
        amp[:, q * SLAB : (q + 1) * SLAB] = ((2.0 * d - s) / denom).astype(BF16)

    @pl.loop(0, pieces[0].shape[1] // STEP)
    def _(k):
        part = pl.ds(pl.multiple_of(k * STEP, STEP), STEP)
        right = jnp.concatenate([r[:, part] for r in pieces], axis=0)
        out = jnp.dot(amp[...], right, preferred_element_type=F32)
        if visit == 0:
            out = out + before_ref[:, part]
        out_ref[:, part] = out.astype(out_ref.dtype)


def density(visit, e_occ, e_vir, direct, swapped, pieces, before):
    width = pieces[0].shape[1]
    operands = [e_vir, *direct, *(swapped if visit else []), *pieces] + ([] if before is None else [before])
    return pl.pallas_call(
        functools.partial(density_kernel, visit),
        in_specs=[pl.BlockSpec(memory_space=pltpu.SMEM)] + in_vmem(len(operands)),
        out_specs=in_vmem(1)[0],
        out_shape=jax.ShapeDtypeStruct((SLAB, width), BF16 if visit else F32),
        scratch_shapes=[pltpu.VMEM((SLAB, N_SLABS * SLAB), BF16)],
        cost_estimate=pl.CostEstimate(
            flops=2 * SLAB * N_SLABS * SLAB * width,
            bytes_accessed=(1 + N_SLABS) * SLAB * width * 2,
            transcendentals=0,
        ),
        compiler_params=pltpu.CompilerParams(vmem_limit_bytes=8 << 20),
        name="density",
    )(e_occ, *operands)


def on_device(factors, occ_energy, vir_energy, density_in):
    width = factors.shape[2]
    core = lax.axis_index("core")
    home = factors.reshape(SLAB, width)
    e_vir = vir_energy.reshape(N_SLABS, 1, SLAB)
    pieces = gathered(home)
    next_2 = two_blocks_on(home, -1)
    next_1 = to_sibling(jnp.where(core == 0, next_2, pieces[TURNED]))
    rows = [home, next_1, next_2]
    sent = tuple(q for q in range(EARLY) if q != TURNED)
    early, *tiles = integrals(rows, pieces[:EARLY], sent)
    swapped = exchanged(dict(zip(sent, tiles)))
    last = [after(piece, early, *swapped.values()) for piece in pieces[EARLY:]]
    pieces = pieces[:EARLY] + last
    late, tile = integrals(rows, last, (0,))
    swapped |= exchanged({EARLY: tile})
    swapped = [swapped[q] for q in range(N_SLABS) if q != TURNED]
    given = (occ_energy, e_vir, (early, late), swapped, pieces)
    part_1 = density(1, *given, None)
    going = density(2, *given, None).astype(F32) + one_block_on(part_1, 1).astype(F32)
    back = two_blocks_on(going.astype(BF16), 1)
    total = density(0, *given, density_in.reshape(SLAB, width))
    total = total + one_block_on(part_1, 0).astype(F32) + back.astype(F32)
    return total.reshape(density_in.shape)


def solution(mesh):
    fine = Mesh(mesh.devices.reshape(Z, XH, CORE, XL, Y), AXES)
    split = P(("z", "xh", "core"), ("xl", "y"), None)
    return jax.shard_map(
        on_device,
        mesh=fine,
        in_specs=(split, P(), P(), split),
        out_specs=split,
        check_vma=False,
    )
```

time: 119 us -> 108 us (0.908)
  the two profiles are of different devices: /device:TPU:2 before, /device:TPU:1 now
where the time goes in v3:
time: 108 us; the launch traced here: 107 us
  waiting for transfers between devices  48.2 us (45%)
  starting transfers between devices  41.3 us (38%)
  Pallas kernels  15.8 us (15%)
  other arithmetic  1.65 us (2%)
    ppermute x14, waiting for transfers between devices, within(): return lax.ppermute(block, ('core', 'xl', 'y'), pairs)  27.7 us
    ppermute x14, starting transfers between devices, within(): return lax.ppermute(block, ('core', 'xl', 'y'), pairs)  19.7 us
    ppermute x2, waiting for transfers between devices, two_blocks_on(): return lax.ppermute(block, ('z', 'xh', 'core', 'xl'), pairs)  15.9 us
    ppermute x2, starting transfers between devices, one_block_on(): lax.ppermute(block, ('core', 'xl'), [(core * XL + x, (1 - core) * XL + (x...  9.28 us
    ppermute x2, starting transfers between devices, two_blocks_on(): return lax.ppermute(block, ('z', 'xh', 'core', 'xl'), pairs)  8.99 us
    pallas_call x2, Pallas kernels, integrals(): pl.pallas_call(functools.partial(integrals_kernel, count, sent), in_specs...  7.88 us
    pallas_call x3, Pallas kernels, density(): pl.pallas_call(functools.partial(density_kernel, visit), in_specs=[pl.Blo...  7.88 us
    ppermute x2, waiting for transfers between devices, one_block_on(): lax.ppermute(block, ('core', 'xl'), [(core * XL + x, (1 - core) * XL + (x...  4.64 us
  transfers between devices with their start and end apart: 19, of which 10 were waited for; matrix products, arithmetic and copies ran while one was open for 0% of the time, Pallas kernels for 10%

profile of v3, /device:TPU:1, one launch (start us, length us, event | category | flops | bytes accessed | tf_op | source)
XLA Modules:
  0.0 107.1 jit_solution(13896293047493336590)
XLA Ops:
  0.0 2.1 %collective-permute-start.4 = (bf16[128,3072]{1,0:T(8,128)(2,1)}, bf16[128,3072]{1,0:T(8,128)(2,1)S(1)}, u32[]{:S(2)}, u32[]{:S(2)}) collective-permute-start(bf16[128,3072]{1,0:T(8,128)(2,1)} %bitcast.5), channel_id=1, source_target_pairs={{0,3},{1,0},{2,1},{3,2},{4,7},{5,4},{6,5},{7,6},{8,9},{9,10},{10,1... | collective-permute-start | bytes 2359304 | tf_op jit(solution)/shard_map/ppermute | solution.py:50
  2.1 1.5 %collective-permute-start.3 = (bf16[128,3072]{1,0:T(8,128)(2,1)}, bf16[128,3072]{1,0:T(8,128)(2,1)S(1)}, u32[]{:S(2)}, u32[]{:S(2)}) collective-permute-start(bf16[128,3072]{1,0:T(8,128)(2,1)} %bitcast.6), channel_id=1, source_target_pairs={{0,1},{1,2},{2,3},{3,0},{4,5},{5,6},{6,7},{7,4},{8,11},{9,8},{10,9... | collective-permute-start | bytes 2359304 | tf_op jit(solution)/shard_map/ppermute | solution.py:50
  3.6 1.2 %collective-permute-start.1 = (bf16[128,3072]{1,0:T(8,128)(2,1)}, bf16[128,3072]{1,0:T(8,128)(2,1)S(1)}, u32[]{:S(2)}, u32[]{:S(2)}) collective-permute-start(bf16[128,3072]{1,0:T(8,128)(2,1)} %bitcast.7), channel_id=1, source_target_pairs={{0,4},{1,5},{2,6},{3,7},{4,0},{5,1},{6,2},{7,3},{8,12},{9,13},{10,... | collective-permute-start | bytes 2359304 | tf_op jit(solution)/shard_map/ppermute | solution.py:50
  4.9 7.1 %collective-permute-start = (bf16[128,3072]{1,0:T(8,128)(2,1)}, bf16[128,3072]{1,0:T(8,128)(2,1)}, u32[]{:S(2)}, u32[]{:S(2)}) collective-permute-start(bf16[128,3072]{1,0:T(8,128)(2,1)} %bitcast.8), channel_id=1, source_target_pairs={{0,244},{4,240},{8,252},{12,248},{16,4},{20,0},{24,12},{28,8},{32,... | collective-permute-start | bytes 2359304 | tf_op jit(solution)/shard_map/ppermute | solution.py:31
  12.0 6.0 %collective-permute-done.4.refs_5_.refs_2_.refs_9_ = bf16[128,3072]{1,0:T(8,128)(2,1)S(1)} collective-permute-done((bf16[128,3072]{1,0:T(8,128)(2,1)}, bf16[128,3072]{1,0:T(8,128)(2,1)S(1)}, u32[]{:S(2)}, u32[]{:S(2)}) %collective-permute-start.4) | collective-permute-done | bytes 786464 | tf_op jit(solution)/shard_map/ppermute | solution.py:50
  18.0 2.4 %collective-permute-done.3.refs_4_.refs_1_.refs_8_ = bf16[128,3072]{1,0:T(8,128)(2,1)S(1)} collective-permute-done((bf16[128,3072]{1,0:T(8,128)(2,1)}, bf16[128,3072]{1,0:T(8,128)(2,1)S(1)}, u32[]{:S(2)}, u32[]{:S(2)}) %collective-permute-start.3) | collective-permute-done | bytes 786464 | tf_op jit(solution)/shard_map/ppermute | solution.py:50
  20.4 1.0 collective-permute-done.1.refs_7_.refs_4_.refs_11_
  21.4 2.3 %collective-permute-start.6 = (bf16[128,3072]{1,0:T(8,128)(2,1)S(1)}, bf16[128,3072]{1,0:T(8,128)(2,1)S(1)}, u32[]{:S(2)}, u32[]{:S(2)}) collective-permute-start(bf16[128,3072]{1,0:T(8,128)(2,1)S(1)} %collective-permute-done.1.refs_7_.refs_4_.refs_11_), channel_id=1, source_target_pairs={{0,1},{1,2},{2,3},{3,0},{4,5},{5,6},{6,7},{7,4},{8,11},{9,8},{10,9... | collective-permute-start | bytes 2359304 | tf_op jit(solution)/shard_map/ppermute | solution.py:50
  23.7 1.1 %collective-permute-start.7 = (bf16[128,3072]{1,0:T(8,128)(2,1)S(1)}, bf16[128,3072]{1,0:T(8,128)(2,1)S(1)}, u32[]{:S(2)}, u32[]{:S(2)}) collective-permute-start(bf16[128,3072]{1,0:T(8,128)(2,1)S(1)} %collective-permute-done.4.refs_5_.refs_2_.refs_9_), channel_id=1, source_target_pairs={{0,4},{1,5},{2,6},{3,7},{4,0},{5,1},{6,2},{7,3},{8,12},{9,13},{10,... | collective-permute-start | bytes 2359304 | tf_op jit(solution)/shard_map/ppermute | solution.py:50
  24.8 1.2 %collective-permute-start.5 = (bf16[128,3072]{1,0:T(8,128)(2,1)S(1)}, bf16[128,3072]{1,0:T(8,128)(2,1)S(1)}, u32[]{:S(2)}, u32[]{:S(2)}) collective-permute-start(bf16[128,3072]{1,0:T(8,128)(2,1)S(1)} %collective-permute-done.3.refs_4_.refs_1_.refs_8_), channel_id=1, source_target_pairs={{0,1},{1,2},{2,3},{3,0},{4,5},{5,6},{6,7},{7,4},{8,11},{9,8},{10,9... | collective-permute-start | bytes 2359304 | tf_op jit(solution)/shard_map/ppermute | solution.py:50
  26.0 2.0 %collective-permute-done.refs_2_ = bf16[128,3072]{1,0:T(8,128)(2,1)} collective-permute-done((bf16[128,3072]{1,0:T(8,128)(2,1)}, bf16[128,3072]{1,0:T(8,128)(2,1)}, u32[]{:S(2)}, u32[]{:S(2)}) %collective-permute-start) | collective-permute-done | bytes 786464 | tf_op jit(solution)/shard_map/ppermute | solution.py:31
  28.0 3.3 %collective-permute-start.2 = (bf16[128,3072]{1,0:T(8,128)(2,1)S(1)}, bf16[128,3072]{1,0:T(8,128)(2,1)S(1)}, u32[]{:S(2)}, u32[]{:S(2)}) collective-permute-start(bf16[128,3072]{1,0:T(8,128)(2,1)S(1)} %broadcast_select_fusion), channel_id=1, source_target_pairs={{0,8},{8,0},{1,9},{9,1},{2,10},{10,2},{3,11},{11,3},{4,12},{12,4},... | collective-permute-start | bytes 2359304 | tf_op jit(solution)/shard_map/ppermute | solution.py:39
  31.3 9.9 %collective-permute-done.5.refs_6_.refs_3_.refs_10_ = bf16[128,3072]{1,0:T(8,128)(2,1)S(1)} collective-permute-done((bf16[128,3072]{1,0:T(8,128)(2,1)S(1)}, bf16[128,3072]{1,0:T(8,128)(2,1)S(1)}, u32[]{:S(2)}, u32[]{:S(2)}) %collective-permute-start.5) | collective-permute-done | bytes 786464 | tf_op jit(solution)/shard_map/ppermute | solution.py:50
  41.2 2.9 %collective-permute-start.8 = (bf16[128,3072]{1,0:T(8,128)(2,1)S(1)}, bf16[128,3072]{1,0:T(8,128)(2,1)S(1)}, u32[]{:S(2)}, u32[]{:S(2)}) collective-permute-start(bf16[128,3072]{1,0:T(8,128)(2,1)S(1)} %collective-permute-done.6.refs_8_.refs_5_.refs_12_), channel_id=1, source_target_pairs={{0,1},{1,2},{2,3},{3,0},{4,5},{5,6},{6,7},{7,4},{8,11},{9,8},{10,9... | collective-permute-start | bytes 2359304 | tf_op jit(solution)/shard_map/ppermute | solution.py:50
  44.2 5.0 %integrals.2 = (bf16[384,896]{1,0:T(8,128)(2,1)S(1)}, bf16[2,128,128]{2,1,0:T(8,128)(2,1)S(1)}, bf16[2,128,128]{2,1,0:T(8,128)(2,1)S(1)}, bf16[2,128,128]{2,1,0:...) custom-call(bf16[128,3072]{1,0:T(8,128)(2,1)S(1)} %bitcast.9, ...), custom_call_target="tpu_custom_call" | custom-call | flops 2113929216 | bytes 7864320 | tf_op jit(solution)/shard_map/integrals/pallas_call | solution.py:105
  49.2 1.2 %collective-permute-start.9 = (bf16[2,128,128]{2,1,0:T(8,128)(2,1)S(1)}, bf16[2,128,128]{2,1,0:T(8,128)(2,1)S(1)}, u32[]{:S(2)}, u32[]{:S(2)}) collective-permute-start(bf16[2,128,128]{2,1,0:T(8,128)(2,1)S(1)} %get-tuple-element.20), channel_id=1, source_target_pairs={{0,4},{1,5},{2,6},{3,7},{4,0},{5,1},{6,2},{7,3},{8,12},{9,13},{10,... | collective-permute-start | bytes 196616 | tf_op jit(solution)/shard_map/ppermute | solution.py:50
  50.4 3.6 %collective-permute-start.11 = (bf16[2,128,128]{2,1,0:T(8,128)(2,1)S(1)}, bf16[2,128,128]{2,1,0:T(8,128)(2,1)S(1)}, u32[]{:S(2)}, u32[]{:S(2)}) collective-permute-start(bf16[2,128,128]{2,1,0:T(8,128)(2,1)S(1)} %get-tuple-element.22), channel_id=1, source_target_pairs={{0,5},{1,6},{2,7},{3,4},{4,1},{5,2},{6,3},{7,0},{8,15},{9,12},{10,... | collective-permute-start | bytes 196616 | tf_op jit(solution)/shard_map/ppermute | solution.py:50
  54.6 1.2 %collective-permute-done.10.refs_2_ = bf16[2,128,128]{2,1,0:T(8,128)(2,1)S(1)} collective-permute-done((bf16[2,128,128]{2,1,0:T(8,128)(2,1)S(1)}, bf16[2,128,128]{2,1,0:T(8,128)(2,1)S(1)}, u32[]{:S(2)}, u32[]{:S(2)}) %collective-permute-start.10) | collective-permute-done | bytes 65568 | tf_op jit(solution)/shard_map/ppermute | solution.py:50
  55.7 0.9 collective-permute-start.14
  56.7 3.4 %collective-permute-done.12.refs_3_ = bf16[2,128,128]{2,1,0:T(8,128)(2,1)S(1)} collective-permute-done((bf16[2,128,128]{2,1,0:T(8,128)(2,1)S(1)}, bf16[2,128,128]{2,1,0:T(8,128)(2,1)S(1)}, u32[]{:S(2)}, u32[]{:S(2)}) %collective-permute-start.12) | collective-permute-done | bytes 65568 | tf_op jit(solution)/shard_map/ppermute | solution.py:50
  60.1 2.8 %integrals.3 = (bf16[384,128]{1,0:T(8,128)(2,1)S(1)}, bf16[2,128,128]{2,1,0:T(8,128)(2,1)S(1)}) custom-call(bf16[128,3072]{1,0:T(8,128)(2,1)S(1)} %bitcast.11, bf16[128,3072]{1,0:T(8,128)(2,1)S(1)} %collective-permute-done.2.refs_1_, bf16[128,3072]{1,0:T(8,128)(2,1)} %collective-permute-done.refs_2_, ...), custom_call_target="tpu_custom_call" | custom-call | flops 301989888 | bytes 3145728 | tf_op jit(solution)/shard_map/integrals/pallas_call | solution.py:105
  62.9 1.1 collective-permute-start.15
  64.0 3.8 %collective-permute-done.15.refs_6_ = bf16[2,128,128]{2,1,0:T(8,128)(2,1)S(1)} collective-permute-done((bf16[2,128,128]{2,1,0:T(8,128)(2,1)S(1)}, bf16[2,128,128]{2,1,0:T(8,128)(2,1)S(1)}, u32[]{:S(2)}, u32[]{:S(2)}) %collective-permute-start.15) | collective-permute-done | bytes 65568 | tf_op jit(solution)/shard_map/ppermute | solution.py:50
  67.8 2.6 %density.4 = bf16[128,3072]{1,0:T(8,128)(2,1)S(1)} custom-call(f32[32]{0:T(128)S(1)} %copy-done.3, f32[8,1,128]{2,1,0:T(1,128)S(1)} %bitcast.16, bf16[384,896]{1,0:T(8,128)(2,1)S(1)} %get-tuple-element.18.early_ref, bf16[384,128]{1,0:T(8,128)(2,1)S(1)} %get-tuple-element.27.late_ref, bf16[2,128,128]{2,1,0:T(8,128)(2,1)S(1)} %collective-permute-done.9.refs_0_, ...), custom_call_target="tpu_custom_call" | custom-call | flops 805306368 | bytes 7077888 | tf_op jit(solution)/shard_map/density/pallas_call | solution.py:156
  70.5 8.0 %collective-permute-start.17 = (bf16[128,3072]{1,0:T(8,128)(2,1)S(1)}, bf16[128,3072]{1,0:T(8,128)(2,1)S(1)}, u32[]{:S(2)}, u32[]{:S(2)}) collective-permute-start(bf16[128,3072]{1,0:T(8,128)(2,1)S(1)} %density.4), channel_id=1, source_target_pairs={{8,0},{12,4},{9,1},{13,5},{10,2},{14,6},{11,3},{15,7},{24,16},{28,... | collective-permute-start | bytes 2359304 | tf_op jit(solution)/shard_map/ppermute | solution.py:35
  78.5 1.3 %collective-permute-start.16 = (bf16[128,3072]{1,0:T(8,128)(2,1)S(1)}, bf16[128,3072]{1,0:T(8,128)(2,1)S(1)}, u32[]{:S(2)}, u32[]{:S(2)}) collective-permute-start(bf16[128,3072]{1,0:T(8,128)(2,1)S(1)} %density.4), channel_id=1, source_target_pairs={{0,12},{4,8},{1,13},{5,9},{2,14},{6,10},{3,15},{7,11},{16,28},{20,... | collective-permute-start | bytes 2359304 | tf_op jit(solution)/shard_map/ppermute | solution.py:35
  79.8 2.6 %density.5 = bf16[128,3072]{1,0:T(8,128)(2,1)S(1)} custom-call(f32[32]{0:T(128)S(1)} %copy-done.3, f32[8,1,128]{2,1,0:T(1,128)S(1)} %bitcast.17, bf16[384,896]{1,0:T(8,128)(2,1)S(1)} %get-tuple-element.18.early_ref, bf16[384,128]{1,0:T(8,128)(2,1)S(1)} %get-tuple-element.27.late_ref, bf16[2,128,128]{2,1,0:T(8,128)(2,1)S(1)} %collective-permute-done.9.refs_0_, ...), custom_call_target="tpu_custom_call" | custom-call | flops 805306368 | bytes 7077888 | tf_op jit(solution)/shard_map/density/pallas_call | solution.py:156
  82.6 1.9 %collective-permute-start.18 = (bf16[128,3072]{1,0:T(8,128)(2,1)S(1)}, bf16[128,3072]{1,0:T(8,128)(2,1)S(1)}, u32[]{:S(2)}, u32[]{:S(2)}) collective-permute-start(bf16[128,3072]{1,0:T(8,128)(2,1)S(1)} %add_convert_fusion), channel_id=1, source_target_pairs={{0,20},{4,16},{8,28},{12,24},{16,36},{20,32},{24,44},{28,40},{32,5... | collective-permute-start | bytes 2359304 | tf_op jit(solution)/shard_map/ppermute | solution.py:31
  84.5 2.6 %density.3 = f32[128,3072]{1,0:T(8,128)S(1)} custom-call(f32[32]{0:T(128)S(1)} %copy-done.3, f32[8,1,128]{2,1,0:T(1,128)S(1)} %bitcast.18, bf16[384,896]{1,0:T(8,128)(2,1)S(1)} %get-tuple-element.18.early_ref, bf16[384,128]{1,0:T(8,128)(2,1)S(1)} %get-tuple-element.27.late_ref, bf16[128,3072]{1,0:T(8,128)(2,1)S(1)} %bitcast.14, ...), custom_call_target="tpu_custom_call" | custom-call | flops 805306368 | bytes 7077888 | tf_op jit(solution)/shard_map/density/pallas_call | solution.py:156
  87.1 4.6 %collective-permute-done.16 = bf16[128,3072]{1,0:T(8,128)(2,1)S(1)} collective-permute-done((bf16[128,3072]{1,0:T(8,128)(2,1)S(1)}, bf16[128,3072]{1,0:T(8,128)(2,1)S(1)}, u32[]{:S(2)}, u32[]{:S(2)}) %collective-permute-start.16) | collective-permute-done | bytes 786464 | tf_op jit(solution)/shard_map/ppermute | solution.py:35
  91.8 13.9 %collective-permute-done.18 = bf16[128,3072]{1,0:T(8,128)(2,1)S(1)} collective-permute-done((bf16[128,3072]{1,0:T(8,128)(2,1)S(1)}, bf16[128,3072]{1,0:T(8,128)(2,1)S(1)}, u32[]{:S(2)}, u32[]{:S(2)}) %collective-permute-start.18) | collective-permute-done | bytes 786464 | tf_op jit(solution)/shard_map/ppermute | solution.py:31
  105.7 1.4 %add_bitcast_fusion = f32[1,128,3072]{2,1,0:T(8,128)} fusion(bf16[128,3072]{1,0:T(8,128)(2,1)S(1)} %collective-permute-done.18, f32[128,3072]{1,0:T(8,128)S(1)} %density.3, bf16[128,3072]{1,0:T(8,128)(2,1)S(1)} %collective-permute-done.16), kind=kLoop, calls=%fused_computation | loop fusion | flops 1572864 | bytes 4718592 | tf_op jit(solution)/shard_map/reshape | solution.py:195
  (22 shorter events, 0.9 us)
Async XLA Ops:
  0.0 44.2 %copy-start = (bf16[1,128,3072]{2,1,0:T(8,128)(2,1)S(1)}, bf16[1,128,3072]{2,1,0:T(8,128)(2,1)}, u32[]{:S(2)}) copy-start(bf16[1,128,3072]{2,1,0:T(8,128)(2,1)} %param.4) | copy-start | bytes 2359300
  0.0 18.0 %collective-permute-start.4 = (bf16[128,3072]{1,0:T(8,128)(2,1)}, bf16[128,3072]{1,0:T(8,128)(2,1)S(1)}, u32[]{:S(2)}, u32[]{:S(2)}) collective-permute-start(bf16[128,3072]{1,0:T(8,128)(2,1)} %bitcast.5), channel_id=1, source_target_pairs={{0,3},{1,0},{2,1},{3,2},{4,7},{5,4},{6,5},{7,6},{8,9},{9,10},{10,1... | collective-permute-start | bytes 2359304 | tf_op jit(solution)/shard_map/ppermute | solution.py:50
  2.1 18.2 %collective-permute-start.3 = (bf16[128,3072]{1,0:T(8,128)(2,1)}, bf16[128,3072]{1,0:T(8,128)(2,1)S(1)}, u32[]{:S(2)}, u32[]{:S(2)}) collective-permute-start(bf16[128,3072]{1,0:T(8,128)(2,1)} %bitcast.6), channel_id=1, source_target_pairs={{0,1},{1,2},{2,3},{3,0},{4,5},{5,6},{6,7},{7,4},{8,11},{9,8},{10,9... | collective-permute-start | bytes 2359304 | tf_op jit(solution)/shard_map/ppermute | solution.py:50
  3.6 17.7 %collective-permute-start.1 = (bf16[128,3072]{1,0:T(8,128)(2,1)}, bf16[128,3072]{1,0:T(8,128)(2,1)S(1)}, u32[]{:S(2)}, u32[]{:S(2)}) collective-permute-start(bf16[128,3072]{1,0:T(8,128)(2,1)} %bitcast.7), channel_id=1, source_target_pairs={{0,4},{1,5},{2,6},{3,7},{4,0},{5,1},{6,2},{7,3},{8,12},{9,13},{10,... | collective-permute-start | bytes 2359304 | tf_op jit(solution)/shard_map/ppermute | solution.py:50
  4.9 23.1 %collective-permute-start = (bf16[128,3072]{1,0:T(8,128)(2,1)}, bf16[128,3072]{1,0:T(8,128)(2,1)}, u32[]{:S(2)}, u32[]{:S(2)}) collective-permute-start(bf16[128,3072]{1,0:T(8,128)(2,1)} %bitcast.8), channel_id=1, source_target_pairs={{0,244},{4,240},{8,252},{12,248},{16,4},{20,0},{24,12},{28,8},{32,... | collective-permute-start | bytes 2359304 | tf_op jit(solution)/shard_map/ppermute | solution.py:31
  21.4 19.9 %collective-permute-start.6 = (bf16[128,3072]{1,0:T(8,128)(2,1)S(1)}, bf16[128,3072]{1,0:T(8,128)(2,1)S(1)}, u32[]{:S(2)}, u32[]{:S(2)}) collective-permute-start(bf16[128,3072]{1,0:T(8,128)(2,1)S(1)} %collective-permute-done.1.refs_7_.refs_4_.refs_11_), channel_id=1, source_target_pairs={{0,1},{1,2},{2,3},{3,0},{4,5},{5,6},{6,7},{7,4},{8,11},{9,8},{10,9... | collective-permute-start | bytes 2359304 | tf_op jit(solution)/shard_map/ppermute | solution.py:50
  23.7 20.5 %collective-permute-start.7 = (bf16[128,3072]{1,0:T(8,128)(2,1)S(1)}, bf16[128,3072]{1,0:T(8,128)(2,1)S(1)}, u32[]{:S(2)}, u32[]{:S(2)}) collective-permute-start(bf16[128,3072]{1,0:T(8,128)(2,1)S(1)} %collective-permute-done.4.refs_5_.refs_2_.refs_9_), channel_id=1, source_target_pairs={{0,4},{1,5},{2,6},{3,7},{4,0},{5,1},{6,2},{7,3},{8,12},{9,13},{10,... | collective-permute-start | bytes 2359304 | tf_op jit(solution)/shard_map/ppermute | solution.py:50
  24.8 16.5 %collective-permute-start.5 = (bf16[128,3072]{1,0:T(8,128)(2,1)S(1)}, bf16[128,3072]{1,0:T(8,128)(2,1)S(1)}, u32[]{:S(2)}, u32[]{:S(2)}) collective-permute-start(bf16[128,3072]{1,0:T(8,128)(2,1)S(1)} %collective-permute-done.3.refs_4_.refs_1_.refs_8_), channel_id=1, source_target_pairs={{0,1},{1,2},{2,3},{3,0},{4,5},{5,6},{6,7},{7,4},{8,11},{9,8},{10,9... | collective-permute-start | bytes 2359304 | tf_op jit(solution)/shard_map/ppermute | solution.py:50
  28.0 16.1 %collective-permute-start.2 = (bf16[128,3072]{1,0:T(8,128)(2,1)S(1)}, bf16[128,3072]{1,0:T(8,128)(2,1)S(1)}, u32[]{:S(2)}, u32[]{:S(2)}) collective-permute-start(bf16[128,3072]{1,0:T(8,128)(2,1)S(1)} %broadcast_select_fusion), channel_id=1, source_target_pairs={{0,8},{8,0},{1,9},{9,1},{2,10},{10,2},{3,11},{11,3},{4,12},{12,4},... | collective-permute-start | bytes 2359304 | tf_op jit(solution)/shard_map/ppermute | solution.py:39
  41.2 18.8 %collective-permute-start.8 = (bf16[128,3072]{1,0:T(8,128)(2,1)S(1)}, bf16[128,3072]{1,0:T(8,128)(2,1)S(1)}, u32[]{:S(2)}, u32[]{:S(2)}) collective-permute-start(bf16[128,3072]{1,0:T(8,128)(2,1)S(1)} %collective-permute-done.6.refs_8_.refs_5_.refs_12_), channel_id=1, source_target_pairs={{0,1},{1,2},{2,3},{3,0},{4,5},{5,6},{6,7},{7,4},{8,11},{9,8},{10,9... | collective-permute-start | bytes 2359304 | tf_op jit(solution)/shard_map/ppermute | solution.py:50
  49.2 4.8 %collective-permute-start.9 = (bf16[2,128,128]{2,1,0:T(8,128)(2,1)S(1)}, bf16[2,128,128]{2,1,0:T(8,128)(2,1)S(1)}, u32[]{:S(2)}, u32[]{:S(2)}) collective-permute-start(bf16[2,128,128]{2,1,0:T(8,128)(2,1)S(1)} %get-tuple-element.20), channel_id=1, source_target_pairs={{0,4},{1,5},{2,6},{3,7},{4,0},{5,1},{6,2},{7,3},{8,12},{9,13},{10,... | collective-permute-start | bytes 196616 | tf_op jit(solution)/shard_map/ppermute | solution.py:50
  50.4 5.3 %collective-permute-start.10 = (bf16[2,128,128]{2,1,0:T(8,128)(2,1)S(1)}, bf16[2,128,128]{2,1,0:T(8,128)(2,1)S(1)}, u32[]{:S(2)}, u32[]{:S(2)}) collective-permute-start(bf16[2,128,128]{2,1,0:T(8,128)(2,1)S(1)} %get-tuple-element.21), channel_id=1, source_target_pairs={{0,7},{1,4},{2,5},{3,6},{4,3},{5,0},{6,1},{7,2},{8,13},{9,14},{10,... | collective-permute-start | bytes 196616 | tf_op jit(solution)/shard_map/ppermute | solution.py:50
  50.4 6.3 %collective-permute-start.11 = (bf16[2,128,128]{2,1,0:T(8,128)(2,1)S(1)}, bf16[2,128,128]{2,1,0:T(8,128)(2,1)S(1)}, u32[]{:S(2)}, u32[]{:S(2)}) collective-permute-start(bf16[2,128,128]{2,1,0:T(8,128)(2,1)S(1)} %get-tuple-element.22), channel_id=1, source_target_pairs={{0,5},{1,6},{2,7},{3,4},{4,1},{5,2},{6,3},{7,0},{8,15},{9,12},{10,... | collective-permute-start | bytes 196616 | tf_op jit(solution)/shard_map/ppermute | solution.py:50
  54.0 6.1 %collective-permute-start.12 = (bf16[2,128,128]{2,1,0:T(8,128)(2,1)S(1)}, bf16[2,128,128]{2,1,0:T(8,128)(2,1)S(1)}, u32[]{:S(2)}, u32[]{:S(2)}) collective-permute-start(bf16[2,128,128]{2,1,0:T(8,128)(2,1)S(1)} %get-tuple-element.23), channel_id=1, source_target_pairs={{0,6},{1,7},{2,4},{3,5},{4,2},{5,3},{6,0},{7,1},{8,14},{9,15},{10,... | collective-permute-start | bytes 196616 | tf_op jit(solution)/shard_map/ppermute | solution.py:50
  54.0 6.1 %collective-permute-start.13 = (bf16[2,128,128]{2,1,0:T(8,128)(2,1)S(1)}, bf16[2,128,128]{2,1,0:T(8,128)(2,1)S(1)}, u32[]{:S(2)}, u32[]{:S(2)}) collective-permute-start(bf16[2,128,128]{2,1,0:T(8,128)(2,1)S(1)} %get-tuple-element.24), channel_id=1, source_target_pairs={{0,3},{1,0},{2,1},{3,2},{4,7},{5,4},{6,5},{7,6},{8,9},{9,10},{10,1... | collective-permute-start | bytes 196616 | tf_op jit(solution)/shard_map/ppermute | solution.py:50
  55.7 4.3 %collective-permute-start.14 = (bf16[2,128,128]{2,1,0:T(8,128)(2,1)S(1)}, bf16[2,128,128]{2,1,0:T(8,128)(2,1)S(1)}, u32[]{:S(2)}, u32[]{:S(2)}) collective-permute-start(bf16[2,128,128]{2,1,0:T(8,128)(2,1)S(1)} %get-tuple-element.25), channel_id=1, source_target_pairs={{0,1},{1,2},{2,3},{3,0},{4,5},{5,6},{6,7},{7,4},{8,11},{9,8},{10,9... | collective-permute-start | bytes 196616 | tf_op jit(solution)/shard_map/ppermute | solution.py:50
  60.1 7.8 %copy-start.2 = (f32[1024]{0:T(1024)S(1)}, f32[1024]{0:T(1024)}, u32[]{:S(2)}) copy-start(f32[1024]{0:T(1024)} %param.6) | copy-start | bytes 12292
  60.1 7.7 %copy-start.3 = (f32[32]{0:T(128)S(1)}, f32[32]{0:T(128)}, u32[]{:S(2)}) copy-start(f32[32]{0:T(128)} %e_occ.5) | copy-start | bytes 388
  62.9 4.9 %collective-permute-start.15 = (bf16[2,128,128]{2,1,0:T(8,128)(2,1)S(1)}, bf16[2,128,128]{2,1,0:T(8,128)(2,1)S(1)}, u32[]{:S(2)}, u32[]{:S(2)}) collective-permute-start(bf16[2,128,128]{2,1,0:T(8,128)(2,1)S(1)} %get-tuple-element.28), channel_id=1, source_target_pairs={{0,2},{1,3},{2,0},{3,1},{4,6},{5,7},{6,4},{7,5},{8,10},{9,11},{10,... | collective-permute-start | bytes 196616 | tf_op jit(solution)/shard_map/ppermute | solution.py:50
  70.5 12.0 %collective-permute-start.17 = (bf16[128,3072]{1,0:T(8,128)(2,1)S(1)}, bf16[128,3072]{1,0:T(8,128)(2,1)S(1)}, u32[]{:S(2)}, u32[]{:S(2)}) collective-permute-start(bf16[128,3072]{1,0:T(8,128)(2,1)S(1)} %density.4), channel_id=1, source_target_pairs={{8,0},{12,4},{9,1},{13,5},{10,2},{14,6},{11,3},{15,7},{24,16},{28,... | collective-permute-start | bytes 2359304 | tf_op jit(solution)/shard_map/ppermute | solution.py:35
  78.5 13.3 %collective-permute-start.16 = (bf16[128,3072]{1,0:T(8,128)(2,1)S(1)}, bf16[128,3072]{1,0:T(8,128)(2,1)S(1)}, u32[]{:S(2)}, u32[]{:S(2)}) collective-permute-start(bf16[128,3072]{1,0:T(8,128)(2,1)S(1)} %density.4), channel_id=1, source_target_pairs={{0,12},{4,8},{1,13},{5,9},{2,14},{6,10},{3,15},{7,11},{16,28},{20,... | collective-permute-start | bytes 2359304 | tf_op jit(solution)/shard_map/ppermute | solution.py:35
  82.4 2.1 %copy-start.1 = (f32[1,128,3072]{2,1,0:T(8,128)S(1)}, f32[1,128,3072]{2,1,0:T(8,128)}, u32[]{:S(2)}) copy-start(f32[1,128,3072]{2,1,0:T(8,128)} %param.7) | copy-start | bytes 4718596
  82.6 23.1 %collective-permute-start.18 = (bf16[128,3072]{1,0:T(8,128)(2,1)S(1)}, bf16[128,3072]{1,0:T(8,128)(2,1)S(1)}, u32[]{:S(2)}, u32[]{:S(2)}) collective-permute-start(bf16[128,3072]{1,0:T(8,128)(2,1)S(1)} %add_convert_fusion), channel_id=1, source_target_pairs={{0,20},{4,16},{8,28},{12,24},{16,36},{20,32},{24,44},{28,40},{32,5... | collective-permute-start | bytes 2359304 | tf_op jit(solution)/shard_map/ppermute | solution.py:31

commit v4 on v3

--- a/solution.py
+++ b/solution.py
@@ -15,6 +15,7 @@
 N_SLABS = XL * Y
 PIECES = ((0, 0), (0, -1), (0, 1), (0, 2), (1, 0), (1, -1), (1, 1), (1, 2))
 BACK = (0, 2, 1, 3, 4, 6, 5, 7)
+INNER = 1536
 STEP = 512
 EARLY = 7
 TURNED = 4
@@ -85,9 +86,9 @@
     direct_ref, tile_refs, total = refs[0], refs[1:-1], refs[-1]
     total[...] = jnp.zeros_like(total)
 
-    @pl.loop(0, rows[0].shape[1] // STEP)
+    @pl.loop(0, rows[0].shape[1] // INNER)
     def _(k):
-        part = pl.ds(pl.multiple_of(k * STEP, STEP), STEP)
+        part = pl.ds(pl.multiple_of(k * INNER, INNER), INNER)
         left = jnp.concatenate([r[:, part] for r in rows], axis=0)
         right = jnp.concatenate([r[:, part] for r in pieces], axis=0)
         total[...] += lax.dot_general(left, right, (((1,), (1,)), ((), ())), preferred_element_type=F32)
@@ -114,7 +115,7 @@
             bytes_accessed=(3 + count) * SLAB * width * 2,
             transcendentals=0,
         ),
-        compiler_params=pltpu.CompilerParams(vmem_limit_bytes=8 << 20),
+        compiler_params=pltpu.CompilerParams(vmem_limit_bytes=10 << 20),
         name="integrals",
     )(*rows, *pieces)
 
@@ -164,7 +165,7 @@
             bytes_accessed=(1 + N_SLABS) * SLAB * width * 2,
             transcendentals=0,
         ),
-        compiler_params=pltpu.CompilerParams(vmem_limit_bytes=8 << 20),
+        compiler_params=pltpu.CompilerParams(vmem_limit_bytes=10 << 20),
         name="density",
     )(e_occ, *operands)
 
@@ -181,7 +182,7 @@
     sent = tuple(q for q in range(EARLY) if q != TURNED)
     early, *tiles = integrals(rows, pieces[:EARLY], sent)
     swapped = exchanged(dict(zip(sent, tiles)))
-    last = [after(piece, early, *swapped.values()) for piece in pieces[EARLY:]]
+    last = [after(piece, early, *list(swapped.values())[:4]) for piece in pieces[EARLY:]]
     pieces = pieces[:EARLY] + last
     late, tile = integrals(rows, last, (0,))
     swapped |= exchanged({EARLY: tile})

time: 108 us -> 105 us (0.972)
  starting transfers between devices: 41.3 us -> 38.8 us
  Pallas kernels: 15.8 us -> 14.3 us
  waiting for transfers between devices: 48.2 us -> 49.7 us
    ppermute x2, starting transfers between devices: 9.28 us -> 6.89 us  [one_block_on(): lax.ppermute(block, ('core', 'xl'), [(core * XL + x, (1 - core) * XL + (x...]
    ppermute x2, waiting for transfers between devices: 15.9 us -> 17.4 us  [two_blocks_on(): return lax.ppermute(block, ('z', 'xh', 'core', 'xl'), pairs)]
    pallas_call x2, Pallas kernels: 7.88 us -> 6.45 us  [integrals(): pl.pallas_call(functools.partial(integrals_kernel, count, sent), in_specs...]
    ppermute x14, starting transfers between devices: 19.7 us -> 18.5 us  [within(): return lax.ppermute(block, ('core', 'xl', 'y'), pairs)]
  transfers between devices with their start and end apart: 19 -> 19, of which waited for: 10 -> 11; matrix products, arithmetic and copies ran while one was open for 0% -> 0% of each run, Pallas kernels for 10% -> 11%
where the time goes in v4:
time: 105 us
  waiting for transfers between devices  49.7 us (47%)
  starting transfers between devices  38.8 us (37%)
  Pallas kernels  14.3 us (14%)
  other arithmetic  1.65 us (2%)
    ppermute x14, waiting for transfers between devices, within(): return lax.ppermute(block, ('core', 'xl', 'y'), pairs)  28.7 us
    ppermute x14, starting transfers between devices, within(): return lax.ppermute(block, ('core', 'xl', 'y'), pairs)  18.5 us
    ppermute x2, waiting for transfers between devices, two_blocks_on(): return lax.ppermute(block, ('z', 'xh', 'core', 'xl'), pairs)  17.4 us
    ppermute x2, starting transfers between devices, two_blocks_on(): return lax.ppermute(block, ('z', 'xh', 'core', 'xl'), pairs)  10.1 us
    pallas_call x3, Pallas kernels, density(): pl.pallas_call(functools.partial(density_kernel, visit), in_specs=[pl.Blo...  7.88 us
    ppermute x2, starting transfers between devices, one_block_on(): lax.ppermute(block, ('core', 'xl'), [(core * XL + x, (1 - core) * XL + (x...  6.89 us
    pallas_call x2, Pallas kernels, integrals(): pl.pallas_call(functools.partial(integrals_kernel, count, sent), in_specs...  6.45 us
    ppermute x2, waiting for transfers between devices, one_block_on(): lax.ppermute(block, ('core', 'xl'), [(core * XL + x, (1 - core) * XL + (x...  3.58 us
  transfers between devices with their start and end apart: 19, of which 11 were waited for; matrix products, arithmetic and copies ran while one was open for 0% of the time, Pallas kernels for 11%

profile of v4, /device:TPU:1, one launch (start us, length us, event | category | flops | bytes accessed | tf_op | source)
XLA Modules:
  0.0 104.6 jit_solution(9494717610947090618)
XLA Ops:
  0.0 2.1 %collective-permute-start.4 = (bf16[128,3072]{1,0:T(8,128)(2,1)}, bf16[128,3072]{1,0:T(8,128)(2,1)S(1)}, u32[]{:S(2)}, u32[]{:S(2)}) collective-permute-start(bf16[128,3072]{1,0:T(8,128)(2,1)} %bitcast.5), channel_id=1, source_target_pairs={{0,3},{1,0},{2,1},{3,2},{4,7},{5,4},{6,5},{7,6},{8,9},{9,10},{10,1... | collective-permute-start | bytes 2359304 | tf_op jit(solution)/shard_map/ppermute | solution.py:51
  2.1 1.5 %collective-permute-start.3 = (bf16[128,3072]{1,0:T(8,128)(2,1)}, bf16[128,3072]{1,0:T(8,128)(2,1)S(1)}, u32[]{:S(2)}, u32[]{:S(2)}) collective-permute-start(bf16[128,3072]{1,0:T(8,128)(2,1)} %bitcast.6), channel_id=1, source_target_pairs={{0,1},{1,2},{2,3},{3,0},{4,5},{5,6},{6,7},{7,4},{8,11},{9,8},{10,9... | collective-permute-start | bytes 2359304 | tf_op jit(solution)/shard_map/ppermute | solution.py:51
  3.6 1.2 %collective-permute-start.1 = (bf16[128,3072]{1,0:T(8,128)(2,1)}, bf16[128,3072]{1,0:T(8,128)(2,1)S(1)}, u32[]{:S(2)}, u32[]{:S(2)}) collective-permute-start(bf16[128,3072]{1,0:T(8,128)(2,1)} %bitcast.7), channel_id=1, source_target_pairs={{0,4},{1,5},{2,6},{3,7},{4,0},{5,1},{6,2},{7,3},{8,12},{9,13},{10,... | collective-permute-start | bytes 2359304 | tf_op jit(solution)/shard_map/ppermute | solution.py:51
  4.9 7.1 %collective-permute-start = (bf16[128,3072]{1,0:T(8,128)(2,1)}, bf16[128,3072]{1,0:T(8,128)(2,1)}, u32[]{:S(2)}, u32[]{:S(2)}) collective-permute-start(bf16[128,3072]{1,0:T(8,128)(2,1)} %bitcast.8), channel_id=1, source_target_pairs={{0,244},{4,240},{8,252},{12,248},{16,4},{20,0},{24,12},{28,8},{32,... | collective-permute-start | bytes 2359304 | tf_op jit(solution)/shard_map/ppermute | solution.py:32
  12.0 6.0 %collective-permute-done.4.refs_5_.refs_2_.refs_9_ = bf16[128,3072]{1,0:T(8,128)(2,1)S(1)} collective-permute-done((bf16[128,3072]{1,0:T(8,128)(2,1)}, bf16[128,3072]{1,0:T(8,128)(2,1)S(1)}, u32[]{:S(2)}, u32[]{:S(2)}) %collective-permute-start.4) | collective-permute-done | bytes 786464 | tf_op jit(solution)/shard_map/ppermute | solution.py:51
  18.0 2.4 %collective-permute-done.3.refs_4_.refs_1_.refs_8_ = bf16[128,3072]{1,0:T(8,128)(2,1)S(1)} collective-permute-done((bf16[128,3072]{1,0:T(8,128)(2,1)}, bf16[128,3072]{1,0:T(8,128)(2,1)S(1)}, u32[]{:S(2)}, u32[]{:S(2)}) %collective-permute-start.3) | collective-permute-done | bytes 786464 | tf_op jit(solution)/shard_map/ppermute | solution.py:51
  20.4 1.0 collective-permute-done.1.refs_7_.refs_4_.refs_11_
  21.4 2.3 %collective-permute-start.6 = (bf16[128,3072]{1,0:T(8,128)(2,1)S(1)}, bf16[128,3072]{1,0:T(8,128)(2,1)S(1)}, u32[]{:S(2)}, u32[]{:S(2)}) collective-permute-start(bf16[128,3072]{1,0:T(8,128)(2,1)S(1)} %collective-permute-done.1.refs_7_.refs_4_.refs_11_), channel_id=1, source_target_pairs={{0,1},{1,2},{2,3},{3,0},{4,5},{5,6},{6,7},{7,4},{8,11},{9,8},{10,9... | collective-permute-start | bytes 2359304 | tf_op jit(solution)/shard_map/ppermute | solution.py:51
  23.7 1.1 %collective-permute-start.7 = (bf16[128,3072]{1,0:T(8,128)(2,1)S(1)}, bf16[128,3072]{1,0:T(8,128)(2,1)S(1)}, u32[]{:S(2)}, u32[]{:S(2)}) collective-permute-start(bf16[128,3072]{1,0:T(8,128)(2,1)S(1)} %collective-permute-done.4.refs_5_.refs_2_.refs_9_), channel_id=1, source_target_pairs={{0,4},{1,5},{2,6},{3,7},{4,0},{5,1},{6,2},{7,3},{8,12},{9,13},{10,... | collective-permute-start | bytes 2359304 | tf_op jit(solution)/shard_map/ppermute | solution.py:51
  24.8 1.2 %collective-permute-start.5 = (bf16[128,3072]{1,0:T(8,128)(2,1)S(1)}, bf16[128,3072]{1,0:T(8,128)(2,1)S(1)}, u32[]{:S(2)}, u32[]{:S(2)}) collective-permute-start(bf16[128,3072]{1,0:T(8,128)(2,1)S(1)} %collective-permute-done.3.refs_4_.refs_1_.refs_8_), channel_id=1, source_target_pairs={{0,1},{1,2},{2,3},{3,0},{4,5},{5,6},{6,7},{7,4},{8,11},{9,8},{10,9... | collective-permute-start | bytes 2359304 | tf_op jit(solution)/shard_map/ppermute | solution.py:51
  26.0 2.0 %collective-permute-done.refs_2_ = bf16[128,3072]{1,0:T(8,128)(2,1)} collective-permute-done((bf16[128,3072]{1,0:T(8,128)(2,1)}, bf16[128,3072]{1,0:T(8,128)(2,1)}, u32[]{:S(2)}, u32[]{:S(2)}) %collective-permute-start) | collective-permute-done | bytes 786464 | tf_op jit(solution)/shard_map/ppermute | solution.py:32
  28.0 3.3 %collective-permute-start.2 = (bf16[128,3072]{1,0:T(8,128)(2,1)S(1)}, bf16[128,3072]{1,0:T(8,128)(2,1)S(1)}, u32[]{:S(2)}, u32[]{:S(2)}) collective-permute-start(bf16[128,3072]{1,0:T(8,128)(2,1)S(1)} %broadcast_select_fusion), channel_id=1, source_target_pairs={{0,8},{8,0},{1,9},{9,1},{2,10},{10,2},{3,11},{11,3},{4,12},{12,4},... | collective-permute-start | bytes 2359304 | tf_op jit(solution)/shard_map/ppermute | solution.py:40
  31.3 9.9 %collective-permute-done.5.refs_6_.refs_3_.refs_10_ = bf16[128,3072]{1,0:T(8,128)(2,1)S(1)} collective-permute-done((bf16[128,3072]{1,0:T(8,128)(2,1)S(1)}, bf16[128,3072]{1,0:T(8,128)(2,1)S(1)}, u32[]{:S(2)}, u32[]{:S(2)}) %collective-permute-start.5) | collective-permute-done | bytes 786464 | tf_op jit(solution)/shard_map/ppermute | solution.py:51
  41.2 2.9 %collective-permute-start.8 = (bf16[128,3072]{1,0:T(8,128)(2,1)S(1)}, bf16[128,3072]{1,0:T(8,128)(2,1)S(1)}, u32[]{:S(2)}, u32[]{:S(2)}) collective-permute-start(bf16[128,3072]{1,0:T(8,128)(2,1)S(1)} %collective-permute-done.6.refs_8_.refs_5_.refs_12_), channel_id=1, source_target_pairs={{0,1},{1,2},{2,3},{3,0},{4,5},{5,6},{6,7},{7,4},{8,11},{9,8},{10,9... | collective-permute-start | bytes 2359304 | tf_op jit(solution)/shard_map/ppermute | solution.py:51
  44.2 4.2 %integrals.2 = (bf16[384,896]{1,0:T(8,128)(2,1)S(1)}, bf16[2,128,128]{2,1,0:T(8,128)(2,1)S(1)}, bf16[2,128,128]{2,1,0:T(8,128)(2,1)S(1)}, bf16[2,128,128]{2,1,0:...) custom-call(bf16[128,3072]{1,0:T(8,128)(2,1)S(1)} %bitcast.9, ...), custom_call_target="tpu_custom_call" | custom-call | flops 2113929216 | bytes 7864320 | tf_op jit(solution)/shard_map/integrals/pallas_call | solution.py:106
  48.4 1.2 %collective-permute-start.9 = (bf16[2,128,128]{2,1,0:T(8,128)(2,1)S(1)}, bf16[2,128,128]{2,1,0:T(8,128)(2,1)S(1)}, u32[]{:S(2)}, u32[]{:S(2)}) collective-permute-start(bf16[2,128,128]{2,1,0:T(8,128)(2,1)S(1)} %get-tuple-element.20), channel_id=1, source_target_pairs={{0,4},{1,5},{2,6},{3,7},{4,0},{5,1},{6,2},{7,3},{8,12},{9,13},{10,... | collective-permute-start | bytes 196616 | tf_op jit(solution)/shard_map/ppermute | solution.py:51
  49.6 3.6 %collective-permute-start.11 = (bf16[2,128,128]{2,1,0:T(8,128)(2,1)S(1)}, bf16[2,128,128]{2,1,0:T(8,128)(2,1)S(1)}, u32[]{:S(2)}, u32[]{:S(2)}) collective-permute-start(bf16[2,128,128]{2,1,0:T(8,128)(2,1)S(1)} %get-tuple-element.22), channel_id=1, source_target_pairs={{0,5},{1,6},{2,7},{3,4},{4,1},{5,2},{6,3},{7,0},{8,15},{9,12},{10,... | collective-permute-start | bytes 196616 | tf_op jit(solution)/shard_map/ppermute | solution.py:51
  53.2 1.2 %collective-permute-start.13 = (bf16[2,128,128]{2,1,0:T(8,128)(2,1)S(1)}, bf16[2,128,128]{2,1,0:T(8,128)(2,1)S(1)}, u32[]{:S(2)}, u32[]{:S(2)}) collective-permute-start(bf16[2,128,128]{2,1,0:T(8,128)(2,1)S(1)} %get-tuple-element.26), channel_id=1, source_target_pairs={{0,1},{1,2},{2,3},{3,0},{4,5},{5,6},{6,7},{7,4},{8,11},{9,8},{10,9... | collective-permute-start | bytes 196616 | tf_op jit(solution)/shard_map/ppermute | solution.py:51
  54.4 0.6 collective-permute-done.10.refs_2_
  54.9 4.3 %collective-permute-done.12.refs_3_ = bf16[2,128,128]{2,1,0:T(8,128)(2,1)S(1)} collective-permute-done((bf16[2,128,128]{2,1,0:T(8,128)(2,1)S(1)}, bf16[2,128,128]{2,1,0:T(8,128)(2,1)S(1)}, u32[]{:S(2)}, u32[]{:S(2)}) %collective-permute-start.12) | collective-permute-done | bytes 65568 | tf_op jit(solution)/shard_map/ppermute | solution.py:51
  59.3 2.2 %integrals.3 = (bf16[384,128]{1,0:T(8,128)(2,1)S(1)}, bf16[2,128,128]{2,1,0:T(8,128)(2,1)S(1)}) custom-call(bf16[128,3072]{1,0:T(8,128)(2,1)S(1)} %bitcast.11, bf16[128,3072]{1,0:T(8,128)(2,1)S(1)} %collective-permute-done.2.refs_1_, bf16[128,3072]{1,0:T(8,128)(2,1)} %collective-permute-done.refs_2_, ...), custom_call_target="tpu_custom_call" | custom-call | flops 301989888 | bytes 3145728 | tf_op jit(solution)/shard_map/integrals/pallas_call | solution.py:106
  61.7 0.5 collective-permute-done.14.refs_5_
  62.1 4.1 %collective-permute-done.15.refs_6_ = bf16[2,128,128]{2,1,0:T(8,128)(2,1)S(1)} collective-permute-done((bf16[2,128,128]{2,1,0:T(8,128)(2,1)S(1)}, bf16[2,128,128]{2,1,0:T(8,128)(2,1)S(1)}, u32[]{:S(2)}, u32[]{:S(2)}) %collective-permute-start.15) | collective-permute-done | bytes 65568 | tf_op jit(solution)/shard_map/ppermute | solution.py:51
  66.2 2.6 %density.4 = bf16[128,3072]{1,0:T(8,128)(2,1)S(1)} custom-call(f32[32]{0:T(128)S(1)} %copy-done.3, f32[8,1,128]{2,1,0:T(1,128)S(1)} %bitcast.16, bf16[384,896]{1,0:T(8,128)(2,1)S(1)} %get-tuple-element.18.early_ref, bf16[384,128]{1,0:T(8,128)(2,1)S(1)} %get-tuple-element.25.late_ref, bf16[2,128,128]{2,1,0:T(8,128)(2,1)S(1)} %collective-permute-done.9.refs_0_, ...), custom_call_target="tpu_custom_call" | custom-call | flops 805306368 | bytes 7077888 | tf_op jit(solution)/shard_map/density/pallas_call | solution.py:157
  68.8 5.6 %collective-permute-start.17 = (bf16[128,3072]{1,0:T(8,128)(2,1)S(1)}, bf16[128,3072]{1,0:T(8,128)(2,1)S(1)}, u32[]{:S(2)}, u32[]{:S(2)}) collective-permute-start(bf16[128,3072]{1,0:T(8,128)(2,1)S(1)} %density.4), channel_id=1, source_target_pairs={{8,0},{12,4},{9,1},{13,5},{10,2},{14,6},{11,3},{15,7},{24,16},{28,... | collective-permute-start | bytes 2359304 | tf_op jit(solution)/shard_map/ppermute | solution.py:36
  74.4 1.3 %collective-permute-start.16 = (bf16[128,3072]{1,0:T(8,128)(2,1)S(1)}, bf16[128,3072]{1,0:T(8,128)(2,1)S(1)}, u32[]{:S(2)}, u32[]{:S(2)}) collective-permute-start(bf16[128,3072]{1,0:T(8,128)(2,1)S(1)} %density.4), channel_id=1, source_target_pairs={{0,12},{4,8},{1,13},{5,9},{2,14},{6,10},{3,15},{7,11},{16,28},{20,... | collective-permute-start | bytes 2359304 | tf_op jit(solution)/shard_map/ppermute | solution.py:36
  75.7 2.6 %density.5 = bf16[128,3072]{1,0:T(8,128)(2,1)S(1)} custom-call(f32[32]{0:T(128)S(1)} %copy-done.3, f32[8,1,128]{2,1,0:T(1,128)S(1)} %bitcast.17, bf16[384,896]{1,0:T(8,128)(2,1)S(1)} %get-tuple-element.18.early_ref, bf16[384,128]{1,0:T(8,128)(2,1)S(1)} %get-tuple-element.25.late_ref, bf16[2,128,128]{2,1,0:T(8,128)(2,1)S(1)} %collective-permute-done.9.refs_0_, ...), custom_call_target="tpu_custom_call" | custom-call | flops 805306368 | bytes 7077888 | tf_op jit(solution)/shard_map/density/pallas_call | solution.py:157
  78.6 2.9 %collective-permute-start.18 = (bf16[128,3072]{1,0:T(8,128)(2,1)S(1)}, bf16[128,3072]{1,0:T(8,128)(2,1)S(1)}, u32[]{:S(2)}, u32[]{:S(2)}) collective-permute-start(bf16[128,3072]{1,0:T(8,128)(2,1)S(1)} %add_convert_fusion), channel_id=1, source_target_pairs={{0,20},{4,16},{8,28},{12,24},{16,36},{20,32},{24,44},{28,40},{32,5... | collective-permute-start | bytes 2359304 | tf_op jit(solution)/shard_map/ppermute | solution.py:32
  81.6 2.6 %density.3 = f32[128,3072]{1,0:T(8,128)S(1)} custom-call(f32[32]{0:T(128)S(1)} %copy-done.3, f32[8,1,128]{2,1,0:T(1,128)S(1)} %bitcast.18, bf16[384,896]{1,0:T(8,128)(2,1)S(1)} %get-tuple-element.18.early_ref, bf16[384,128]{1,0:T(8,128)(2,1)S(1)} %get-tuple-element.25.late_ref, bf16[128,3072]{1,0:T(8,128)(2,1)S(1)} %bitcast.14, ...), custom_call_target="tpu_custom_call" | custom-call | flops 805306368 | bytes 7077888 | tf_op jit(solution)/shard_map/density/pallas_call | solution.py:157
  84.2 3.6 %collective-permute-done.16 = bf16[128,3072]{1,0:T(8,128)(2,1)S(1)} collective-permute-done((bf16[128,3072]{1,0:T(8,128)(2,1)S(1)}, bf16[128,3072]{1,0:T(8,128)(2,1)S(1)}, u32[]{:S(2)}, u32[]{:S(2)}) %collective-permute-start.16) | collective-permute-done | bytes 786464 | tf_op jit(solution)/shard_map/ppermute | solution.py:36
  87.8 15.5 %collective-permute-done.18 = bf16[128,3072]{1,0:T(8,128)(2,1)S(1)} collective-permute-done((bf16[128,3072]{1,0:T(8,128)(2,1)S(1)}, bf16[128,3072]{1,0:T(8,128)(2,1)S(1)}, u32[]{:S(2)}, u32[]{:S(2)}) %collective-permute-start.18) | collective-permute-done | bytes 786464 | tf_op jit(solution)/shard_map/ppermute | solution.py:32
  103.2 1.4 %add_bitcast_fusion = f32[1,128,3072]{2,1,0:T(8,128)} fusion(bf16[128,3072]{1,0:T(8,128)(2,1)S(1)} %collective-permute-done.18, f32[128,3072]{1,0:T(8,128)S(1)} %density.3, bf16[128,3072]{1,0:T(8,128)(2,1)S(1)} %collective-permute-done.16), kind=kLoop, calls=%fused_computation | loop fusion | flops 1572864 | bytes 4718592 | tf_op jit(solution)/shard_map/reshape | solution.py:196
  (22 shorter events, 0.5 us)
Async XLA Ops:
  0.0 44.2 %copy-start = (bf16[1,128,3072]{2,1,0:T(8,128)(2,1)S(1)}, bf16[1,128,3072]{2,1,0:T(8,128)(2,1)}, u32[]{:S(2)}) copy-start(bf16[1,128,3072]{2,1,0:T(8,128)(2,1)} %param.4) | copy-start | bytes 2359300
  0.0 18.0 %collective-permute-start.4 = (bf16[128,3072]{1,0:T(8,128)(2,1)}, bf16[128,3072]{1,0:T(8,128)(2,1)S(1)}, u32[]{:S(2)}, u32[]{:S(2)}) collective-permute-start(bf16[128,3072]{1,0:T(8,128)(2,1)} %bitcast.5), channel_id=1, source_target_pairs={{0,3},{1,0},{2,1},{3,2},{4,7},{5,4},{6,5},{7,6},{8,9},{9,10},{10,1... | collective-permute-start | bytes 2359304 | tf_op jit(solution)/shard_map/ppermute | solution.py:51
  2.1 18.2 %collective-permute-start.3 = (bf16[128,3072]{1,0:T(8,128)(2,1)}, bf16[128,3072]{1,0:T(8,128)(2,1)S(1)}, u32[]{:S(2)}, u32[]{:S(2)}) collective-permute-start(bf16[128,3072]{1,0:T(8,128)(2,1)} %bitcast.6), channel_id=1, source_target_pairs={{0,1},{1,2},{2,3},{3,0},{4,5},{5,6},{6,7},{7,4},{8,11},{9,8},{10,9... | collective-permute-start | bytes 2359304 | tf_op jit(solution)/shard_map/ppermute | solution.py:51
  3.6 17.7 %collective-permute-start.1 = (bf16[128,3072]{1,0:T(8,128)(2,1)}, bf16[128,3072]{1,0:T(8,128)(2,1)S(1)}, u32[]{:S(2)}, u32[]{:S(2)}) collective-permute-start(bf16[128,3072]{1,0:T(8,128)(2,1)} %bitcast.7), channel_id=1, source_target_pairs={{0,4},{1,5},{2,6},{3,7},{4,0},{5,1},{6,2},{7,3},{8,12},{9,13},{10,... | collective-permute-start | bytes 2359304 | tf_op jit(solution)/shard_map/ppermute | solution.py:51
  4.9 23.1 %collective-permute-start = (bf16[128,3072]{1,0:T(8,128)(2,1)}, bf16[128,3072]{1,0:T(8,128)(2,1)}, u32[]{:S(2)}, u32[]{:S(2)}) collective-permute-start(bf16[128,3072]{1,0:T(8,128)(2,1)} %bitcast.8), channel_id=1, source_target_pairs={{0,244},{4,240},{8,252},{12,248},{16,4},{20,0},{24,12},{28,8},{32,... | collective-permute-start | bytes 2359304 | tf_op jit(solution)/shard_map/ppermute | solution.py:32
  21.4 19.9 %collective-permute-start.6 = (bf16[128,3072]{1,0:T(8,128)(2,1)S(1)}, bf16[128,3072]{1,0:T(8,128)(2,1)S(1)}, u32[]{:S(2)}, u32[]{:S(2)}) collective-permute-start(bf16[128,3072]{1,0:T(8,128)(2,1)S(1)} %collective-permute-done.1.refs_7_.refs_4_.refs_11_), channel_id=1, source_target_pairs={{0,1},{1,2},{2,3},{3,0},{4,5},{5,6},{6,7},{7,4},{8,11},{9,8},{10,9... | collective-permute-start | bytes 2359304 | tf_op jit(solution)/shard_map/ppermute | solution.py:51
  23.7 20.5 %collective-permute-start.7 = (bf16[128,3072]{1,0:T(8,128)(2,1)S(1)}, bf16[128,3072]{1,0:T(8,128)(2,1)S(1)}, u32[]{:S(2)}, u32[]{:S(2)}) collective-permute-start(bf16[128,3072]{1,0:T(8,128)(2,1)S(1)} %collective-permute-done.4.refs_5_.refs_2_.refs_9_), channel_id=1, source_target_pairs={{0,4},{1,5},{2,6},{3,7},{4,0},{5,1},{6,2},{7,3},{8,12},{9,13},{10,... | collective-permute-start | bytes 2359304 | tf_op jit(solution)/shard_map/ppermute | solution.py:51
  24.8 16.5 %collective-permute-start.5 = (bf16[128,3072]{1,0:T(8,128)(2,1)S(1)}, bf16[128,3072]{1,0:T(8,128)(2,1)S(1)}, u32[]{:S(2)}, u32[]{:S(2)}) collective-permute-start(bf16[128,3072]{1,0:T(8,128)(2,1)S(1)} %collective-permute-done.3.refs_4_.refs_1_.refs_8_), channel_id=1, source_target_pairs={{0,1},{1,2},{2,3},{3,0},{4,5},{5,6},{6,7},{7,4},{8,11},{9,8},{10,9... | collective-permute-start | bytes 2359304 | tf_op jit(solution)/shard_map/ppermute | solution.py:51
  28.0 16.1 %collective-permute-start.2 = (bf16[128,3072]{1,0:T(8,128)(2,1)S(1)}, bf16[128,3072]{1,0:T(8,128)(2,1)S(1)}, u32[]{:S(2)}, u32[]{:S(2)}) collective-permute-start(bf16[128,3072]{1,0:T(8,128)(2,1)S(1)} %broadcast_select_fusion), channel_id=1, source_target_pairs={{0,8},{8,0},{1,9},{9,1},{2,10},{10,2},{3,11},{11,3},{4,12},{12,4},... | collective-permute-start | bytes 2359304 | tf_op jit(solution)/shard_map/ppermute | solution.py:40
  41.2 18.0 %collective-permute-start.8 = (bf16[128,3072]{1,0:T(8,128)(2,1)S(1)}, bf16[128,3072]{1,0:T(8,128)(2,1)S(1)}, u32[]{:S(2)}, u32[]{:S(2)}) collective-permute-start(bf16[128,3072]{1,0:T(8,128)(2,1)S(1)} %collective-permute-done.6.refs_8_.refs_5_.refs_12_), channel_id=1, source_target_pairs={{0,1},{1,2},{2,3},{3,0},{4,5},{5,6},{6,7},{7,4},{8,11},{9,8},{10,9... | collective-permute-start | bytes 2359304 | tf_op jit(solution)/shard_map/ppermute | solution.py:51
  48.4 4.8 %collective-permute-start.9 = (bf16[2,128,128]{2,1,0:T(8,128)(2,1)S(1)}, bf16[2,128,128]{2,1,0:T(8,128)(2,1)S(1)}, u32[]{:S(2)}, u32[]{:S(2)}) collective-permute-start(bf16[2,128,128]{2,1,0:T(8,128)(2,1)S(1)} %get-tuple-element.20), channel_id=1, source_target_pairs={{0,4},{1,5},{2,6},{3,7},{4,0},{5,1},{6,2},{7,3},{8,12},{9,13},{10,... | collective-permute-start | bytes 196616 | tf_op jit(solution)/shard_map/ppermute | solution.py:51
  49.6 5.3 %collective-permute-start.10 = (bf16[2,128,128]{2,1,0:T(8,128)(2,1)S(1)}, bf16[2,128,128]{2,1,0:T(8,128)(2,1)S(1)}, u32[]{:S(2)}, u32[]{:S(2)}) collective-permute-start(bf16[2,128,128]{2,1,0:T(8,128)(2,1)S(1)} %get-tuple-element.21), channel_id=1, source_target_pairs={{0,7},{1,4},{2,5},{3,6},{4,3},{5,0},{6,1},{7,2},{8,13},{9,14},{10,... | collective-permute-start | bytes 196616 | tf_op jit(solution)/shard_map/ppermute | solution.py:51
  49.6 5.3 %collective-permute-start.11 = (bf16[2,128,128]{2,1,0:T(8,128)(2,1)S(1)}, bf16[2,128,128]{2,1,0:T(8,128)(2,1)S(1)}, u32[]{:S(2)}, u32[]{:S(2)}) collective-permute-start(bf16[2,128,128]{2,1,0:T(8,128)(2,1)S(1)} %get-tuple-element.22), channel_id=1, source_target_pairs={{0,5},{1,6},{2,7},{3,4},{4,1},{5,2},{6,3},{7,0},{8,15},{9,12},{10,... | collective-permute-start | bytes 196616 | tf_op jit(solution)/shard_map/ppermute | solution.py:51
  53.2 6.1 %collective-permute-start.12 = (bf16[2,128,128]{2,1,0:T(8,128)(2,1)S(1)}, bf16[2,128,128]{2,1,0:T(8,128)(2,1)S(1)}, u32[]{:S(2)}, u32[]{:S(2)}) collective-permute-start(bf16[2,128,128]{2,1,0:T(8,128)(2,1)S(1)} %get-tuple-element.23), channel_id=1, source_target_pairs={{0,6},{1,7},{2,4},{3,5},{4,2},{5,3},{6,0},{7,1},{8,14},{9,15},{10,... | collective-permute-start | bytes 196616 | tf_op jit(solution)/shard_map/ppermute | solution.py:51
  53.2 8.5 %collective-permute-start.13 = (bf16[2,128,128]{2,1,0:T(8,128)(2,1)S(1)}, bf16[2,128,128]{2,1,0:T(8,128)(2,1)S(1)}, u32[]{:S(2)}, u32[]{:S(2)}) collective-permute-start(bf16[2,128,128]{2,1,0:T(8,128)(2,1)S(1)} %get-tuple-element.26), channel_id=1, source_target_pairs={{0,1},{1,2},{2,3},{3,0},{4,5},{5,6},{6,7},{7,4},{8,11},{9,8},{10,9... | collective-permute-start | bytes 196616 | tf_op jit(solution)/shard_map/ppermute | solution.py:51
  54.9 7.2 %collective-permute-start.14 = (bf16[2,128,128]{2,1,0:T(8,128)(2,1)S(1)}, bf16[2,128,128]{2,1,0:T(8,128)(2,1)S(1)}, u32[]{:S(2)}, u32[]{:S(2)}) collective-permute-start(bf16[2,128,128]{2,1,0:T(8,128)(2,1)S(1)} %get-tuple-element.27), channel_id=1, source_target_pairs={{0,3},{1,0},{2,1},{3,2},{4,7},{5,4},{6,5},{7,6},{8,9},{9,10},{10,1... | collective-permute-start | bytes 196616 | tf_op jit(solution)/shard_map/ppermute | solution.py:51
  59.3 6.9 %copy-start.2 = (f32[1024]{0:T(1024)S(1)}, f32[1024]{0:T(1024)}, u32[]{:S(2)}) copy-start(f32[1024]{0:T(1024)} %param.6) | copy-start | bytes 12292
  59.3 6.9 %copy-start.3 = (f32[32]{0:T(128)S(1)}, f32[32]{0:T(128)}, u32[]{:S(2)}) copy-start(f32[32]{0:T(128)} %e_occ.5) | copy-start | bytes 388
  61.5 4.7 %collective-permute-start.15 = (bf16[2,128,128]{2,1,0:T(8,128)(2,1)S(1)}, bf16[2,128,128]{2,1,0:T(8,128)(2,1)S(1)}, u32[]{:S(2)}, u32[]{:S(2)}) collective-permute-start(bf16[2,128,128]{2,1,0:T(8,128)(2,1)S(1)} %get-tuple-element.28), channel_id=1, source_target_pairs={{0,2},{1,3},{2,0},{3,1},{4,6},{5,7},{6,4},{7,5},{8,10},{9,11},{10,... | collective-permute-start | bytes 196616 | tf_op jit(solution)/shard_map/ppermute | solution.py:51
  68.8 9.6 %collective-permute-start.17 = (bf16[128,3072]{1,0:T(8,128)(2,1)S(1)}, bf16[128,3072]{1,0:T(8,128)(2,1)S(1)}, u32[]{:S(2)}, u32[]{:S(2)}) collective-permute-start(bf16[128,3072]{1,0:T(8,128)(2,1)S(1)} %density.4), channel_id=1, source_target_pairs={{8,0},{12,4},{9,1},{13,5},{10,2},{14,6},{11,3},{15,7},{24,16},{28,... | collective-permute-start | bytes 2359304 | tf_op jit(solution)/shard_map/ppermute | solution.py:36
  74.4 13.3 %collective-permute-start.16 = (bf16[128,3072]{1,0:T(8,128)(2,1)S(1)}, bf16[128,3072]{1,0:T(8,128)(2,1)S(1)}, u32[]{:S(2)}, u32[]{:S(2)}) collective-permute-start(bf16[128,3072]{1,0:T(8,128)(2,1)S(1)} %density.4), channel_id=1, source_target_pairs={{0,12},{4,8},{1,13},{5,9},{2,14},{6,10},{3,15},{7,11},{16,28},{20,... | collective-permute-start | bytes 2359304 | tf_op jit(solution)/shard_map/ppermute | solution.py:36
  78.4 3.2 %copy-start.1 = (f32[1,128,3072]{2,1,0:T(8,128)S(1)}, f32[1,128,3072]{2,1,0:T(8,128)}, u32[]{:S(2)}) copy-start(f32[1,128,3072]{2,1,0:T(8,128)} %param.7) | copy-start | bytes 4718596
  78.6 24.6 %collective-permute-start.18 = (bf16[128,3072]{1,0:T(8,128)(2,1)S(1)}, bf16[128,3072]{1,0:T(8,128)(2,1)S(1)}, u32[]{:S(2)}, u32[]{:S(2)}) collective-permute-start(bf16[128,3072]{1,0:T(8,128)(2,1)S(1)} %add_convert_fusion), channel_id=1, source_target_pairs={{0,20},{4,16},{8,28},{12,24},{16,36},{20,32},{24,44},{28,40},{32,5... | collective-permute-start | bytes 2359304 | tf_op jit(solution)/shard_map/ppermute | solution.py:32

commit v5 on v4

--- a/solution.py
+++ b/solution.py
@@ -15,8 +15,7 @@
 N_SLABS = XL * Y
 PIECES = ((0, 0), (0, -1), (0, 1), (0, 2), (1, 0), (1, -1), (1, 1), (1, 2))
 BACK = (0, 2, 1, 3, 4, 6, 5, 7)
-INNER = 1536
-STEP = 512
+STEP = 1024
 EARLY = 7
 TURNED = 4
 BF16, F32 = jnp.bfloat16, jnp.float32
@@ -84,11 +83,12 @@
 def integrals_kernel(count, sent, *refs):
     rows, pieces, refs = refs[:3], refs[3 : 3 + count], refs[3 + count :]
     direct_ref, tile_refs, total = refs[0], refs[1:-1], refs[-1]
+    inner = rows[0].shape[1] // (2 if count > 1 else 1)
     total[...] = jnp.zeros_like(total)
 
-    @pl.loop(0, rows[0].shape[1] // INNER)
+    @pl.loop(0, rows[0].shape[1] // inner)
     def _(k):
-        part = pl.ds(pl.multiple_of(k * INNER, INNER), INNER)
+        part = pl.ds(pl.multiple_of(k * inner, inner), inner)
         left = jnp.concatenate([r[:, part] for r in rows], axis=0)
         right = jnp.concatenate([r[:, part] for r in pieces], axis=0)
         total[...] += lax.dot_general(left, right, (((1,), (1,)), ((), ())), preferred_element_type=F32)
@@ -182,7 +182,7 @@
     sent = tuple(q for q in range(EARLY) if q != TURNED)
     early, *tiles = integrals(rows, pieces[:EARLY], sent)
     swapped = exchanged(dict(zip(sent, tiles)))
-    last = [after(piece, early, *list(swapped.values())[:4]) for piece in pieces[EARLY:]]
+    last = [after(piece, early, *list(swapped.values())[:2]) for piece in pieces[EARLY:]]
     pieces = pieces[:EARLY] + last
     late, tile = integrals(rows, last, (0,))
     swapped |= exchanged({EARLY: tile})
@@ -190,9 +190,11 @@
     given = (occ_energy, e_vir, (early, late), swapped, pieces)
     part_1 = density(1, *given, None)
     going = density(2, *given, None).astype(F32) + one_block_on(part_1, 1).astype(F32)
-    back = two_blocks_on(going.astype(BF16), 1)
+    going = going.astype(BF16)
+    back = two_blocks_on(going, 1)
     total = density(0, *given, density_in.reshape(SLAB, width))
-    total = total + one_block_on(part_1, 0).astype(F32) + back.astype(F32)
+    beside = one_block_on(after(part_1, going), 0)
+    total = lax.optimization_barrier(total + back.astype(F32)) + beside.astype(F32)
     return total.reshape(density_in.shape)
 
 

time: 105 us -> 105 us (level)
  starting transfers between devices: 38.8 us -> 45.3 us
  waiting for transfers between devices: 49.7 us -> 44.6 us
  Pallas kernels: 14.3 us -> 12.5 us
    ppermute x14, waiting for transfers between devices: 28.7 us -> 22.9 us  [within(): return lax.ppermute(block, ('core', 'xl', 'y'), pairs)]
    ppermute x2, waiting for transfers between devices: 17.4 us -> 21.7 us  [two_blocks_on(): return lax.ppermute(block, ('z', 'xh', 'core', 'xl'), pairs)]
    ppermute x2, waiting for transfers between devices: 3.58 us -> 0.01 us  [one_block_on(): lax.ppermute(block, ('core', 'xl'), [(core * XL + x, (1 - core) * XL + (x...]
    ppermute x2, starting transfers between devices: 6.89 us -> 10.1 us  [one_block_on(): lax.ppermute(block, ('core', 'xl'), [(core * XL + x, (1 - core) * XL + (x...]
    ppermute x14, starting transfers between devices: 18.5 us -> 21.2 us  [within(): return lax.ppermute(block, ('core', 'xl', 'y'), pairs)]
    pallas_call x3, Pallas kernels: 7.88 us -> 6.28 us  [density(): pl.pallas_call(functools.partial(density_kernel, visit), in_specs=[pl.Blo...]
  transfers between devices with their start and end apart: 19 -> 19, of which waited for: 11 -> 8; matrix products, arithmetic and copies ran while one was open for 0% -> 0% of each run, Pallas kernels for 11% -> 10%
where the time goes in v5:
time: 105 us; the launch traced here: 104 us
  starting transfers between devices  45.3 us (43%)
  waiting for transfers between devices  44.6 us (42%)
  Pallas kernels  12.5 us (12%)
  other arithmetic  1.78 us (2%)
    ppermute x14, waiting for transfers between devices, within(): return lax.ppermute(block, ('core', 'xl', 'y'), pairs)  22.9 us
    ppermute x2, waiting for transfers between devices, two_blocks_on(): return lax.ppermute(block, ('z', 'xh', 'core', 'xl'), pairs)  21.7 us
    ppermute x14, starting transfers between devices, within(): return lax.ppermute(block, ('core', 'xl', 'y'), pairs)  21.2 us
    ppermute x2, starting transfers between devices, two_blocks_on(): return lax.ppermute(block, ('z', 'xh', 'core', 'xl'), pairs)  10.6 us
    ppermute x2, starting transfers between devices, one_block_on(): lax.ppermute(block, ('core', 'xl'), [(core * XL + x, (1 - core) * XL + (x...  10.1 us
    pallas_call x3, Pallas kernels, density(): pl.pallas_call(functools.partial(density_kernel, visit), in_specs=[pl.Blo...  6.28 us
    pallas_call x2, Pallas kernels, integrals(): pl.pallas_call(functools.partial(integrals_kernel, count, sent), in_specs...  6.22 us
    ppermute x1, starting transfers between devices, to_sibling(): return lax.ppermute(block, 'core', [(0, 1), (1, 0)])  3.3 us
  transfers between devices with their start and end apart: 19, of which 8 were waited for; matrix products, arithmetic and copies ran while one was open for 0% of the time, Pallas kernels for 10%

profile of v5, /device:TPU:1, one launch (start us, length us, event | category | flops | bytes accessed | tf_op | source)
XLA Modules:
  0.0 104.3 jit_solution(15658971573735355595)
XLA Ops:
  0.0 2.1 %collective-permute-start.4 = (bf16[128,3072]{1,0:T(8,128)(2,1)}, bf16[128,3072]{1,0:T(8,128)(2,1)S(1)}, u32[]{:S(2)}, u32[]{:S(2)}) collective-permute-start(bf16[128,3072]{1,0:T(8,128)(2,1)} %bitcast.5), channel_id=1, source_target_pairs={{0,3},{1,0},{2,1},{3,2},{4,7},{5,4},{6,5},{7,6},{8,9},{9,10},{10,1... | collective-permute-start | bytes 2359304 | tf_op jit(solution)/shard_map/ppermute | solution.py:50
  2.1 1.5 %collective-permute-start.3 = (bf16[128,3072]{1,0:T(8,128)(2,1)}, bf16[128,3072]{1,0:T(8,128)(2,1)S(1)}, u32[]{:S(2)}, u32[]{:S(2)}) collective-permute-start(bf16[128,3072]{1,0:T(8,128)(2,1)} %bitcast.6), channel_id=1, source_target_pairs={{0,1},{1,2},{2,3},{3,0},{4,5},{5,6},{6,7},{7,4},{8,11},{9,8},{10,9... | collective-permute-start | bytes 2359304 | tf_op jit(solution)/shard_map/ppermute | solution.py:50
  3.6 1.2 %collective-permute-start.1 = (bf16[128,3072]{1,0:T(8,128)(2,1)}, bf16[128,3072]{1,0:T(8,128)(2,1)S(1)}, u32[]{:S(2)}, u32[]{:S(2)}) collective-permute-start(bf16[128,3072]{1,0:T(8,128)(2,1)} %bitcast.7), channel_id=1, source_target_pairs={{0,4},{1,5},{2,6},{3,7},{4,0},{5,1},{6,2},{7,3},{8,12},{9,13},{10,... | collective-permute-start | bytes 2359304 | tf_op jit(solution)/shard_map/ppermute | solution.py:50
  4.9 7.1 %collective-permute-start = (bf16[128,3072]{1,0:T(8,128)(2,1)}, bf16[128,3072]{1,0:T(8,128)(2,1)}, u32[]{:S(2)}, u32[]{:S(2)}) collective-permute-start(bf16[128,3072]{1,0:T(8,128)(2,1)} %bitcast.8), channel_id=1, source_target_pairs={{0,244},{4,240},{8,252},{12,248},{16,4},{20,0},{24,12},{28,8},{32,... | collective-permute-start | bytes 2359304 | tf_op jit(solution)/shard_map/ppermute | solution.py:31
  12.0 6.0 %collective-permute-done.4.refs_5_.refs_2_.refs_9_ = bf16[128,3072]{1,0:T(8,128)(2,1)S(1)} collective-permute-done((bf16[128,3072]{1,0:T(8,128)(2,1)}, bf16[128,3072]{1,0:T(8,128)(2,1)S(1)}, u32[]{:S(2)}, u32[]{:S(2)}) %collective-permute-start.4) | collective-permute-done | bytes 786464 | tf_op jit(solution)/shard_map/ppermute | solution.py:50
  18.0 2.4 %collective-permute-done.3.refs_4_.refs_1_.refs_8_ = bf16[128,3072]{1,0:T(8,128)(2,1)S(1)} collective-permute-done((bf16[128,3072]{1,0:T(8,128)(2,1)}, bf16[128,3072]{1,0:T(8,128)(2,1)S(1)}, u32[]{:S(2)}, u32[]{:S(2)}) %collective-permute-start.3) | collective-permute-done | bytes 786464 | tf_op jit(solution)/shard_map/ppermute | solution.py:50
  20.4 1.0 collective-permute-done.1.refs_7_.refs_4_.refs_11_
  21.4 2.3 %collective-permute-start.6 = (bf16[128,3072]{1,0:T(8,128)(2,1)S(1)}, bf16[128,3072]{1,0:T(8,128)(2,1)S(1)}, u32[]{:S(2)}, u32[]{:S(2)}) collective-permute-start(bf16[128,3072]{1,0:T(8,128)(2,1)S(1)} %collective-permute-done.1.refs_7_.refs_4_.refs_11_), channel_id=1, source_target_pairs={{0,1},{1,2},{2,3},{3,0},{4,5},{5,6},{6,7},{7,4},{8,11},{9,8},{10,9... | collective-permute-start | bytes 2359304 | tf_op jit(solution)/shard_map/ppermute | solution.py:50
  23.7 1.1 %collective-permute-start.7 = (bf16[128,3072]{1,0:T(8,128)(2,1)S(1)}, bf16[128,3072]{1,0:T(8,128)(2,1)S(1)}, u32[]{:S(2)}, u32[]{:S(2)}) collective-permute-start(bf16[128,3072]{1,0:T(8,128)(2,1)S(1)} %collective-permute-done.4.refs_5_.refs_2_.refs_9_), channel_id=1, source_target_pairs={{0,4},{1,5},{2,6},{3,7},{4,0},{5,1},{6,2},{7,3},{8,12},{9,13},{10,... | collective-permute-start | bytes 2359304 | tf_op jit(solution)/shard_map/ppermute | solution.py:50
  24.8 1.2 %collective-permute-start.5 = (bf16[128,3072]{1,0:T(8,128)(2,1)S(1)}, bf16[128,3072]{1,0:T(8,128)(2,1)S(1)}, u32[]{:S(2)}, u32[]{:S(2)}) collective-permute-start(bf16[128,3072]{1,0:T(8,128)(2,1)S(1)} %collective-permute-done.3.refs_4_.refs_1_.refs_8_), channel_id=1, source_target_pairs={{0,1},{1,2},{2,3},{3,0},{4,5},{5,6},{6,7},{7,4},{8,11},{9,8},{10,9... | collective-permute-start | bytes 2359304 | tf_op jit(solution)/shard_map/ppermute | solution.py:50
  26.0 2.0 %collective-permute-done.refs_2_ = bf16[128,3072]{1,0:T(8,128)(2,1)} collective-permute-done((bf16[128,3072]{1,0:T(8,128)(2,1)}, bf16[128,3072]{1,0:T(8,128)(2,1)}, u32[]{:S(2)}, u32[]{:S(2)}) %collective-permute-start) | collective-permute-done | bytes 786464 | tf_op jit(solution)/shard_map/ppermute | solution.py:31
  28.0 3.3 %collective-permute-start.2 = (bf16[128,3072]{1,0:T(8,128)(2,1)S(1)}, bf16[128,3072]{1,0:T(8,128)(2,1)S(1)}, u32[]{:S(2)}, u32[]{:S(2)}) collective-permute-start(bf16[128,3072]{1,0:T(8,128)(2,1)S(1)} %broadcast_select_fusion), channel_id=1, source_target_pairs={{0,8},{8,0},{1,9},{9,1},{2,10},{10,2},{3,11},{11,3},{4,12},{12,4},... | collective-permute-start | bytes 2359304 | tf_op jit(solution)/shard_map/ppermute | solution.py:39
  31.3 9.9 %collective-permute-done.5.refs_6_.refs_3_.refs_10_ = bf16[128,3072]{1,0:T(8,128)(2,1)S(1)} collective-permute-done((bf16[128,3072]{1,0:T(8,128)(2,1)S(1)}, bf16[128,3072]{1,0:T(8,128)(2,1)S(1)}, u32[]{:S(2)}, u32[]{:S(2)}) %collective-permute-start.5) | collective-permute-done | bytes 786464 | tf_op jit(solution)/shard_map/ppermute | solution.py:50
  41.2 2.9 %collective-permute-start.8 = (bf16[128,3072]{1,0:T(8,128)(2,1)S(1)}, bf16[128,3072]{1,0:T(8,128)(2,1)S(1)}, u32[]{:S(2)}, u32[]{:S(2)}) collective-permute-start(bf16[128,3072]{1,0:T(8,128)(2,1)S(1)} %collective-permute-done.6.refs_8_.refs_5_.refs_12_), channel_id=1, source_target_pairs={{0,1},{1,2},{2,3},{3,0},{4,5},{5,6},{6,7},{7,4},{8,11},{9,8},{10,9... | collective-permute-start | bytes 2359304 | tf_op jit(solution)/shard_map/ppermute | solution.py:50
  44.2 4.2 %integrals.2 = (bf16[384,896]{1,0:T(8,128)(2,1)S(1)}, bf16[2,128,128]{2,1,0:T(8,128)(2,1)S(1)}, bf16[2,128,128]{2,1,0:T(8,128)(2,1)S(1)}, bf16[2,128,128]{2,1,0:...) custom-call(bf16[128,3072]{1,0:T(8,128)(2,1)S(1)} %bitcast.9, ...), custom_call_target="tpu_custom_call" | custom-call | flops 2113929216 | bytes 7864320 | tf_op jit(solution)/shard_map/integrals/pallas_call | solution.py:106
  48.4 1.2 %collective-permute-start.9 = (bf16[2,128,128]{2,1,0:T(8,128)(2,1)S(1)}, bf16[2,128,128]{2,1,0:T(8,128)(2,1)S(1)}, u32[]{:S(2)}, u32[]{:S(2)}) collective-permute-start(bf16[2,128,128]{2,1,0:T(8,128)(2,1)S(1)} %get-tuple-element.21), channel_id=1, source_target_pairs={{0,4},{1,5},{2,6},{3,7},{4,0},{5,1},{6,2},{7,3},{8,12},{9,13},{10,... | collective-permute-start | bytes 196616 | tf_op jit(solution)/shard_map/ppermute | solution.py:50
  49.6 3.6 %collective-permute-start.11 = (bf16[2,128,128]{2,1,0:T(8,128)(2,1)S(1)}, bf16[2,128,128]{2,1,0:T(8,128)(2,1)S(1)}, u32[]{:S(2)}, u32[]{:S(2)}) collective-permute-start(bf16[2,128,128]{2,1,0:T(8,128)(2,1)S(1)} %get-tuple-element.25), channel_id=1, source_target_pairs={{0,5},{1,6},{2,7},{3,4},{4,1},{5,2},{6,3},{7,0},{8,15},{9,12},{10,... | collective-permute-start | bytes 196616 | tf_op jit(solution)/shard_map/ppermute | solution.py:50
  53.2 1.2 %collective-permute-start.13 = (bf16[2,128,128]{2,1,0:T(8,128)(2,1)S(1)}, bf16[2,128,128]{2,1,0:T(8,128)(2,1)S(1)}, u32[]{:S(2)}, u32[]{:S(2)}) collective-permute-start(bf16[2,128,128]{2,1,0:T(8,128)(2,1)S(1)} %get-tuple-element.27), channel_id=1, source_target_pairs={{0,1},{1,2},{2,3},{3,0},{4,5},{5,6},{6,7},{7,4},{8,11},{9,8},{10,9... | collective-permute-start | bytes 196616 | tf_op jit(solution)/shard_map/ppermute | solution.py:50
  54.4 0.6 collective-permute-done.10.refs_2_
  55.0 2.0 %integrals.3 = (bf16[384,128]{1,0:T(8,128)(2,1)S(1)}, bf16[2,128,128]{2,1,0:T(8,128)(2,1)S(1)}) custom-call(bf16[128,3072]{1,0:T(8,128)(2,1)S(1)} %bitcast.11, bf16[128,3072]{1,0:T(8,128)(2,1)S(1)} %collective-permute-done.2.refs_1_, bf16[128,3072]{1,0:T(8,128)(2,1)} %collective-permute-done.refs_2_, ...), custom_call_target="tpu_custom_call" | custom-call | flops 301989888 | bytes 3145728 | tf_op jit(solution)/shard_map/integrals/pallas_call | solution.py:106
  56.9 2.9 %collective-permute-start.15 = (bf16[2,128,128]{2,1,0:T(8,128)(2,1)S(1)}, bf16[2,128,128]{2,1,0:T(8,128)(2,1)S(1)}, u32[]{:S(2)}, u32[]{:S(2)}) collective-permute-start(bf16[2,128,128]{2,1,0:T(8,128)(2,1)S(1)} %get-tuple-element.29), channel_id=1, source_target_pairs={{0,2},{1,3},{2,0},{3,1},{4,6},{5,7},{6,4},{7,5},{8,10},{9,11},{10,... | collective-permute-start | bytes 196616 | tf_op jit(solution)/shard_map/ppermute | solution.py:50
  59.8 3.0 %collective-permute-done.14.refs_5_ = bf16[2,128,128]{2,1,0:T(8,128)(2,1)S(1)} collective-permute-done((bf16[2,128,128]{2,1,0:T(8,128)(2,1)S(1)}, bf16[2,128,128]{2,1,0:T(8,128)(2,1)S(1)}, u32[]{:S(2)}, u32[]{:S(2)}) %collective-permute-start.14) | collective-permute-done | bytes 65568 | tf_op jit(solution)/shard_map/ppermute | solution.py:50
  62.9 2.1 %density.5 = bf16[128,3072]{1,0:T(8,128)(2,1)S(1)} custom-call(f32[32]{0:T(128)S(1)} %copy-done.3, f32[8,1,128]{2,1,0:T(1,128)S(1)} %bitcast.16, bf16[384,896]{1,0:T(8,128)(2,1)S(1)} %get-tuple-element.19.early_ref, bf16[384,128]{1,0:T(8,128)(2,1)S(1)} %get-tuple-element.24.late_ref, bf16[2,128,128]{2,1,0:T(8,128)(2,1)S(1)} %collective-permute-done.9.refs_0_, ...), custom_call_target="tpu_custom_call" | custom-call | flops 805306368 | bytes 7077888 | tf_op jit(solution)/shard_map/density/pallas_call | solution.py:157
  65.0 8.9 %collective-permute-start.16 = (bf16[128,3072]{1,0:T(8,128)(2,1)S(1)}, bf16[128,3072]{1,0:T(8,128)(2,1)S(1)}, u32[]{:S(2)}, u32[]{:S(2)}) collective-permute-start(bf16[128,3072]{1,0:T(8,128)(2,1)S(1)} %density.5), channel_id=1, source_target_pairs={{8,0},{12,4},{9,1},{13,5},{10,2},{14,6},{11,3},{15,7},{24,16},{28,... | collective-permute-start | bytes 2359304 | tf_op jit(solution)/shard_map/ppermute | solution.py:35
  73.8 2.1 %density.4 = bf16[128,3072]{1,0:T(8,128)(2,1)S(1)} custom-call(f32[32]{0:T(128)S(1)} %copy-done.3, f32[8,1,128]{2,1,0:T(1,128)S(1)} %bitcast.17, bf16[384,896]{1,0:T(8,128)(2,1)S(1)} %get-tuple-element.19.early_ref, bf16[384,128]{1,0:T(8,128)(2,1)S(1)} %get-tuple-element.24.late_ref, bf16[2,128,128]{2,1,0:T(8,128)(2,1)S(1)} %collective-permute-done.9.refs_0_, ...), custom_call_target="tpu_custom_call" | custom-call | flops 805306368 | bytes 7077888 | tf_op jit(solution)/shard_map/density/pallas_call | solution.py:157
  75.9 0.2 add_convert_fusion
  76.1 3.5 %collective-permute-start.17 = (bf16[128,3072]{1,0:T(8,128)(2,1)S(1)}, bf16[128,3072]{1,0:T(8,128)(2,1)S(1)}, u32[]{:S(2)}, u32[]{:S(2)}) collective-permute-start(bf16[128,3072]{1,0:T(8,128)(2,1)S(1)} %add_convert_fusion), channel_id=1, source_target_pairs={{0,20},{4,16},{8,28},{12,24},{16,36},{20,32},{24,44},{28,40},{32,5... | collective-permute-start | bytes 2359304 | tf_op jit(solution)/shard_map/ppermute | solution.py:31
  79.7 1.3 %collective-permute-start.18 = (bf16[128,3072]{1,0:T(8,128)(2,1)S(1)}, bf16[128,3072]{1,0:T(8,128)(2,1)S(1)}, u32[]{:S(2)}, u32[]{:S(2)}) collective-permute-start(bf16[128,3072]{1,0:T(8,128)(2,1)S(1)} %density.5), channel_id=1, source_target_pairs={{0,12},{4,8},{1,13},{5,9},{2,14},{6,10},{3,15},{7,11},{16,28},{20,... | collective-permute-start | bytes 2359304 | tf_op jit(solution)/shard_map/ppermute | solution.py:35
  81.0 2.1 %density.3 = f32[128,3072]{1,0:T(8,128)S(1)} custom-call(f32[32]{0:T(128)S(1)} %copy-done.3, f32[8,1,128]{2,1,0:T(1,128)S(1)} %bitcast.18, bf16[384,896]{1,0:T(8,128)(2,1)S(1)} %get-tuple-element.19.early_ref, bf16[384,128]{1,0:T(8,128)(2,1)S(1)} %get-tuple-element.24.late_ref, bf16[128,3072]{1,0:T(8,128)(2,1)S(1)} %bitcast.14, ...), custom_call_target="tpu_custom_call" | custom-call | flops 805306368 | bytes 7077888 | tf_op jit(solution)/shard_map/density/pallas_call | solution.py:157
  83.1 19.7 %collective-permute-done.17 = bf16[128,3072]{1,0:T(8,128)(2,1)S(1)} collective-permute-done((bf16[128,3072]{1,0:T(8,128)(2,1)S(1)}, bf16[128,3072]{1,0:T(8,128)(2,1)S(1)}, u32[]{:S(2)}, u32[]{:S(2)}) %collective-permute-start.17) | collective-permute-done | bytes 786464 | tf_op jit(solution)/shard_map/ppermute | solution.py:31
  102.8 0.1 convert_add_fusion
  102.9 1.4 %add_bitcast_fusion = f32[1,128,3072]{2,1,0:T(8,128)} fusion(f32[128,3072]{1,0:T(8,128)S(1)} %convert_add_fusion, bf16[128,3072]{1,0:T(8,128)(2,1)S(1)} %collective-permute-done.18), kind=kLoop, calls=%fused_computation | loop fusion | flops 786432 | bytes 3932160 | tf_op jit(solution)/shard_map/reshape | solution.py:198
  (23 shorter events, 0.1 us)
Async XLA Ops:
  0.0 44.2 %copy-start = (bf16[1,128,3072]{2,1,0:T(8,128)(2,1)S(1)}, bf16[1,128,3072]{2,1,0:T(8,128)(2,1)}, u32[]{:S(2)}) copy-start(bf16[1,128,3072]{2,1,0:T(8,128)(2,1)} %param.4) | copy-start | bytes 2359300
  0.0 18.0 %collective-permute-start.4 = (bf16[128,3072]{1,0:T(8,128)(2,1)}, bf16[128,3072]{1,0:T(8,128)(2,1)S(1)}, u32[]{:S(2)}, u32[]{:S(2)}) collective-permute-start(bf16[128,3072]{1,0:T(8,128)(2,1)} %bitcast.5), channel_id=1, source_target_pairs={{0,3},{1,0},{2,1},{3,2},{4,7},{5,4},{6,5},{7,6},{8,9},{9,10},{10,1... | collective-permute-start | bytes 2359304 | tf_op jit(solution)/shard_map/ppermute | solution.py:50
  2.1 18.2 %collective-permute-start.3 = (bf16[128,3072]{1,0:T(8,128)(2,1)}, bf16[128,3072]{1,0:T(8,128)(2,1)S(1)}, u32[]{:S(2)}, u32[]{:S(2)}) collective-permute-start(bf16[128,3072]{1,0:T(8,128)(2,1)} %bitcast.6), channel_id=1, source_target_pairs={{0,1},{1,2},{2,3},{3,0},{4,5},{5,6},{6,7},{7,4},{8,11},{9,8},{10,9... | collective-permute-start | bytes 2359304 | tf_op jit(solution)/shard_map/ppermute | solution.py:50
  3.6 17.7 %collective-permute-start.1 = (bf16[128,3072]{1,0:T(8,128)(2,1)}, bf16[128,3072]{1,0:T(8,128)(2,1)S(1)}, u32[]{:S(2)}, u32[]{:S(2)}) collective-permute-start(bf16[128,3072]{1,0:T(8,128)(2,1)} %bitcast.7), channel_id=1, source_target_pairs={{0,4},{1,5},{2,6},{3,7},{4,0},{5,1},{6,2},{7,3},{8,12},{9,13},{10,... | collective-permute-start | bytes 2359304 | tf_op jit(solution)/shard_map/ppermute | solution.py:50
  4.9 23.1 %collective-permute-start = (bf16[128,3072]{1,0:T(8,128)(2,1)}, bf16[128,3072]{1,0:T(8,128)(2,1)}, u32[]{:S(2)}, u32[]{:S(2)}) collective-permute-start(bf16[128,3072]{1,0:T(8,128)(2,1)} %bitcast.8), channel_id=1, source_target_pairs={{0,244},{4,240},{8,252},{12,248},{16,4},{20,0},{24,12},{28,8},{32,... | collective-permute-start | bytes 2359304 | tf_op jit(solution)/shard_map/ppermute | solution.py:31
  21.4 19.9 %collective-permute-start.6 = (bf16[128,3072]{1,0:T(8,128)(2,1)S(1)}, bf16[128,3072]{1,0:T(8,128)(2,1)S(1)}, u32[]{:S(2)}, u32[]{:S(2)}) collective-permute-start(bf16[128,3072]{1,0:T(8,128)(2,1)S(1)} %collective-permute-done.1.refs_7_.refs_4_.refs_11_), channel_id=1, source_target_pairs={{0,1},{1,2},{2,3},{3,0},{4,5},{5,6},{6,7},{7,4},{8,11},{9,8},{10,9... | collective-permute-start | bytes 2359304 | tf_op jit(solution)/shard_map/ppermute | solution.py:50
  23.7 20.5 %collective-permute-start.7 = (bf16[128,3072]{1,0:T(8,128)(2,1)S(1)}, bf16[128,3072]{1,0:T(8,128)(2,1)S(1)}, u32[]{:S(2)}, u32[]{:S(2)}) collective-permute-start(bf16[128,3072]{1,0:T(8,128)(2,1)S(1)} %collective-permute-done.4.refs_5_.refs_2_.refs_9_), channel_id=1, source_target_pairs={{0,4},{1,5},{2,6},{3,7},{4,0},{5,1},{6,2},{7,3},{8,12},{9,13},{10,... | collective-permute-start | bytes 2359304 | tf_op jit(solution)/shard_map/ppermute | solution.py:50
  24.8 16.5 %collective-permute-start.5 = (bf16[128,3072]{1,0:T(8,128)(2,1)S(1)}, bf16[128,3072]{1,0:T(8,128)(2,1)S(1)}, u32[]{:S(2)}, u32[]{:S(2)}) collective-permute-start(bf16[128,3072]{1,0:T(8,128)(2,1)S(1)} %collective-permute-done.3.refs_4_.refs_1_.refs_8_), channel_id=1, source_target_pairs={{0,1},{1,2},{2,3},{3,0},{4,5},{5,6},{6,7},{7,4},{8,11},{9,8},{10,9... | collective-permute-start | bytes 2359304 | tf_op jit(solution)/shard_map/ppermute | solution.py:50
  28.0 16.1 %collective-permute-start.2 = (bf16[128,3072]{1,0:T(8,128)(2,1)S(1)}, bf16[128,3072]{1,0:T(8,128)(2,1)S(1)}, u32[]{:S(2)}, u32[]{:S(2)}) collective-permute-start(bf16[128,3072]{1,0:T(8,128)(2,1)S(1)} %broadcast_select_fusion), channel_id=1, source_target_pairs={{0,8},{8,0},{1,9},{9,1},{2,10},{10,2},{3,11},{11,3},{4,12},{12,4},... | collective-permute-start | bytes 2359304 | tf_op jit(solution)/shard_map/ppermute | solution.py:39
  41.2 13.7 %collective-permute-start.8 = (bf16[128,3072]{1,0:T(8,128)(2,1)S(1)}, bf16[128,3072]{1,0:T(8,128)(2,1)S(1)}, u32[]{:S(2)}, u32[]{:S(2)}) collective-permute-start(bf16[128,3072]{1,0:T(8,128)(2,1)S(1)} %collective-permute-done.6.refs_8_.refs_5_.refs_12_), channel_id=1, source_target_pairs={{0,1},{1,2},{2,3},{3,0},{4,5},{5,6},{6,7},{7,4},{8,11},{9,8},{10,9... | collective-permute-start | bytes 2359304 | tf_op jit(solution)/shard_map/ppermute | solution.py:50
  48.4 4.8 %collective-permute-start.9 = (bf16[2,128,128]{2,1,0:T(8,128)(2,1)S(1)}, bf16[2,128,128]{2,1,0:T(8,128)(2,1)S(1)}, u32[]{:S(2)}, u32[]{:S(2)}) collective-permute-start(bf16[2,128,128]{2,1,0:T(8,128)(2,1)S(1)} %get-tuple-element.21), channel_id=1, source_target_pairs={{0,4},{1,5},{2,6},{3,7},{4,0},{5,1},{6,2},{7,3},{8,12},{9,13},{10,... | collective-permute-start | bytes 196616 | tf_op jit(solution)/shard_map/ppermute | solution.py:50
  49.6 5.3 %collective-permute-start.10 = (bf16[2,128,128]{2,1,0:T(8,128)(2,1)S(1)}, bf16[2,128,128]{2,1,0:T(8,128)(2,1)S(1)}, u32[]{:S(2)}, u32[]{:S(2)}) collective-permute-start(bf16[2,128,128]{2,1,0:T(8,128)(2,1)S(1)} %get-tuple-element.22), channel_id=1, source_target_pairs={{0,7},{1,4},{2,5},{3,6},{4,3},{5,0},{6,1},{7,2},{8,13},{9,14},{10,... | collective-permute-start | bytes 196616 | tf_op jit(solution)/shard_map/ppermute | solution.py:50
  49.6 10.2 %collective-permute-start.11 = (bf16[2,128,128]{2,1,0:T(8,128)(2,1)S(1)}, bf16[2,128,128]{2,1,0:T(8,128)(2,1)S(1)}, u32[]{:S(2)}, u32[]{:S(2)}) collective-permute-start(bf16[2,128,128]{2,1,0:T(8,128)(2,1)S(1)} %get-tuple-element.25), channel_id=1, source_target_pairs={{0,5},{1,6},{2,7},{3,4},{4,1},{5,2},{6,3},{7,0},{8,15},{9,12},{10,... | collective-permute-start | bytes 196616 | tf_op jit(solution)/shard_map/ppermute | solution.py:50
  53.2 6.6 %collective-permute-start.12 = (bf16[2,128,128]{2,1,0:T(8,128)(2,1)S(1)}, bf16[2,128,128]{2,1,0:T(8,128)(2,1)S(1)}, u32[]{:S(2)}, u32[]{:S(2)}) collective-permute-start(bf16[2,128,128]{2,1,0:T(8,128)(2,1)S(1)} %get-tuple-element.26), channel_id=1, source_target_pairs={{0,6},{1,7},{2,4},{3,5},{4,2},{5,3},{6,0},{7,1},{8,14},{9,15},{10,... | collective-permute-start | bytes 196616 | tf_op jit(solution)/shard_map/ppermute | solution.py:50
  53.2 6.6 %collective-permute-start.13 = (bf16[2,128,128]{2,1,0:T(8,128)(2,1)S(1)}, bf16[2,128,128]{2,1,0:T(8,128)(2,1)S(1)}, u32[]{:S(2)}, u32[]{:S(2)}) collective-permute-start(bf16[2,128,128]{2,1,0:T(8,128)(2,1)S(1)} %get-tuple-element.27), channel_id=1, source_target_pairs={{0,1},{1,2},{2,3},{3,0},{4,5},{5,6},{6,7},{7,4},{8,11},{9,8},{10,9... | collective-permute-start | bytes 196616 | tf_op jit(solution)/shard_map/ppermute | solution.py:50
  54.9 7.9 %collective-permute-start.14 = (bf16[2,128,128]{2,1,0:T(8,128)(2,1)S(1)}, bf16[2,128,128]{2,1,0:T(8,128)(2,1)S(1)}, u32[]{:S(2)}, u32[]{:S(2)}) collective-permute-start(bf16[2,128,128]{2,1,0:T(8,128)(2,1)S(1)} %get-tuple-element.28), channel_id=1, source_target_pairs={{0,3},{1,0},{2,1},{3,2},{4,7},{5,4},{6,5},{7,6},{8,9},{9,10},{10,1... | collective-permute-start | bytes 196616 | tf_op jit(solution)/shard_map/ppermute | solution.py:50
  54.9 7.9 %copy-start.2 = (f32[1024]{0:T(1024)S(1)}, f32[1024]{0:T(1024)}, u32[]{:S(2)}) copy-start(f32[1024]{0:T(1024)} %param.6) | copy-start | bytes 12292
  54.9 7.9 %copy-start.3 = (f32[32]{0:T(128)S(1)}, f32[32]{0:T(128)}, u32[]{:S(2)}) copy-start(f32[32]{0:T(128)} %e_occ.5) | copy-start | bytes 388
  56.9 5.9 %collective-permute-start.15 = (bf16[2,128,128]{2,1,0:T(8,128)(2,1)S(1)}, bf16[2,128,128]{2,1,0:T(8,128)(2,1)S(1)}, u32[]{:S(2)}, u32[]{:S(2)}) collective-permute-start(bf16[2,128,128]{2,1,0:T(8,128)(2,1)S(1)} %get-tuple-element.29), channel_id=1, source_target_pairs={{0,2},{1,3},{2,0},{3,1},{4,6},{5,7},{6,4},{7,5},{8,10},{9,11},{10,... | collective-permute-start | bytes 196616 | tf_op jit(solution)/shard_map/ppermute | solution.py:50
  65.0 11.0 %collective-permute-start.16 = (bf16[128,3072]{1,0:T(8,128)(2,1)S(1)}, bf16[128,3072]{1,0:T(8,128)(2,1)S(1)}, u32[]{:S(2)}, u32[]{:S(2)}) collective-permute-start(bf16[128,3072]{1,0:T(8,128)(2,1)S(1)} %density.5), channel_id=1, source_target_pairs={{8,0},{12,4},{9,1},{13,5},{10,2},{14,6},{11,3},{15,7},{24,16},{28,... | collective-permute-start | bytes 2359304 | tf_op jit(solution)/shard_map/ppermute | solution.py:35
  75.9 5.0 %copy-start.1 = (f32[1,128,3072]{2,1,0:T(8,128)S(1)}, f32[1,128,3072]{2,1,0:T(8,128)}, u32[]{:S(2)}) copy-start(f32[1,128,3072]{2,1,0:T(8,128)} %param.7) | copy-start | bytes 4718596
  76.1 26.6 %collective-permute-start.17 = (bf16[128,3072]{1,0:T(8,128)(2,1)S(1)}, bf16[128,3072]{1,0:T(8,128)(2,1)S(1)}, u32[]{:S(2)}, u32[]{:S(2)}) collective-permute-start(bf16[128,3072]{1,0:T(8,128)(2,1)S(1)} %add_convert_fusion), channel_id=1, source_target_pairs={{0,20},{4,16},{8,28},{12,24},{16,36},{20,32},{24,44},{28,40},{32,5... | collective-permute-start | bytes 2359304 | tf_op jit(solution)/shard_map/ppermute | solution.py:31
  79.7 23.3 %collective-permute-start.18 = (bf16[128,3072]{1,0:T(8,128)(2,1)S(1)}, bf16[128,3072]{1,0:T(8,128)(2,1)S(1)}, u32[]{:S(2)}, u32[]{:S(2)}) collective-permute-start(bf16[128,3072]{1,0:T(8,128)(2,1)S(1)} %density.5), channel_id=1, source_target_pairs={{0,12},{4,8},{1,13},{5,9},{2,14},{6,10},{3,15},{7,11},{16,28},{20,... | collective-permute-start | bytes 2359304 | tf_op jit(solution)/shard_map/ppermute | solution.py:35

commit v6 on v5

--- a/solution.py
+++ b/solution.py
@@ -15,7 +15,7 @@
 N_SLABS = XL * Y
 PIECES = ((0, 0), (0, -1), (0, 1), (0, 2), (1, 0), (1, -1), (1, 1), (1, 2))
 BACK = (0, 2, 1, 3, 4, 6, 5, 7)
-STEP = 1024
+STEP = 1536
 EARLY = 7
 TURNED = 4
 BF16, F32 = jnp.bfloat16, jnp.float32
@@ -179,7 +179,7 @@
     next_2 = two_blocks_on(home, -1)
     next_1 = to_sibling(jnp.where(core == 0, next_2, pieces[TURNED]))
     rows = [home, next_1, next_2]
-    sent = tuple(q for q in range(EARLY) if q != TURNED)
+    sent = (3, 0, 5, 6, 1, 2)
     early, *tiles = integrals(rows, pieces[:EARLY], sent)
     swapped = exchanged(dict(zip(sent, tiles)))
     last = [after(piece, early, *list(swapped.values())[:2]) for piece in pieces[EARLY:]]

time: 105 us -> 103 us (0.981)
  starting transfers between devices: 45.3 us -> 42.2 us
  waiting for transfers between devices: 44.6 us -> 47 us
    ppermute x14, starting transfers between devices: 21.2 us -> 18.8 us  [within(): return lax.ppermute(block, ('core', 'xl', 'y'), pairs)]
    ppermute x14, waiting for transfers between devices: 22.9 us -> 25.2 us  [within(): return lax.ppermute(block, ('core', 'xl', 'y'), pairs)]
  transfers between devices with their start and end apart: 19 -> 19, of which waited for: 8 -> 9; matrix products, arithmetic and copies ran while one was open for 0% -> 0% of each run, Pallas kernels for 10% -> 10%
where the time goes in v6:
time: 103 us
  waiting for transfers between devices  47 us (46%)
  starting transfers between devices  42.2 us (41%)
  Pallas kernels  12 us (12%)
  other arithmetic  1.78 us (2%)
    ppermute x14, waiting for transfers between devices, within(): return lax.ppermute(block, ('core', 'xl', 'y'), pairs)  25.2 us
    ppermute x2, waiting for transfers between devices, two_blocks_on(): return lax.ppermute(block, ('z', 'xh', 'core', 'xl'), pairs)  21.8 us
    ppermute x14, starting transfers between devices, within(): return lax.ppermute(block, ('core', 'xl', 'y'), pairs)  18.8 us
    ppermute x2, starting transfers between devices, one_block_on(): lax.ppermute(block, ('core', 'xl'), [(core * XL + x, (1 - core) * XL + (x...  10.5 us
    ppermute x2, starting transfers between devices, two_blocks_on(): return lax.ppermute(block, ('z', 'xh', 'core', 'xl'), pairs)  9.67 us
    pallas_call x2, Pallas kernels, integrals(): pl.pallas_call(functools.partial(integrals_kernel, count, sent), in_specs...  6.24 us
    pallas_call x3, Pallas kernels, density(): pl.pallas_call(functools.partial(density_kernel, visit), in_specs=[pl.Blo...  5.72 us
    ppermute x1, starting transfers between devices, to_sibling(): return lax.ppermute(block, 'core', [(0, 1), (1, 0)])  3.3 us
  transfers between devices with their start and end apart: 19, of which 9 were waited for; matrix products, arithmetic and copies ran while one was open for 0% of the time, Pallas kernels for 10%

profile of v6, /device:TPU:1, one launch (start us, length us, event | category | flops | bytes accessed | tf_op | source)
XLA Modules:
  0.0 103.1 jit_solution(14214241204896037206)
XLA Ops:
  0.0 2.1 %collective-permute-start.4 = (bf16[128,3072]{1,0:T(8,128)(2,1)}, bf16[128,3072]{1,0:T(8,128)(2,1)S(1)}, u32[]{:S(2)}, u32[]{:S(2)}) collective-permute-start(bf16[128,3072]{1,0:T(8,128)(2,1)} %bitcast.5), channel_id=1, source_target_pairs={{0,3},{1,0},{2,1},{3,2},{4,7},{5,4},{6,5},{7,6},{8,9},{9,10},{10,1... | collective-permute-start | bytes 2359304 | tf_op jit(solution)/shard_map/ppermute | solution.py:50
  2.1 1.5 %collective-permute-start.3 = (bf16[128,3072]{1,0:T(8,128)(2,1)}, bf16[128,3072]{1,0:T(8,128)(2,1)S(1)}, u32[]{:S(2)}, u32[]{:S(2)}) collective-permute-start(bf16[128,3072]{1,0:T(8,128)(2,1)} %bitcast.6), channel_id=1, source_target_pairs={{0,1},{1,2},{2,3},{3,0},{4,5},{5,6},{6,7},{7,4},{8,11},{9,8},{10,9... | collective-permute-start | bytes 2359304 | tf_op jit(solution)/shard_map/ppermute | solution.py:50
  3.6 1.2 %collective-permute-start.1 = (bf16[128,3072]{1,0:T(8,128)(2,1)}, bf16[128,3072]{1,0:T(8,128)(2,1)S(1)}, u32[]{:S(2)}, u32[]{:S(2)}) collective-permute-start(bf16[128,3072]{1,0:T(8,128)(2,1)} %bitcast.7), channel_id=1, source_target_pairs={{0,4},{1,5},{2,6},{3,7},{4,0},{5,1},{6,2},{7,3},{8,12},{9,13},{10,... | collective-permute-start | bytes 2359304 | tf_op jit(solution)/shard_map/ppermute | solution.py:50
  4.9 7.1 %collective-permute-start = (bf16[128,3072]{1,0:T(8,128)(2,1)}, bf16[128,3072]{1,0:T(8,128)(2,1)}, u32[]{:S(2)}, u32[]{:S(2)}) collective-permute-start(bf16[128,3072]{1,0:T(8,128)(2,1)} %bitcast.8), channel_id=1, source_target_pairs={{0,244},{4,240},{8,252},{12,248},{16,4},{20,0},{24,12},{28,8},{32,... | collective-permute-start | bytes 2359304 | tf_op jit(solution)/shard_map/ppermute | solution.py:31
  12.0 6.0 %collective-permute-done.4.refs_5_.refs_2_.refs_9_ = bf16[128,3072]{1,0:T(8,128)(2,1)S(1)} collective-permute-done((bf16[128,3072]{1,0:T(8,128)(2,1)}, bf16[128,3072]{1,0:T(8,128)(2,1)S(1)}, u32[]{:S(2)}, u32[]{:S(2)}) %collective-permute-start.4) | collective-permute-done | bytes 786464 | tf_op jit(solution)/shard_map/ppermute | solution.py:50
  18.0 2.4 %collective-permute-done.3.refs_4_.refs_1_.refs_8_ = bf16[128,3072]{1,0:T(8,128)(2,1)S(1)} collective-permute-done((bf16[128,3072]{1,0:T(8,128)(2,1)}, bf16[128,3072]{1,0:T(8,128)(2,1)S(1)}, u32[]{:S(2)}, u32[]{:S(2)}) %collective-permute-start.3) | collective-permute-done | bytes 786464 | tf_op jit(solution)/shard_map/ppermute | solution.py:50
  20.4 1.0 collective-permute-done.1.refs_7_.refs_4_.refs_11_
  21.4 2.3 %collective-permute-start.6 = (bf16[128,3072]{1,0:T(8,128)(2,1)S(1)}, bf16[128,3072]{1,0:T(8,128)(2,1)S(1)}, u32[]{:S(2)}, u32[]{:S(2)}) collective-permute-start(bf16[128,3072]{1,0:T(8,128)(2,1)S(1)} %collective-permute-done.1.refs_7_.refs_4_.refs_11_), channel_id=1, source_target_pairs={{0,1},{1,2},{2,3},{3,0},{4,5},{5,6},{6,7},{7,4},{8,11},{9,8},{10,9... | collective-permute-start | bytes 2359304 | tf_op jit(solution)/shard_map/ppermute | solution.py:50
  23.7 1.1 %collective-permute-start.7 = (bf16[128,3072]{1,0:T(8,128)(2,1)S(1)}, bf16[128,3072]{1,0:T(8,128)(2,1)S(1)}, u32[]{:S(2)}, u32[]{:S(2)}) collective-permute-start(bf16[128,3072]{1,0:T(8,128)(2,1)S(1)} %collective-permute-done.4.refs_5_.refs_2_.refs_9_), channel_id=1, source_target_pairs={{0,4},{1,5},{2,6},{3,7},{4,0},{5,1},{6,2},{7,3},{8,12},{9,13},{10,... | collective-permute-start | bytes 2359304 | tf_op jit(solution)/shard_map/ppermute | solution.py:50
  24.8 1.2 %collective-permute-start.5 = (bf16[128,3072]{1,0:T(8,128)(2,1)S(1)}, bf16[128,3072]{1,0:T(8,128)(2,1)S(1)}, u32[]{:S(2)}, u32[]{:S(2)}) collective-permute-start(bf16[128,3072]{1,0:T(8,128)(2,1)S(1)} %collective-permute-done.3.refs_4_.refs_1_.refs_8_), channel_id=1, source_target_pairs={{0,1},{1,2},{2,3},{3,0},{4,5},{5,6},{6,7},{7,4},{8,11},{9,8},{10,9... | collective-permute-start | bytes 2359304 | tf_op jit(solution)/shard_map/ppermute | solution.py:50
  26.0 2.0 %collective-permute-done.refs_2_ = bf16[128,3072]{1,0:T(8,128)(2,1)} collective-permute-done((bf16[128,3072]{1,0:T(8,128)(2,1)}, bf16[128,3072]{1,0:T(8,128)(2,1)}, u32[]{:S(2)}, u32[]{:S(2)}) %collective-permute-start) | collective-permute-done | bytes 786464 | tf_op jit(solution)/shard_map/ppermute | solution.py:31
  28.0 3.3 %collective-permute-start.2 = (bf16[128,3072]{1,0:T(8,128)(2,1)S(1)}, bf16[128,3072]{1,0:T(8,128)(2,1)S(1)}, u32[]{:S(2)}, u32[]{:S(2)}) collective-permute-start(bf16[128,3072]{1,0:T(8,128)(2,1)S(1)} %broadcast_select_fusion), channel_id=1, source_target_pairs={{0,8},{8,0},{1,9},{9,1},{2,10},{10,2},{3,11},{11,3},{4,12},{12,4},... | collective-permute-start | bytes 2359304 | tf_op jit(solution)/shard_map/ppermute | solution.py:39
  31.3 9.9 %collective-permute-done.5.refs_6_.refs_3_.refs_10_ = bf16[128,3072]{1,0:T(8,128)(2,1)S(1)} collective-permute-done((bf16[128,3072]{1,0:T(8,128)(2,1)S(1)}, bf16[128,3072]{1,0:T(8,128)(2,1)S(1)}, u32[]{:S(2)}, u32[]{:S(2)}) %collective-permute-start.5) | collective-permute-done | bytes 786464 | tf_op jit(solution)/shard_map/ppermute | solution.py:50
  41.2 2.9 %collective-permute-start.8 = (bf16[128,3072]{1,0:T(8,128)(2,1)S(1)}, bf16[128,3072]{1,0:T(8,128)(2,1)S(1)}, u32[]{:S(2)}, u32[]{:S(2)}) collective-permute-start(bf16[128,3072]{1,0:T(8,128)(2,1)S(1)} %collective-permute-done.6.refs_8_.refs_5_.refs_12_), channel_id=1, source_target_pairs={{0,1},{1,2},{2,3},{3,0},{4,5},{5,6},{6,7},{7,4},{8,11},{9,8},{10,9... | collective-permute-start | bytes 2359304 | tf_op jit(solution)/shard_map/ppermute | solution.py:50
  44.2 4.2 %integrals.2 = (bf16[384,896]{1,0:T(8,128)(2,1)S(1)}, bf16[2,128,128]{2,1,0:T(8,128)(2,1)S(1)}, bf16[2,128,128]{2,1,0:T(8,128)(2,1)S(1)}, bf16[2,128,128]{2,1,0:...) custom-call(bf16[128,3072]{1,0:T(8,128)(2,1)S(1)} %bitcast.9, ...), custom_call_target="tpu_custom_call" | custom-call | flops 2113929216 | bytes 7864320 | tf_op jit(solution)/shard_map/integrals/pallas_call | solution.py:106
  48.4 1.4 %collective-permute-start.9 = (bf16[2,128,128]{2,1,0:T(8,128)(2,1)S(1)}, bf16[2,128,128]{2,1,0:T(8,128)(2,1)S(1)}, u32[]{:S(2)}, u32[]{:S(2)}) collective-permute-start(bf16[2,128,128]{2,1,0:T(8,128)(2,1)S(1)} %get-tuple-element.21), channel_id=1, source_target_pairs={{0,6},{1,7},{2,4},{3,5},{4,2},{5,3},{6,0},{7,1},{8,14},{9,15},{10,... | collective-permute-start | bytes 196616 | tf_op jit(solution)/shard_map/ppermute | solution.py:50
  50.0 2.0 %collective-permute-start.11 = (bf16[2,128,128]{2,1,0:T(8,128)(2,1)S(1)}, bf16[2,128,128]{2,1,0:T(8,128)(2,1)S(1)}, u32[]{:S(2)}, u32[]{:S(2)}) collective-permute-start(bf16[2,128,128]{2,1,0:T(8,128)(2,1)S(1)} %get-tuple-element.25), channel_id=1, source_target_pairs={{0,5},{1,6},{2,7},{3,4},{4,1},{5,2},{6,3},{7,0},{8,15},{9,12},{10,... | collective-permute-start | bytes 196616 | tf_op jit(solution)/shard_map/ppermute | solution.py:50
  52.0 0.4 collective-permute-start.12
  52.4 1.8 %collective-permute-done.9.refs_3_ = bf16[2,128,128]{2,1,0:T(8,128)(2,1)S(1)} collective-permute-done((bf16[2,128,128]{2,1,0:T(8,128)(2,1)S(1)}, bf16[2,128,128]{2,1,0:T(8,128)(2,1)S(1)}, u32[]{:S(2)}, u32[]{:S(2)}) %collective-permute-start.9) | collective-permute-done | bytes 65568 | tf_op jit(solution)/shard_map/ppermute | solution.py:50
  54.4 1.2 %collective-permute-start.14 = (bf16[2,128,128]{2,1,0:T(8,128)(2,1)S(1)}, bf16[2,128,128]{2,1,0:T(8,128)(2,1)S(1)}, u32[]{:S(2)}, u32[]{:S(2)}) collective-permute-start(bf16[2,128,128]{2,1,0:T(8,128)(2,1)S(1)} %get-tuple-element.28), channel_id=1, source_target_pairs={{0,3},{1,0},{2,1},{3,2},{4,7},{5,4},{6,5},{7,6},{8,9},{9,10},{10,1... | collective-permute-start | bytes 196616 | tf_op jit(solution)/shard_map/ppermute | solution.py:50
  55.7 2.0 %integrals.3 = (bf16[384,128]{1,0:T(8,128)(2,1)S(1)}, bf16[2,128,128]{2,1,0:T(8,128)(2,1)S(1)}) custom-call(bf16[128,3072]{1,0:T(8,128)(2,1)S(1)} %bitcast.11, bf16[128,3072]{1,0:T(8,128)(2,1)S(1)} %collective-permute-done.2.refs_1_, bf16[128,3072]{1,0:T(8,128)(2,1)} %collective-permute-done.refs_2_, ...), custom_call_target="tpu_custom_call" | custom-call | flops 301989888 | bytes 3145728 | tf_op jit(solution)/shard_map/integrals/pallas_call | solution.py:106
  57.7 0.9 collective-permute-start.15
  58.6 1.9 %collective-permute-done.14.refs_5_ = bf16[2,128,128]{2,1,0:T(8,128)(2,1)S(1)} collective-permute-done((bf16[2,128,128]{2,1,0:T(8,128)(2,1)S(1)}, bf16[2,128,128]{2,1,0:T(8,128)(2,1)S(1)}, u32[]{:S(2)}, u32[]{:S(2)}) %collective-permute-start.14) | collective-permute-done | bytes 65568 | tf_op jit(solution)/shard_map/ppermute | solution.py:50
  60.5 2.2 %collective-permute-done.15.refs_6_ = bf16[2,128,128]{2,1,0:T(8,128)(2,1)S(1)} collective-permute-done((bf16[2,128,128]{2,1,0:T(8,128)(2,1)S(1)}, bf16[2,128,128]{2,1,0:T(8,128)(2,1)S(1)}, u32[]{:S(2)}, u32[]{:S(2)}) %collective-permute-start.15) | collective-permute-done | bytes 65568 | tf_op jit(solution)/shard_map/ppermute | solution.py:50
  62.7 1.9 %density.5 = bf16[128,3072]{1,0:T(8,128)(2,1)S(1)} custom-call(f32[32]{0:T(128)S(1)} %copy-done.3, f32[8,1,128]{2,1,0:T(1,128)S(1)} %bitcast.16, bf16[384,896]{1,0:T(8,128)(2,1)S(1)} %get-tuple-element.19.early_ref, bf16[384,128]{1,0:T(8,128)(2,1)S(1)} %get-tuple-element.24.late_ref, bf16[2,128,128]{2,1,0:T(8,128)(2,1)S(1)} %collective-permute-done.10.refs_0_, ...), custom_call_target="tpu_custom_call" | custom-call | flops 805306368 | bytes 7077888 | tf_op jit(solution)/shard_map/density/pallas_call | solution.py:157
  64.6 9.2 %collective-permute-start.16 = (bf16[128,3072]{1,0:T(8,128)(2,1)S(1)}, bf16[128,3072]{1,0:T(8,128)(2,1)S(1)}, u32[]{:S(2)}, u32[]{:S(2)}) collective-permute-start(bf16[128,3072]{1,0:T(8,128)(2,1)S(1)} %density.5), channel_id=1, source_target_pairs={{8,0},{12,4},{9,1},{13,5},{10,2},{14,6},{11,3},{15,7},{24,16},{28,... | collective-permute-start | bytes 2359304 | tf_op jit(solution)/shard_map/ppermute | solution.py:35
  73.9 1.9 %density.4 = bf16[128,3072]{1,0:T(8,128)(2,1)S(1)} custom-call(f32[32]{0:T(128)S(1)} %copy-done.3, f32[8,1,128]{2,1,0:T(1,128)S(1)} %bitcast.17, bf16[384,896]{1,0:T(8,128)(2,1)S(1)} %get-tuple-element.19.early_ref, bf16[384,128]{1,0:T(8,128)(2,1)S(1)} %get-tuple-element.24.late_ref, bf16[2,128,128]{2,1,0:T(8,128)(2,1)S(1)} %collective-permute-done.10.refs_0_, ...), custom_call_target="tpu_custom_call" | custom-call | flops 805306368 | bytes 7077888 | tf_op jit(solution)/shard_map/density/pallas_call | solution.py:157
  76.0 2.6 %collective-permute-start.17 = (bf16[128,3072]{1,0:T(8,128)(2,1)S(1)}, bf16[128,3072]{1,0:T(8,128)(2,1)S(1)}, u32[]{:S(2)}, u32[]{:S(2)}) collective-permute-start(bf16[128,3072]{1,0:T(8,128)(2,1)S(1)} %add_convert_fusion), channel_id=1, source_target_pairs={{0,20},{4,16},{8,28},{12,24},{16,36},{20,32},{24,44},{28,40},{32,5... | collective-permute-start | bytes 2359304 | tf_op jit(solution)/shard_map/ppermute | solution.py:31
  78.6 1.3 %collective-permute-start.18 = (bf16[128,3072]{1,0:T(8,128)(2,1)S(1)}, bf16[128,3072]{1,0:T(8,128)(2,1)S(1)}, u32[]{:S(2)}, u32[]{:S(2)}) collective-permute-start(bf16[128,3072]{1,0:T(8,128)(2,1)S(1)} %density.5), channel_id=1, source_target_pairs={{0,12},{4,8},{1,13},{5,9},{2,14},{6,10},{3,15},{7,11},{16,28},{20,... | collective-permute-start | bytes 2359304 | tf_op jit(solution)/shard_map/ppermute | solution.py:35
  79.9 1.9 %density.3 = f32[128,3072]{1,0:T(8,128)S(1)} custom-call(f32[32]{0:T(128)S(1)} %copy-done.3, f32[8,1,128]{2,1,0:T(1,128)S(1)} %bitcast.18, bf16[384,896]{1,0:T(8,128)(2,1)S(1)} %get-tuple-element.19.early_ref, bf16[384,128]{1,0:T(8,128)(2,1)S(1)} %get-tuple-element.24.late_ref, bf16[128,3072]{1,0:T(8,128)(2,1)S(1)} %bitcast.14, ...), custom_call_target="tpu_custom_call" | custom-call | flops 805306368 | bytes 7077888 | tf_op jit(solution)/shard_map/density/pallas_call | solution.py:157
  81.8 19.8 %collective-permute-done.17 = bf16[128,3072]{1,0:T(8,128)(2,1)S(1)} collective-permute-done((bf16[128,3072]{1,0:T(8,128)(2,1)S(1)}, bf16[128,3072]{1,0:T(8,128)(2,1)S(1)}, u32[]{:S(2)}, u32[]{:S(2)}) %collective-permute-start.17) | collective-permute-done | bytes 786464 | tf_op jit(solution)/shard_map/ppermute | solution.py:31
  101.7 1.4 %add_bitcast_fusion = f32[1,128,3072]{2,1,0:T(8,128)} fusion(f32[128,3072]{1,0:T(8,128)S(1)} %convert_add_fusion, bf16[128,3072]{1,0:T(8,128)(2,1)S(1)} %collective-permute-done.18), kind=kLoop, calls=%fused_computation | loop fusion | flops 786432 | bytes 3932160 | tf_op jit(solution)/shard_map/reshape | solution.py:198
  (23 shorter events, 1.0 us)
Async XLA Ops:
  0.0 44.2 %copy-start = (bf16[1,128,3072]{2,1,0:T(8,128)(2,1)S(1)}, bf16[1,128,3072]{2,1,0:T(8,128)(2,1)}, u32[]{:S(2)}) copy-start(bf16[1,128,3072]{2,1,0:T(8,128)(2,1)} %param.4) | copy-start | bytes 2359300
  0.0 18.0 %collective-permute-start.4 = (bf16[128,3072]{1,0:T(8,128)(2,1)}, bf16[128,3072]{1,0:T(8,128)(2,1)S(1)}, u32[]{:S(2)}, u32[]{:S(2)}) collective-permute-start(bf16[128,3072]{1,0:T(8,128)(2,1)} %bitcast.5), channel_id=1, source_target_pairs={{0,3},{1,0},{2,1},{3,2},{4,7},{5,4},{6,5},{7,6},{8,9},{9,10},{10,1... | collective-permute-start | bytes 2359304 | tf_op jit(solution)/shard_map/ppermute | solution.py:50
  2.1 18.2 %collective-permute-start.3 = (bf16[128,3072]{1,0:T(8,128)(2,1)}, bf16[128,3072]{1,0:T(8,128)(2,1)S(1)}, u32[]{:S(2)}, u32[]{:S(2)}) collective-permute-start(bf16[128,3072]{1,0:T(8,128)(2,1)} %bitcast.6), channel_id=1, source_target_pairs={{0,1},{1,2},{2,3},{3,0},{4,5},{5,6},{6,7},{7,4},{8,11},{9,8},{10,9... | collective-permute-start | bytes 2359304 | tf_op jit(solution)/shard_map/ppermute | solution.py:50
  3.6 17.7 %collective-permute-start.1 = (bf16[128,3072]{1,0:T(8,128)(2,1)}, bf16[128,3072]{1,0:T(8,128)(2,1)S(1)}, u32[]{:S(2)}, u32[]{:S(2)}) collective-permute-start(bf16[128,3072]{1,0:T(8,128)(2,1)} %bitcast.7), channel_id=1, source_target_pairs={{0,4},{1,5},{2,6},{3,7},{4,0},{5,1},{6,2},{7,3},{8,12},{9,13},{10,... | collective-permute-start | bytes 2359304 | tf_op jit(solution)/shard_map/ppermute | solution.py:50
  4.9 23.1 %collective-permute-start = (bf16[128,3072]{1,0:T(8,128)(2,1)}, bf16[128,3072]{1,0:T(8,128)(2,1)}, u32[]{:S(2)}, u32[]{:S(2)}) collective-permute-start(bf16[128,3072]{1,0:T(8,128)(2,1)} %bitcast.8), channel_id=1, source_target_pairs={{0,244},{4,240},{8,252},{12,248},{16,4},{20,0},{24,12},{28,8},{32,... | collective-permute-start | bytes 2359304 | tf_op jit(solution)/shard_map/ppermute | solution.py:31
  21.4 19.9 %collective-permute-start.6 = (bf16[128,3072]{1,0:T(8,128)(2,1)S(1)}, bf16[128,3072]{1,0:T(8,128)(2,1)S(1)}, u32[]{:S(2)}, u32[]{:S(2)}) collective-permute-start(bf16[128,3072]{1,0:T(8,128)(2,1)S(1)} %collective-permute-done.1.refs_7_.refs_4_.refs_11_), channel_id=1, source_target_pairs={{0,1},{1,2},{2,3},{3,0},{4,5},{5,6},{6,7},{7,4},{8,11},{9,8},{10,9... | collective-permute-start | bytes 2359304 | tf_op jit(solution)/shard_map/ppermute | solution.py:50
  23.7 20.5 %collective-permute-start.7 = (bf16[128,3072]{1,0:T(8,128)(2,1)S(1)}, bf16[128,3072]{1,0:T(8,128)(2,1)S(1)}, u32[]{:S(2)}, u32[]{:S(2)}) collective-permute-start(bf16[128,3072]{1,0:T(8,128)(2,1)S(1)} %collective-permute-done.4.refs_5_.refs_2_.refs_9_), channel_id=1, source_target_pairs={{0,4},{1,5},{2,6},{3,7},{4,0},{5,1},{6,2},{7,3},{8,12},{9,13},{10,... | collective-permute-start | bytes 2359304 | tf_op jit(solution)/shard_map/ppermute | solution.py:50
  24.8 16.5 %collective-permute-start.5 = (bf16[128,3072]{1,0:T(8,128)(2,1)S(1)}, bf16[128,3072]{1,0:T(8,128)(2,1)S(1)}, u32[]{:S(2)}, u32[]{:S(2)}) collective-permute-start(bf16[128,3072]{1,0:T(8,128)(2,1)S(1)} %collective-permute-done.3.refs_4_.refs_1_.refs_8_), channel_id=1, source_target_pairs={{0,1},{1,2},{2,3},{3,0},{4,5},{5,6},{6,7},{7,4},{8,11},{9,8},{10,9... | collective-permute-start | bytes 2359304 | tf_op jit(solution)/shard_map/ppermute | solution.py:50
  28.0 16.1 %collective-permute-start.2 = (bf16[128,3072]{1,0:T(8,128)(2,1)S(1)}, bf16[128,3072]{1,0:T(8,128)(2,1)S(1)}, u32[]{:S(2)}, u32[]{:S(2)}) collective-permute-start(bf16[128,3072]{1,0:T(8,128)(2,1)S(1)} %broadcast_select_fusion), channel_id=1, source_target_pairs={{0,8},{8,0},{1,9},{9,1},{2,10},{10,2},{3,11},{11,3},{4,12},{12,4},... | collective-permute-start | bytes 2359304 | tf_op jit(solution)/shard_map/ppermute | solution.py:39
  41.2 14.4 %collective-permute-start.8 = (bf16[128,3072]{1,0:T(8,128)(2,1)S(1)}, bf16[128,3072]{1,0:T(8,128)(2,1)S(1)}, u32[]{:S(2)}, u32[]{:S(2)}) collective-permute-start(bf16[128,3072]{1,0:T(8,128)(2,1)S(1)} %collective-permute-done.6.refs_8_.refs_5_.refs_12_), channel_id=1, source_target_pairs={{0,1},{1,2},{2,3},{3,0},{4,5},{5,6},{6,7},{7,4},{8,11},{9,8},{10,9... | collective-permute-start | bytes 2359304 | tf_op jit(solution)/shard_map/ppermute | solution.py:50
  48.4 5.8 %collective-permute-start.9 = (bf16[2,128,128]{2,1,0:T(8,128)(2,1)S(1)}, bf16[2,128,128]{2,1,0:T(8,128)(2,1)S(1)}, u32[]{:S(2)}, u32[]{:S(2)}) collective-permute-start(bf16[2,128,128]{2,1,0:T(8,128)(2,1)S(1)} %get-tuple-element.21), channel_id=1, source_target_pairs={{0,6},{1,7},{2,4},{3,5},{4,2},{5,3},{6,0},{7,1},{8,14},{9,15},{10,... | collective-permute-start | bytes 196616 | tf_op jit(solution)/shard_map/ppermute | solution.py:50
  49.8 4.6 %collective-permute-start.10 = (bf16[2,128,128]{2,1,0:T(8,128)(2,1)S(1)}, bf16[2,128,128]{2,1,0:T(8,128)(2,1)S(1)}, u32[]{:S(2)}, u32[]{:S(2)}) collective-permute-start(bf16[2,128,128]{2,1,0:T(8,128)(2,1)S(1)} %get-tuple-element.22), channel_id=1, source_target_pairs={{0,4},{1,5},{2,6},{3,7},{4,0},{5,1},{6,2},{7,3},{8,12},{9,13},{10,... | collective-permute-start | bytes 196616 | tf_op jit(solution)/shard_map/ppermute | solution.py:50
  50.0 8.6 %collective-permute-start.11 = (bf16[2,128,128]{2,1,0:T(8,128)(2,1)S(1)}, bf16[2,128,128]{2,1,0:T(8,128)(2,1)S(1)}, u32[]{:S(2)}, u32[]{:S(2)}) collective-permute-start(bf16[2,128,128]{2,1,0:T(8,128)(2,1)S(1)} %get-tuple-element.25), channel_id=1, source_target_pairs={{0,5},{1,6},{2,7},{3,4},{4,1},{5,2},{6,3},{7,0},{8,15},{9,12},{10,... | collective-permute-start | bytes 196616 | tf_op jit(solution)/shard_map/ppermute | solution.py:50
  52.0 6.6 %collective-permute-start.12 = (bf16[2,128,128]{2,1,0:T(8,128)(2,1)S(1)}, bf16[2,128,128]{2,1,0:T(8,128)(2,1)S(1)}, u32[]{:S(2)}, u32[]{:S(2)}) collective-permute-start(bf16[2,128,128]{2,1,0:T(8,128)(2,1)S(1)} %get-tuple-element.26), channel_id=1, source_target_pairs={{0,7},{1,4},{2,5},{3,6},{4,3},{5,0},{6,1},{7,2},{8,13},{9,14},{10,... | collective-permute-start | bytes 196616 | tf_op jit(solution)/shard_map/ppermute | solution.py:50
  54.2 4.4 %collective-permute-start.13 = (bf16[2,128,128]{2,1,0:T(8,128)(2,1)S(1)}, bf16[2,128,128]{2,1,0:T(8,128)(2,1)S(1)}, u32[]{:S(2)}, u32[]{:S(2)}) collective-permute-start(bf16[2,128,128]{2,1,0:T(8,128)(2,1)S(1)} %get-tuple-element.27), channel_id=1, source_target_pairs={{0,1},{1,2},{2,3},{3,0},{4,5},{5,6},{6,7},{7,4},{8,11},{9,8},{10,9... | collective-permute-start | bytes 196616 | tf_op jit(solution)/shard_map/ppermute | solution.py:50
  54.4 6.1 %collective-permute-start.14 = (bf16[2,128,128]{2,1,0:T(8,128)(2,1)S(1)}, bf16[2,128,128]{2,1,0:T(8,128)(2,1)S(1)}, u32[]{:S(2)}, u32[]{:S(2)}) collective-permute-start(bf16[2,128,128]{2,1,0:T(8,128)(2,1)S(1)} %get-tuple-element.28), channel_id=1, source_target_pairs={{0,3},{1,0},{2,1},{3,2},{4,7},{5,4},{6,5},{7,6},{8,9},{9,10},{10,1... | collective-permute-start | bytes 196616 | tf_op jit(solution)/shard_map/ppermute | solution.py:50
  55.6 7.1 %copy-start.2 = (f32[1024]{0:T(1024)S(1)}, f32[1024]{0:T(1024)}, u32[]{:S(2)}) copy-start(f32[1024]{0:T(1024)} %param.6) | copy-start | bytes 12292
  55.6 7.1 %copy-start.3 = (f32[32]{0:T(128)S(1)}, f32[32]{0:T(128)}, u32[]{:S(2)}) copy-start(f32[32]{0:T(128)} %e_occ.5) | copy-start | bytes 388
  57.7 5.1 %collective-permute-start.15 = (bf16[2,128,128]{2,1,0:T(8,128)(2,1)S(1)}, bf16[2,128,128]{2,1,0:T(8,128)(2,1)S(1)}, u32[]{:S(2)}, u32[]{:S(2)}) collective-permute-start(bf16[2,128,128]{2,1,0:T(8,128)(2,1)S(1)} %get-tuple-element.29), channel_id=1, source_target_pairs={{0,2},{1,3},{2,0},{3,1},{4,6},{5,7},{6,4},{7,5},{8,10},{9,11},{10,... | collective-permute-start | bytes 196616 | tf_op jit(solution)/shard_map/ppermute | solution.py:50
  64.6 11.2 %collective-permute-start.16 = (bf16[128,3072]{1,0:T(8,128)(2,1)S(1)}, bf16[128,3072]{1,0:T(8,128)(2,1)S(1)}, u32[]{:S(2)}, u32[]{:S(2)}) collective-permute-start(bf16[128,3072]{1,0:T(8,128)(2,1)S(1)} %density.5), channel_id=1, source_target_pairs={{8,0},{12,4},{9,1},{13,5},{10,2},{14,6},{11,3},{15,7},{24,16},{28,... | collective-permute-start | bytes 2359304 | tf_op jit(solution)/shard_map/ppermute | solution.py:35
  75.8 4.1 %copy-start.1 = (f32[1,128,3072]{2,1,0:T(8,128)S(1)}, f32[1,128,3072]{2,1,0:T(8,128)}, u32[]{:S(2)}) copy-start(f32[1,128,3072]{2,1,0:T(8,128)} %param.7) | copy-start | bytes 4718596
  76.0 25.6 %collective-permute-start.17 = (bf16[128,3072]{1,0:T(8,128)(2,1)S(1)}, bf16[128,3072]{1,0:T(8,128)(2,1)S(1)}, u32[]{:S(2)}, u32[]{:S(2)}) collective-permute-start(bf16[128,3072]{1,0:T(8,128)(2,1)S(1)} %add_convert_fusion), channel_id=1, source_target_pairs={{0,20},{4,16},{8,28},{12,24},{16,36},{20,32},{24,44},{28,40},{32,5... | collective-permute-start | bytes 2359304 | tf_op jit(solution)/shard_map/ppermute | solution.py:31
  78.6 23.2 %collective-permute-start.18 = (bf16[128,3072]{1,0:T(8,128)(2,1)S(1)}, bf16[128,3072]{1,0:T(8,128)(2,1)S(1)}, u32[]{:S(2)}, u32[]{:S(2)}) collective-permute-start(bf16[128,3072]{1,0:T(8,128)(2,1)S(1)} %density.5), channel_id=1, source_target_pairs={{0,12},{4,8},{1,13},{5,9},{2,14},{6,10},{3,15},{7,11},{16,28},{20,... | collective-permute-start | bytes 2359304 | tf_op jit(solution)/shard_map/ppermute | solution.py:35

commit v7 on v6

--- a/solution.py
+++ b/solution.py
@@ -182,7 +182,7 @@
     sent = (3, 0, 5, 6, 1, 2)
     early, *tiles = integrals(rows, pieces[:EARLY], sent)
     swapped = exchanged(dict(zip(sent, tiles)))
-    last = [after(piece, early, *list(swapped.values())[:2]) for piece in pieces[EARLY:]]
+    last = [after(piece, early, *list(swapped.values())[:3]) for piece in pieces[EARLY:]]
     pieces = pieces[:EARLY] + last
     late, tile = integrals(rows, last, (0,))
     swapped |= exchanged({EARLY: tile})

time: 103 us -> 103 us (level)
    ppermute x14, starting transfers between devices: 18.8 us -> 21.2 us  [within(): return lax.ppermute(block, ('core', 'xl', 'y'), pairs)]
    ppermute x2, starting transfers between devices: 10.5 us -> 8.85 us  [one_block_on(): lax.ppermute(block, ('core', 'xl'), [(core * XL + x, (1 - core) * XL + (x...]
  transfers between devices with their start and end apart: 19 -> 19, of which waited for: 9 -> 8; matrix products, arithmetic and copies ran while one was open for 0% -> 0% of each run, Pallas kernels for 10% -> 10%
where the time goes in v7:
time: 103 us
  waiting for transfers between devices  46.2 us (45%)
  starting transfers between devices  43 us (42%)
  Pallas kernels  11.9 us (12%)
  other arithmetic  1.78 us (2%)
    ppermute x14, waiting for transfers between devices, within(): return lax.ppermute(block, ('core', 'xl', 'y'), pairs)  24.4 us
    ppermute x2, waiting for transfers between devices, two_blocks_on(): return lax.ppermute(block, ('z', 'xh', 'core', 'xl'), pairs)  21.7 us
    ppermute x14, starting transfers between devices, within(): return lax.ppermute(block, ('core', 'xl', 'y'), pairs)  21.2 us
    ppermute x2, starting transfers between devices, two_blocks_on(): return lax.ppermute(block, ('z', 'xh', 'core', 'xl'), pairs)  9.67 us
    ppermute x2, starting transfers between devices, one_block_on(): lax.ppermute(block, ('core', 'xl'), [(core * XL + x, (1 - core) * XL + (x...  8.85 us
    pallas_call x2, Pallas kernels, integrals(): pl.pallas_call(functools.partial(integrals_kernel, count, sent), in_specs...  6.22 us
    pallas_call x3, Pallas kernels, density(): pl.pallas_call(functools.partial(density_kernel, visit), in_specs=[pl.Blo...  5.71 us
    ppermute x1, starting transfers between devices, to_sibling(): return lax.ppermute(block, 'core', [(0, 1), (1, 0)])  3.3 us
  transfers between devices with their start and end apart: 19, of which 8 were waited for; matrix products, arithmetic and copies ran while one was open for 0% of the time, Pallas kernels for 10%

profile of v7, /device:TPU:1, one launch (start us, length us, event | category | flops | bytes accessed | tf_op | source)
XLA Modules:
  0.0 103.1 jit_solution(10719968425293253756)
XLA Ops:
  0.0 2.1 %collective-permute-start.4 = (bf16[128,3072]{1,0:T(8,128)(2,1)}, bf16[128,3072]{1,0:T(8,128)(2,1)S(1)}, u32[]{:S(2)}, u32[]{:S(2)}) collective-permute-start(bf16[128,3072]{1,0:T(8,128)(2,1)} %bitcast.5), channel_id=1, source_target_pairs={{0,3},{1,0},{2,1},{3,2},{4,7},{5,4},{6,5},{7,6},{8,9},{9,10},{10,1... | collective-permute-start | bytes 2359304 | tf_op jit(solution)/shard_map/ppermute | solution.py:50
  2.1 1.5 %collective-permute-start.3 = (bf16[128,3072]{1,0:T(8,128)(2,1)}, bf16[128,3072]{1,0:T(8,128)(2,1)S(1)}, u32[]{:S(2)}, u32[]{:S(2)}) collective-permute-start(bf16[128,3072]{1,0:T(8,128)(2,1)} %bitcast.6), channel_id=1, source_target_pairs={{0,1},{1,2},{2,3},{3,0},{4,5},{5,6},{6,7},{7,4},{8,11},{9,8},{10,9... | collective-permute-start | bytes 2359304 | tf_op jit(solution)/shard_map/ppermute | solution.py:50
  3.6 1.2 %collective-permute-start.1 = (bf16[128,3072]{1,0:T(8,128)(2,1)}, bf16[128,3072]{1,0:T(8,128)(2,1)S(1)}, u32[]{:S(2)}, u32[]{:S(2)}) collective-permute-start(bf16[128,3072]{1,0:T(8,128)(2,1)} %bitcast.7), channel_id=1, source_target_pairs={{0,4},{1,5},{2,6},{3,7},{4,0},{5,1},{6,2},{7,3},{8,12},{9,13},{10,... | collective-permute-start | bytes 2359304 | tf_op jit(solution)/shard_map/ppermute | solution.py:50
  4.9 7.1 %collective-permute-start = (bf16[128,3072]{1,0:T(8,128)(2,1)}, bf16[128,3072]{1,0:T(8,128)(2,1)}, u32[]{:S(2)}, u32[]{:S(2)}) collective-permute-start(bf16[128,3072]{1,0:T(8,128)(2,1)} %bitcast.8), channel_id=1, source_target_pairs={{0,244},{4,240},{8,252},{12,248},{16,4},{20,0},{24,12},{28,8},{32,... | collective-permute-start | bytes 2359304 | tf_op jit(solution)/shard_map/ppermute | solution.py:31
  12.0 6.0 %collective-permute-done.4.refs_5_.refs_2_.refs_9_ = bf16[128,3072]{1,0:T(8,128)(2,1)S(1)} collective-permute-done((bf16[128,3072]{1,0:T(8,128)(2,1)}, bf16[128,3072]{1,0:T(8,128)(2,1)S(1)}, u32[]{:S(2)}, u32[]{:S(2)}) %collective-permute-start.4) | collective-permute-done | bytes 786464 | tf_op jit(solution)/shard_map/ppermute | solution.py:50
  18.0 2.4 %collective-permute-done.3.refs_4_.refs_1_.refs_8_ = bf16[128,3072]{1,0:T(8,128)(2,1)S(1)} collective-permute-done((bf16[128,3072]{1,0:T(8,128)(2,1)}, bf16[128,3072]{1,0:T(8,128)(2,1)S(1)}, u32[]{:S(2)}, u32[]{:S(2)}) %collective-permute-start.3) | collective-permute-done | bytes 786464 | tf_op jit(solution)/shard_map/ppermute | solution.py:50
  20.4 1.0 collective-permute-done.1.refs_7_.refs_4_.refs_11_
  21.4 2.3 %collective-permute-start.6 = (bf16[128,3072]{1,0:T(8,128)(2,1)S(1)}, bf16[128,3072]{1,0:T(8,128)(2,1)S(1)}, u32[]{:S(2)}, u32[]{:S(2)}) collective-permute-start(bf16[128,3072]{1,0:T(8,128)(2,1)S(1)} %collective-permute-done.1.refs_7_.refs_4_.refs_11_), channel_id=1, source_target_pairs={{0,1},{1,2},{2,3},{3,0},{4,5},{5,6},{6,7},{7,4},{8,11},{9,8},{10,9... | collective-permute-start | bytes 2359304 | tf_op jit(solution)/shard_map/ppermute | solution.py:50
  23.7 1.1 %collective-permute-start.7 = (bf16[128,3072]{1,0:T(8,128)(2,1)S(1)}, bf16[128,3072]{1,0:T(8,128)(2,1)S(1)}, u32[]{:S(2)}, u32[]{:S(2)}) collective-permute-start(bf16[128,3072]{1,0:T(8,128)(2,1)S(1)} %collective-permute-done.4.refs_5_.refs_2_.refs_9_), channel_id=1, source_target_pairs={{0,4},{1,5},{2,6},{3,7},{4,0},{5,1},{6,2},{7,3},{8,12},{9,13},{10,... | collective-permute-start | bytes 2359304 | tf_op jit(solution)/shard_map/ppermute | solution.py:50
  24.8 1.2 %collective-permute-start.5 = (bf16[128,3072]{1,0:T(8,128)(2,1)S(1)}, bf16[128,3072]{1,0:T(8,128)(2,1)S(1)}, u32[]{:S(2)}, u32[]{:S(2)}) collective-permute-start(bf16[128,3072]{1,0:T(8,128)(2,1)S(1)} %collective-permute-done.3.refs_4_.refs_1_.refs_8_), channel_id=1, source_target_pairs={{0,1},{1,2},{2,3},{3,0},{4,5},{5,6},{6,7},{7,4},{8,11},{9,8},{10,9... | collective-permute-start | bytes 2359304 | tf_op jit(solution)/shard_map/ppermute | solution.py:50
  26.0 2.0 %collective-permute-done.refs_2_ = bf16[128,3072]{1,0:T(8,128)(2,1)} collective-permute-done((bf16[128,3072]{1,0:T(8,128)(2,1)}, bf16[128,3072]{1,0:T(8,128)(2,1)}, u32[]{:S(2)}, u32[]{:S(2)}) %collective-permute-start) | collective-permute-done | bytes 786464 | tf_op jit(solution)/shard_map/ppermute | solution.py:31
  28.0 3.3 %collective-permute-start.2 = (bf16[128,3072]{1,0:T(8,128)(2,1)S(1)}, bf16[128,3072]{1,0:T(8,128)(2,1)S(1)}, u32[]{:S(2)}, u32[]{:S(2)}) collective-permute-start(bf16[128,3072]{1,0:T(8,128)(2,1)S(1)} %broadcast_select_fusion), channel_id=1, source_target_pairs={{0,8},{8,0},{1,9},{9,1},{2,10},{10,2},{3,11},{11,3},{4,12},{12,4},... | collective-permute-start | bytes 2359304 | tf_op jit(solution)/shard_map/ppermute | solution.py:39
  31.3 9.9 %collective-permute-done.5.refs_6_.refs_3_.refs_10_ = bf16[128,3072]{1,0:T(8,128)(2,1)S(1)} collective-permute-done((bf16[128,3072]{1,0:T(8,128)(2,1)S(1)}, bf16[128,3072]{1,0:T(8,128)(2,1)S(1)}, u32[]{:S(2)}, u32[]{:S(2)}) %collective-permute-start.5) | collective-permute-done | bytes 786464 | tf_op jit(solution)/shard_map/ppermute | solution.py:50
  41.2 2.9 %collective-permute-start.8 = (bf16[128,3072]{1,0:T(8,128)(2,1)S(1)}, bf16[128,3072]{1,0:T(8,128)(2,1)S(1)}, u32[]{:S(2)}, u32[]{:S(2)}) collective-permute-start(bf16[128,3072]{1,0:T(8,128)(2,1)S(1)} %collective-permute-done.6.refs_8_.refs_5_.refs_12_), channel_id=1, source_target_pairs={{0,1},{1,2},{2,3},{3,0},{4,5},{5,6},{6,7},{7,4},{8,11},{9,8},{10,9... | collective-permute-start | bytes 2359304 | tf_op jit(solution)/shard_map/ppermute | solution.py:50
  44.2 4.2 %integrals.2 = (bf16[384,896]{1,0:T(8,128)(2,1)S(1)}, bf16[2,128,128]{2,1,0:T(8,128)(2,1)S(1)}, bf16[2,128,128]{2,1,0:T(8,128)(2,1)S(1)}, bf16[2,128,128]{2,1,0:...) custom-call(bf16[128,3072]{1,0:T(8,128)(2,1)S(1)} %bitcast.9, ...), custom_call_target="tpu_custom_call" | custom-call | flops 2113929216 | bytes 7864320 | tf_op jit(solution)/shard_map/integrals/pallas_call | solution.py:106
  48.4 1.4 %collective-permute-start.9 = (bf16[2,128,128]{2,1,0:T(8,128)(2,1)S(1)}, bf16[2,128,128]{2,1,0:T(8,128)(2,1)S(1)}, u32[]{:S(2)}, u32[]{:S(2)}) collective-permute-start(bf16[2,128,128]{2,1,0:T(8,128)(2,1)S(1)} %get-tuple-element.21), channel_id=1, source_target_pairs={{0,6},{1,7},{2,4},{3,5},{4,2},{5,3},{6,0},{7,1},{8,14},{9,15},{10,... | collective-permute-start | bytes 196616 | tf_op jit(solution)/shard_map/ppermute | solution.py:50
  49.8 0.3 collective-permute-start.10
  50.0 0.4 collective-permute-start.11
  50.5 3.2 %collective-permute-start.12 = (bf16[2,128,128]{2,1,0:T(8,128)(2,1)S(1)}, bf16[2,128,128]{2,1,0:T(8,128)(2,1)S(1)}, u32[]{:S(2)}, u32[]{:S(2)}) collective-permute-start(bf16[2,128,128]{2,1,0:T(8,128)(2,1)S(1)} %get-tuple-element.26), channel_id=1, source_target_pairs={{0,5},{1,6},{2,7},{3,4},{4,1},{5,2},{6,3},{7,0},{8,15},{9,12},{10,... | collective-permute-start | bytes 196616 | tf_op jit(solution)/shard_map/ppermute | solution.py:50
  53.6 0.5 collective-permute-done.9.refs_3_
  54.2 3.5 %collective-permute-start.14 = (bf16[2,128,128]{2,1,0:T(8,128)(2,1)S(1)}, bf16[2,128,128]{2,1,0:T(8,128)(2,1)S(1)}, u32[]{:S(2)}, u32[]{:S(2)}) collective-permute-start(bf16[2,128,128]{2,1,0:T(8,128)(2,1)S(1)} %get-tuple-element.28), channel_id=1, source_target_pairs={{0,1},{1,2},{2,3},{3,0},{4,5},{5,6},{6,7},{7,4},{8,11},{9,8},{10,9... | collective-permute-start | bytes 196616 | tf_op jit(solution)/shard_map/ppermute | solution.py:50
  57.7 2.0 %integrals.3 = (bf16[384,128]{1,0:T(8,128)(2,1)S(1)}, bf16[2,128,128]{2,1,0:T(8,128)(2,1)S(1)}) custom-call(bf16[128,3072]{1,0:T(8,128)(2,1)S(1)} %bitcast.11, bf16[128,3072]{1,0:T(8,128)(2,1)S(1)} %collective-permute-done.2.refs_1_, bf16[128,3072]{1,0:T(8,128)(2,1)} %collective-permute-done.refs_2_, ...), custom_call_target="tpu_custom_call" | custom-call | flops 301989888 | bytes 3145728 | tf_op jit(solution)/shard_map/integrals/pallas_call | solution.py:106
  59.8 4.6 %collective-permute-done.15.refs_6_ = bf16[2,128,128]{2,1,0:T(8,128)(2,1)S(1)} collective-permute-done((bf16[2,128,128]{2,1,0:T(8,128)(2,1)S(1)}, bf16[2,128,128]{2,1,0:T(8,128)(2,1)S(1)}, u32[]{:S(2)}, u32[]{:S(2)}) %collective-permute-start.15) | collective-permute-done | bytes 65568 | tf_op jit(solution)/shard_map/ppermute | solution.py:50
  64.4 1.9 %density.5 = bf16[128,3072]{1,0:T(8,128)(2,1)S(1)} custom-call(f32[32]{0:T(128)S(1)} %copy-done.3, f32[8,1,128]{2,1,0:T(1,128)S(1)} %bitcast.16, bf16[384,896]{1,0:T(8,128)(2,1)S(1)} %get-tuple-element.19.early_ref, bf16[384,128]{1,0:T(8,128)(2,1)S(1)} %get-tuple-element.25.late_ref, bf16[2,128,128]{2,1,0:T(8,128)(2,1)S(1)} %collective-permute-done.10.refs_0_, ...), custom_call_target="tpu_custom_call" | custom-call | flops 805306368 | bytes 7077888 | tf_op jit(solution)/shard_map/density/pallas_call | solution.py:157
  66.3 7.6 %collective-permute-start.16 = (bf16[128,3072]{1,0:T(8,128)(2,1)S(1)}, bf16[128,3072]{1,0:T(8,128)(2,1)S(1)}, u32[]{:S(2)}, u32[]{:S(2)}) collective-permute-start(bf16[128,3072]{1,0:T(8,128)(2,1)S(1)} %density.5), channel_id=1, source_target_pairs={{8,0},{12,4},{9,1},{13,5},{10,2},{14,6},{11,3},{15,7},{24,16},{28,... | collective-permute-start | bytes 2359304 | tf_op jit(solution)/shard_map/ppermute | solution.py:35
  73.9 1.9 %density.4 = bf16[128,3072]{1,0:T(8,128)(2,1)S(1)} custom-call(f32[32]{0:T(128)S(1)} %copy-done.3, f32[8,1,128]{2,1,0:T(1,128)S(1)} %bitcast.17, bf16[384,896]{1,0:T(8,128)(2,1)S(1)} %get-tuple-element.19.early_ref, bf16[384,128]{1,0:T(8,128)(2,1)S(1)} %get-tuple-element.25.late_ref, bf16[2,128,128]{2,1,0:T(8,128)(2,1)S(1)} %collective-permute-done.10.refs_0_, ...), custom_call_target="tpu_custom_call" | custom-call | flops 805306368 | bytes 7077888 | tf_op jit(solution)/shard_map/density/pallas_call | solution.py:157
  75.8 0.2 add_convert_fusion
  76.0 2.6 %collective-permute-start.17 = (bf16[128,3072]{1,0:T(8,128)(2,1)S(1)}, bf16[128,3072]{1,0:T(8,128)(2,1)S(1)}, u32[]{:S(2)}, u32[]{:S(2)}) collective-permute-start(bf16[128,3072]{1,0:T(8,128)(2,1)S(1)} %add_convert_fusion), channel_id=1, source_target_pairs={{0,20},{4,16},{8,28},{12,24},{16,36},{20,32},{24,44},{28,40},{32,5... | collective-permute-start | bytes 2359304 | tf_op jit(solution)/shard_map/ppermute | solution.py:31
  78.6 1.3 %collective-permute-start.18 = (bf16[128,3072]{1,0:T(8,128)(2,1)S(1)}, bf16[128,3072]{1,0:T(8,128)(2,1)S(1)}, u32[]{:S(2)}, u32[]{:S(2)}) collective-permute-start(bf16[128,3072]{1,0:T(8,128)(2,1)S(1)} %density.5), channel_id=1, source_target_pairs={{0,12},{4,8},{1,13},{5,9},{2,14},{6,10},{3,15},{7,11},{16,28},{20,... | collective-permute-start | bytes 2359304 | tf_op jit(solution)/shard_map/ppermute | solution.py:35
  79.9 1.9 %density.3 = f32[128,3072]{1,0:T(8,128)S(1)} custom-call(f32[32]{0:T(128)S(1)} %copy-done.3, f32[8,1,128]{2,1,0:T(1,128)S(1)} %bitcast.18, bf16[384,896]{1,0:T(8,128)(2,1)S(1)} %get-tuple-element.19.early_ref, bf16[384,128]{1,0:T(8,128)(2,1)S(1)} %get-tuple-element.25.late_ref, bf16[128,3072]{1,0:T(8,128)(2,1)S(1)} %bitcast.14, ...), custom_call_target="tpu_custom_call" | custom-call | flops 805306368 | bytes 7077888 | tf_op jit(solution)/shard_map/density/pallas_call | solution.py:157
  81.8 19.8 %collective-permute-done.17 = bf16[128,3072]{1,0:T(8,128)(2,1)S(1)} collective-permute-done((bf16[128,3072]{1,0:T(8,128)(2,1)S(1)}, bf16[128,3072]{1,0:T(8,128)(2,1)S(1)}, u32[]{:S(2)}, u32[]{:S(2)}) %collective-permute-start.17) | collective-permute-done | bytes 786464 | tf_op jit(solution)/shard_map/ppermute | solution.py:31
  101.7 1.4 %add_bitcast_fusion = f32[1,128,3072]{2,1,0:T(8,128)} fusion(f32[128,3072]{1,0:T(8,128)S(1)} %convert_add_fusion, bf16[128,3072]{1,0:T(8,128)(2,1)S(1)} %collective-permute-done.18), kind=kLoop, calls=%fused_computation | loop fusion | flops 786432 | bytes 3932160 | tf_op jit(solution)/shard_map/reshape | solution.py:198
  (23 shorter events, 0.4 us)
Async XLA Ops:
  0.0 44.2 %copy-start = (bf16[1,128,3072]{2,1,0:T(8,128)(2,1)S(1)}, bf16[1,128,3072]{2,1,0:T(8,128)(2,1)}, u32[]{:S(2)}) copy-start(bf16[1,128,3072]{2,1,0:T(8,128)(2,1)} %param.4) | copy-start | bytes 2359300
  0.0 18.0 %collective-permute-start.4 = (bf16[128,3072]{1,0:T(8,128)(2,1)}, bf16[128,3072]{1,0:T(8,128)(2,1)S(1)}, u32[]{:S(2)}, u32[]{:S(2)}) collective-permute-start(bf16[128,3072]{1,0:T(8,128)(2,1)} %bitcast.5), channel_id=1, source_target_pairs={{0,3},{1,0},{2,1},{3,2},{4,7},{5,4},{6,5},{7,6},{8,9},{9,10},{10,1... | collective-permute-start | bytes 2359304 | tf_op jit(solution)/shard_map/ppermute | solution.py:50
  2.1 18.2 %collective-permute-start.3 = (bf16[128,3072]{1,0:T(8,128)(2,1)}, bf16[128,3072]{1,0:T(8,128)(2,1)S(1)}, u32[]{:S(2)}, u32[]{:S(2)}) collective-permute-start(bf16[128,3072]{1,0:T(8,128)(2,1)} %bitcast.6), channel_id=1, source_target_pairs={{0,1},{1,2},{2,3},{3,0},{4,5},{5,6},{6,7},{7,4},{8,11},{9,8},{10,9... | collective-permute-start | bytes 2359304 | tf_op jit(solution)/shard_map/ppermute | solution.py:50
  3.6 17.7 %collective-permute-start.1 = (bf16[128,3072]{1,0:T(8,128)(2,1)}, bf16[128,3072]{1,0:T(8,128)(2,1)S(1)}, u32[]{:S(2)}, u32[]{:S(2)}) collective-permute-start(bf16[128,3072]{1,0:T(8,128)(2,1)} %bitcast.7), channel_id=1, source_target_pairs={{0,4},{1,5},{2,6},{3,7},{4,0},{5,1},{6,2},{7,3},{8,12},{9,13},{10,... | collective-permute-start | bytes 2359304 | tf_op jit(solution)/shard_map/ppermute | solution.py:50
  4.9 23.1 %collective-permute-start = (bf16[128,3072]{1,0:T(8,128)(2,1)}, bf16[128,3072]{1,0:T(8,128)(2,1)}, u32[]{:S(2)}, u32[]{:S(2)}) collective-permute-start(bf16[128,3072]{1,0:T(8,128)(2,1)} %bitcast.8), channel_id=1, source_target_pairs={{0,244},{4,240},{8,252},{12,248},{16,4},{20,0},{24,12},{28,8},{32,... | collective-permute-start | bytes 2359304 | tf_op jit(solution)/shard_map/ppermute | solution.py:31
  21.4 19.9 %collective-permute-start.6 = (bf16[128,3072]{1,0:T(8,128)(2,1)S(1)}, bf16[128,3072]{1,0:T(8,128)(2,1)S(1)}, u32[]{:S(2)}, u32[]{:S(2)}) collective-permute-start(bf16[128,3072]{1,0:T(8,128)(2,1)S(1)} %collective-permute-done.1.refs_7_.refs_4_.refs_11_), channel_id=1, source_target_pairs={{0,1},{1,2},{2,3},{3,0},{4,5},{5,6},{6,7},{7,4},{8,11},{9,8},{10,9... | collective-permute-start | bytes 2359304 | tf_op jit(solution)/shard_map/ppermute | solution.py:50
  23.7 20.5 %collective-permute-start.7 = (bf16[128,3072]{1,0:T(8,128)(2,1)S(1)}, bf16[128,3072]{1,0:T(8,128)(2,1)S(1)}, u32[]{:S(2)}, u32[]{:S(2)}) collective-permute-start(bf16[128,3072]{1,0:T(8,128)(2,1)S(1)} %collective-permute-done.4.refs_5_.refs_2_.refs_9_), channel_id=1, source_target_pairs={{0,4},{1,5},{2,6},{3,7},{4,0},{5,1},{6,2},{7,3},{8,12},{9,13},{10,... | collective-permute-start | bytes 2359304 | tf_op jit(solution)/shard_map/ppermute | solution.py:50
  24.8 16.5 %collective-permute-start.5 = (bf16[128,3072]{1,0:T(8,128)(2,1)S(1)}, bf16[128,3072]{1,0:T(8,128)(2,1)S(1)}, u32[]{:S(2)}, u32[]{:S(2)}) collective-permute-start(bf16[128,3072]{1,0:T(8,128)(2,1)S(1)} %collective-permute-done.3.refs_4_.refs_1_.refs_8_), channel_id=1, source_target_pairs={{0,1},{1,2},{2,3},{3,0},{4,5},{5,6},{6,7},{7,4},{8,11},{9,8},{10,9... | collective-permute-start | bytes 2359304 | tf_op jit(solution)/shard_map/ppermute | solution.py:50
  28.0 16.1 %collective-permute-start.2 = (bf16[128,3072]{1,0:T(8,128)(2,1)S(1)}, bf16[128,3072]{1,0:T(8,128)(2,1)S(1)}, u32[]{:S(2)}, u32[]{:S(2)}) collective-permute-start(bf16[128,3072]{1,0:T(8,128)(2,1)S(1)} %broadcast_select_fusion), channel_id=1, source_target_pairs={{0,8},{8,0},{1,9},{9,1},{2,10},{10,2},{3,11},{11,3},{4,12},{12,4},... | collective-permute-start | bytes 2359304 | tf_op jit(solution)/shard_map/ppermute | solution.py:39
  41.2 16.4 %collective-permute-start.8 = (bf16[128,3072]{1,0:T(8,128)(2,1)S(1)}, bf16[128,3072]{1,0:T(8,128)(2,1)S(1)}, u32[]{:S(2)}, u32[]{:S(2)}) collective-permute-start(bf16[128,3072]{1,0:T(8,128)(2,1)S(1)} %collective-permute-done.6.refs_8_.refs_5_.refs_12_), channel_id=1, source_target_pairs={{0,1},{1,2},{2,3},{3,0},{4,5},{5,6},{6,7},{7,4},{8,11},{9,8},{10,9... | collective-permute-start | bytes 2359304 | tf_op jit(solution)/shard_map/ppermute | solution.py:50
  48.4 5.8 %collective-permute-start.9 = (bf16[2,128,128]{2,1,0:T(8,128)(2,1)S(1)}, bf16[2,128,128]{2,1,0:T(8,128)(2,1)S(1)}, u32[]{:S(2)}, u32[]{:S(2)}) collective-permute-start(bf16[2,128,128]{2,1,0:T(8,128)(2,1)S(1)} %get-tuple-element.21), channel_id=1, source_target_pairs={{0,6},{1,7},{2,4},{3,5},{4,2},{5,3},{6,0},{7,1},{8,14},{9,15},{10,... | collective-permute-start | bytes 196616 | tf_op jit(solution)/shard_map/ppermute | solution.py:50
  49.8 4.4 %collective-permute-start.10 = (bf16[2,128,128]{2,1,0:T(8,128)(2,1)S(1)}, bf16[2,128,128]{2,1,0:T(8,128)(2,1)S(1)}, u32[]{:S(2)}, u32[]{:S(2)}) collective-permute-start(bf16[2,128,128]{2,1,0:T(8,128)(2,1)S(1)} %get-tuple-element.22), channel_id=1, source_target_pairs={{0,4},{1,5},{2,6},{3,7},{4,0},{5,1},{6,2},{7,3},{8,12},{9,13},{10,... | collective-permute-start | bytes 196616 | tf_op jit(solution)/shard_map/ppermute | solution.py:50
  50.0 7.6 %collective-permute-start.11 = (bf16[2,128,128]{2,1,0:T(8,128)(2,1)S(1)}, bf16[2,128,128]{2,1,0:T(8,128)(2,1)S(1)}, u32[]{:S(2)}, u32[]{:S(2)}) collective-permute-start(bf16[2,128,128]{2,1,0:T(8,128)(2,1)S(1)} %get-tuple-element.23), channel_id=1, source_target_pairs={{0,3},{1,0},{2,1},{3,2},{4,7},{5,4},{6,5},{7,6},{8,9},{9,10},{10,1... | collective-permute-start | bytes 196616 | tf_op jit(solution)/shard_map/ppermute | solution.py:50
  50.5 9.3 %collective-permute-start.12 = (bf16[2,128,128]{2,1,0:T(8,128)(2,1)S(1)}, bf16[2,128,128]{2,1,0:T(8,128)(2,1)S(1)}, u32[]{:S(2)}, u32[]{:S(2)}) collective-permute-start(bf16[2,128,128]{2,1,0:T(8,128)(2,1)S(1)} %get-tuple-element.26), channel_id=1, source_target_pairs={{0,5},{1,6},{2,7},{3,4},{4,1},{5,2},{6,3},{7,0},{8,15},{9,12},{10,... | collective-permute-start | bytes 196616 | tf_op jit(solution)/shard_map/ppermute | solution.py:50
  54.2 5.6 %collective-permute-start.13 = (bf16[2,128,128]{2,1,0:T(8,128)(2,1)S(1)}, bf16[2,128,128]{2,1,0:T(8,128)(2,1)S(1)}, u32[]{:S(2)}, u32[]{:S(2)}) collective-permute-start(bf16[2,128,128]{2,1,0:T(8,128)(2,1)S(1)} %get-tuple-element.27), channel_id=1, source_target_pairs={{0,7},{1,4},{2,5},{3,6},{4,3},{5,0},{6,1},{7,2},{8,13},{9,14},{10,... | collective-permute-start | bytes 196616 | tf_op jit(solution)/shard_map/ppermute | solution.py:50
  54.2 5.6 %collective-permute-start.14 = (bf16[2,128,128]{2,1,0:T(8,128)(2,1)S(1)}, bf16[2,128,128]{2,1,0:T(8,128)(2,1)S(1)}, u32[]{:S(2)}, u32[]{:S(2)}) collective-permute-start(bf16[2,128,128]{2,1,0:T(8,128)(2,1)S(1)} %get-tuple-element.28), channel_id=1, source_target_pairs={{0,1},{1,2},{2,3},{3,0},{4,5},{5,6},{6,7},{7,4},{8,11},{9,8},{10,9... | collective-permute-start | bytes 196616 | tf_op jit(solution)/shard_map/ppermute | solution.py:50
  57.7 6.7 %copy-start.2 = (f32[1024]{0:T(1024)S(1)}, f32[1024]{0:T(1024)}, u32[]{:S(2)}) copy-start(f32[1024]{0:T(1024)} %param.6) | copy-start | bytes 12292
  57.7 6.7 %copy-start.3 = (f32[32]{0:T(128)S(1)}, f32[32]{0:T(128)}, u32[]{:S(2)}) copy-start(f32[32]{0:T(128)} %e_occ.5) | copy-start | bytes 388
  59.7 4.7 %collective-permute-start.15 = (bf16[2,128,128]{2,1,0:T(8,128)(2,1)S(1)}, bf16[2,128,128]{2,1,0:T(8,128)(2,1)S(1)}, u32[]{:S(2)}, u32[]{:S(2)}) collective-permute-start(bf16[2,128,128]{2,1,0:T(8,128)(2,1)S(1)} %get-tuple-element.29), channel_id=1, source_target_pairs={{0,2},{1,3},{2,0},{3,1},{4,6},{5,7},{6,4},{7,5},{8,10},{9,11},{10,... | collective-permute-start | bytes 196616 | tf_op jit(solution)/shard_map/ppermute | solution.py:50
  66.3 9.5 %collective-permute-start.16 = (bf16[128,3072]{1,0:T(8,128)(2,1)S(1)}, bf16[128,3072]{1,0:T(8,128)(2,1)S(1)}, u32[]{:S(2)}, u32[]{:S(2)}) collective-permute-start(bf16[128,3072]{1,0:T(8,128)(2,1)S(1)} %density.5), channel_id=1, source_target_pairs={{8,0},{12,4},{9,1},{13,5},{10,2},{14,6},{11,3},{15,7},{24,16},{28,... | collective-permute-start | bytes 2359304 | tf_op jit(solution)/shard_map/ppermute | solution.py:35
  75.8 4.1 %copy-start.1 = (f32[1,128,3072]{2,1,0:T(8,128)S(1)}, f32[1,128,3072]{2,1,0:T(8,128)}, u32[]{:S(2)}) copy-start(f32[1,128,3072]{2,1,0:T(8,128)} %param.7) | copy-start | bytes 4718596
  76.0 25.6 %collective-permute-start.17 = (bf16[128,3072]{1,0:T(8,128)(2,1)S(1)}, bf16[128,3072]{1,0:T(8,128)(2,1)S(1)}, u32[]{:S(2)}, u32[]{:S(2)}) collective-permute-start(bf16[128,3072]{1,0:T(8,128)(2,1)S(1)} %add_convert_fusion), channel_id=1, source_target_pairs={{0,20},{4,16},{8,28},{12,24},{16,36},{20,32},{24,44},{28,40},{32,5... | collective-permute-start | bytes 2359304 | tf_op jit(solution)/shard_map/ppermute | solution.py:31
  78.6 23.2 %collective-permute-start.18 = (bf16[128,3072]{1,0:T(8,128)(2,1)S(1)}, bf16[128,3072]{1,0:T(8,128)(2,1)S(1)}, u32[]{:S(2)}, u32[]{:S(2)}) collective-permute-start(bf16[128,3072]{1,0:T(8,128)(2,1)S(1)} %density.5), channel_id=1, source_target_pairs={{0,12},{4,8},{1,13},{5,9},{2,14},{6,10},{3,15},{7,11},{16,28},{20,... | collective-permute-start | bytes 2359304 | tf_op jit(solution)/shard_map/ppermute | solution.py:35
